TPU v7x, 32 devices: a whole 2x2x4 slice. The times are simulated.
32 devices in a mesh: groups: 2 (over x), seq: 16 (over z, y, core).
Axes of the slice: x: 2, y: 2, z: 4, core: 2. Of those that a mesh axis runs over, the one named last changes fastest.
Arguments:
- residual: float32 [4, 16, 128, 1152], P('groups', 'seq'), parts along dimension 0, may hold values from -16 to 16
- w_qkv: bfloat16 [1152, 3456], replicated, may hold values from -0.15 to 0.15
- w_proj: bfloat16 [1152, 1152], replicated, may hold values from -0.1875 to 0.1875
- q_gain: float32 [1152], replicated, may hold values from 0.5 to 7
- k_gain: float32 [1152], replicated, may hold values from 0.5 to 7
- step_mods: float32 [30, 3, 1152], replicated, may hold values from -4 to 4
- timestep: int32 [2], P('groups'), parts along dimension 0, may hold values from 0 to 29, as said below
Outputs:
- updated: float32 [4, 16, 128, 1152], P('groups', 'seq'), parts along dimension 0
There are 2 independent parts, one for each index of `groups`. A program takes and returns all parts, laid end to end along the dimension named above; an argument that names none is the same for every part. Nothing has to cross between parts.
Inputs may be any that keep to these rules, and one draw needn't show every extreme that they name: `timestep`: the first part takes a step from the first half of the table, the second part the last step.
All inputs are finite; a program needn't handle non-finite values.
Results may differ from a plain program's by a relative error of at most 0.002.
Values may be sent and summed in bfloat16 or wider, within the bound.
No kernel may reach another device: no remote copies, remote signals or barrier semaphores. Data moves between devices by JAX's collectives and lax.ppermute only.
A program may use at most 64 MiB of HBM per device.

v0:
```python
import functools

import jax
import jax.numpy as jnp
from jax import lax
from jax.experimental import pallas as pl
from jax.experimental.pallas import tpu as pltpu
from jax.sharding import PartitionSpec as P

HEADS = 16
HEAD_DIM = 72
LANES = 128
LOG2_E = 1.4426950408889634
F32 = jnp.float32
BF16 = jnp.bfloat16
VMEM = pltpu.VMEM


def params(mebibytes):
    return pltpu.CompilerParams(vmem_limit_bytes=mebibytes << 20)


def in_hbm(array):
    return pltpu.with_memory_space_constraint(array, pltpu.HBM)


def block_of(j, r, exchange):
    if not exchange:
        return j
    me = lax.axis_index("seq")
    return jnp.bitwise_xor(me, 2 * j + r)


def modulate_kernel(exchange, step_ref, rows_hbm, mods_hbm, *refs):
    *out_refs, gate_ref, rows_ref, mods_ref, sems = refs
    branch, _, width = rows_ref.shape
    count, _, share, _ = out_refs[0].shape

    def fetch(b):
        return pltpu.make_async_copy(rows_hbm.at[b], rows_ref.at[b], sems.at[b])

    mods = pltpu.make_async_copy(mods_hbm, mods_ref, sems.at[branch])
    fetch(0).start()
    mods.start()
    for b in range(1, branch):
        fetch(b).start()
    mods.wait()
    step = pl.ds(step_ref[0], 1)
    shift_row, scale_row = mods_ref[0, step, :], 1.0 + mods_ref[1, step, :]
    gate_ref[...] = mods_ref[2, step, :]
    group = 1 if exchange else max(1, 32 // share)
    for b in range(branch):
        fetch(b).wait()
        for r, out_ref in enumerate(out_refs):
            for j in range(0, count, group):
                start = block_of(j, r, exchange) * share
                if exchange:
                    start = pl.multiple_of(start, share)
                rows = rows_ref[b, pl.ds(start, group * share)]
                centre = jnp.mean(rows, axis=-1, keepdims=True)
                centred = rows - centre
                variance = jnp.mean(centred * centred, axis=-1, keepdims=True)
                normed = centred * lax.rsqrt(variance + 1e-06) * scale_row + shift_row
                out_ref[j : j + group, b] = normed.reshape(group, share, width).astype(BF16)


def modulate(rows, step_mods, timestep, n, exchange):
    branch, patches, width = rows.shape
    outs = 2 if exchange else 1
    part = VMEM((n // outs, branch, patches // n, width), BF16)
    return pl.pallas_call(
        functools.partial(modulate_kernel, exchange),
        out_shape=[part] * outs + [VMEM((1, width), F32)],
        in_specs=[
            pl.BlockSpec(memory_space=pltpu.SMEM),
            pl.BlockSpec(memory_space=pltpu.HBM),
            pl.BlockSpec(memory_space=pltpu.HBM),
        ],
        out_specs=[pl.BlockSpec(memory_space=VMEM)] * (outs + 1),
        scratch_shapes=[
            VMEM((branch, patches, width), F32),
            VMEM((3, step_mods.shape[0], width), F32),
            pltpu.SemaphoreType.DMA((branch + 1,)),
        ],
        compiler_params=params(8),
        name="modulate",
    )(timestep, in_hbm(rows), in_hbm(jnp.swapaxes(step_mods, 0, 1)))


def fetch_columns(w_hbm, part, w_ref, sem):
    return pltpu.make_async_copy(
        w_hbm.at[:, pl.ds(part * w_ref.shape[1], w_ref.shape[1])], w_ref, sem
    )


def stage_first_kernel(after_ref, w_hbm, w_ref, sem):
    del after_ref
    copy = fetch_columns(w_hbm, 0, w_ref, sem)
    copy.start()
    copy.wait()


def stage_first(w, after):
    width = w.shape[0]
    return pl.pallas_call(
        stage_first_kernel,
        out_shape=VMEM((width, width), w.dtype),
        in_specs=[pl.BlockSpec(memory_space=VMEM), pl.BlockSpec(memory_space=pltpu.HBM)],
        out_specs=pl.BlockSpec(memory_space=VMEM),
        scratch_shapes=[pltpu.SemaphoreType.DMA],
        compiler_params=params(1),
        name="stage_first",
    )(after, in_hbm(w))


def stage_rest_kernel(after_ref, w_hbm, q_gain_hbm, k_gain_hbm, *refs):
    wk_ref, wv_ref, gather_ref, spread_ref, q_row_ref, k_row_ref, line_ref, sems = refs
    del after_ref
    gains = [
        pltpu.make_async_copy(gain, line_ref.at[at], sems.at[at])
        for at, gain in enumerate((q_gain_hbm, k_gain_hbm))
    ]
    columns = [
        fetch_columns(w_hbm, part, ref, sems.at[part + 1])
        for part, ref in ((1, wk_ref), (2, wv_ref))
    ]
    for copy in gains + columns:
        copy.start()
    gather_ref[...] = head_of(gather_ref.shape, 0)
    spread_ref[...] = head_of(spread_ref.shape, 1)
    for at, row_ref in enumerate((q_row_ref, k_row_ref)):
        gains[at].wait()
        row_ref[...] = line_ref[at].reshape(row_ref.shape)
    for copy in columns:
        copy.wait()


def stage_rest(w, q_gain, k_gain, after):
    width = w.shape[0]
    hbm = pl.BlockSpec(memory_space=pltpu.HBM)
    return pl.pallas_call(
        stage_rest_kernel,
        out_shape=[
            VMEM((width, width), w.dtype),
            VMEM((width, width), w.dtype),
            VMEM((width, LANES), BF16),
            VMEM((LANES, width), BF16),
            VMEM((1, width), F32),
            VMEM((1, width), F32),
        ],
        in_specs=[pl.BlockSpec(memory_space=VMEM), hbm, hbm, hbm],
        out_specs=[pl.BlockSpec(memory_space=VMEM)] * 6,
        scratch_shapes=[VMEM((2, width), F32), pltpu.SemaphoreType.DMA((4,))],
        compiler_params=params(2),
        name="stage_rest",
    )(after, in_hbm(w), in_hbm(q_gain), in_hbm(k_gain))


def pack_kernel(keep_ref, got_ref, *out_refs):
    for j, out_ref in enumerate(out_refs):
        out_ref[0] = keep_ref[j]
        out_ref[1] = got_ref[j]


def pack(keep, got):
    count, *part = keep.shape
    return pl.pallas_call(
        pack_kernel,
        out_shape=[VMEM((2, *part), keep.dtype)] * count,
        in_specs=[pl.BlockSpec(memory_space=VMEM)] * 2,
        out_specs=[pl.BlockSpec(memory_space=VMEM)] * count,
        compiler_params=params(1),
        name="pack",
    )(keep, got)


def send_order(n):
    return [*range(n // 4, n // 2), *range(1, n // 4)]


def swap_parts(n, keep, give):
    got = lax.ppermute(give, "seq", [(s, s ^ 1) for s in range(n)])
    parts = list(pack(keep, got))
    for j in send_order(n):
        parts[j] = lax.ppermute(parts[j], "seq", [(s, s ^ (2 * j)) for s in range(n)])
    return parts


def gather_rows(x_refs):
    return jnp.concatenate([ref[...].reshape(-1, ref.shape[-1]) for ref in x_refs], axis=0)


def head_of(shape, feature_dim):
    feature = lax.broadcasted_iota(jnp.int32, shape, feature_dim)
    place = lax.broadcasted_iota(jnp.int32, shape, 1 - feature_dim)
    first = lax.rem(place, HEADS) * HEAD_DIM
    inside = (feature >= first) & (feature < first + HEAD_DIM) & (place < 2 * HEADS)
    return jnp.where(inside, 1.0, 0.0).astype(BF16)


def high_low(wide):
    high = wide.astype(BF16)
    return high, wide - high.astype(F32)


def head_scale(vectors, gather, spread):
    high, low = high_low(vectors * vectors)
    square = jnp.dot(high, gather, preferred_element_type=F32)
    square += jnp.dot(low.astype(BF16), gather, preferred_element_type=F32)
    high, low = high_low(lax.rsqrt(square * (1.0 / HEAD_DIM) + 1e-06))
    place = lax.broadcasted_iota(jnp.int32, low.shape, 1)
    both = jnp.where(place < HEADS, high.astype(F32), low).astype(BF16)
    return vectors * jnp.dot(both, spread, preferred_element_type=F32)


def pair_masks():
    lane = lax.broadcasted_iota(jnp.int32, (1, 2 * LANES), 1)
    for i in range(HEADS // 2):
        masks = []
        for h in (2 * i, 2 * i + 1):
            start = h * HEAD_DIM - i * LANES
            masks.append(jnp.where((lane >= start) & (lane < start + HEAD_DIM), 1.0, 0.0))
        yield i, pl.ds(i * LANES, 2 * LANES), masks


def heads(x_refs, *refs):
    *w_refs, gather_ref, spread_ref, q_gain_ref, k_gain_ref, q_ref, k_ref, v_ref = refs
    _, branch, share, width = x_refs[0].shape
    x = gather_rows(x_refs)
    gather, spread = gather_ref[...], spread_ref[...]

    def product(part):
        return jnp.dot(x, w_refs[part][...], preferred_element_type=F32)

    def per_branch(values):
        values = values.reshape(-1, branch, share, width)
        return [values[:, b].reshape(-1, width) for b in range(branch)]

    def store_pairs(values, gain_ref, ref):
        for b, own in enumerate(per_branch(values)):
            for i, columns, masks in pair_masks():
                for side, mask in enumerate(masks):
                    row = mask if gain_ref is None else mask * gain_ref[:, columns]
                    part = own[:, i * LANES : (i + 2) * LANES]
                    ref[b, i, side] = (part * row).astype(BF16)

    store_pairs(head_scale(product(0), gather, spread), q_gain_ref, q_ref)
    for b, own in enumerate(per_branch(head_scale(product(1), gather, spread))):
        k_ref[b] = (own * k_gain_ref[...]).astype(BF16)
    store_pairs(product(2), None, v_ref)


def head_shapes(xs):
    _, branch, share, width = xs[0].shape
    tokens = sum(x.shape[0] for x in xs) * share
    pairs = (branch, HEADS // 2, 2, tokens, 2 * LANES)
    return [VMEM(shape, BF16) for shape in (pairs, (branch, tokens, width), pairs)]


def heads_kernel(ins, *refs):
    heads(refs[:ins], *refs[ins:])


def early_heads(xs, tables):
    return pl.pallas_call(
        functools.partial(heads_kernel, len(xs)),
        out_shape=head_shapes(xs),
        in_specs=[pl.BlockSpec(memory_space=VMEM)] * (len(xs) + len(tables)),
        out_specs=[pl.BlockSpec(memory_space=VMEM)] * 3,
        compiler_params=params(10),
        name="heads",
    )(*xs, *tables)


def attend_kernel(ins, outs, places, has_early, *refs):
    x_refs, table_refs, refs = refs[:ins], refs[ins : ins + 7], refs[ins + 7 :]
    early, refs = (refs[:3], refs[3:]) if has_early else ((), refs)
    out_refs, late, scores_ref, probs_ref = refs[:outs], refs[outs:-2], refs[-2], refs[-1]
    heads(x_refs, *table_refs, *late)
    _, branch, share, width = x_refs[0].shape
    halves = [early, late] if has_early else [late]
    tokens = sum(half[1].shape[1] for half in halves)
    frames = tokens // share
    same = lax.broadcasted_iota(jnp.int32, (share, 2 * tokens), 0) == lax.rem(
        lax.broadcasted_iota(jnp.int32, (share, 2 * tokens), 1), share
    )

    def rows_of(which, b, i, columns):
        if which == 1:
            return jnp.concatenate([half[1][b, :, columns] for half in halves], axis=0)
        return jnp.concatenate(
            [half[which][b, i, side] for side in range(2) for half in halves], axis=0
        )

    def emit(b, at, block):
        block = block.astype(BF16).reshape(frames // outs, outs, share, LANES)
        for r, out_ref in enumerate(out_refs):
            if places is None:
                out_ref[:, b, :, pl.ds(at, LANES)] = block[:, r]
            else:
                for j, place in enumerate(places):
                    out_ref[place, b, :, pl.ds(at, LANES)] = block[j, r]

    steps = [(i, columns, b) for i, columns, _ in pair_masks() for b in range(branch)]
    carry = [None] * branch

    def score(at):
        i, columns, b = steps[at]
        scores_ref[at] = lax.dot_general(
            rows_of(1, b, i, columns),
            rows_of(0, b, i, columns),
            (((1,), (1,)), ((), ())),
            preferred_element_type=F32,
        )

    def weigh(at):
        scores = scores_ref[at].reshape(frames, share, 2 * tokens)
        top = jnp.max(scores, axis=0)
        weights = jnp.exp2((scores - top) * (HEAD_DIM ** (-0.5) * LOG2_E))
        total = jnp.sum(weights, axis=0)
        probs = weights * jnp.where(same, 1.0 / total, 0.0)
        probs = probs.reshape(tokens, 2 * tokens).astype(BF16)
        probs_ref[at, :tokens] = probs[:, :tokens]
        probs_ref[at, tokens:] = probs[:, tokens:]

    def mix(at):
        i, columns, b = steps[at]
        mixed = lax.dot_general(
            probs_ref[at],
            rows_of(2, b, i, columns),
            (((0,), (0,)), ((), ())),
            preferred_element_type=F32,
        )
        block = mixed[:, :LANES]
        if carry[b] is not None:
            block = block + carry[b]
        carry[b] = mixed[:, LANES:]
        emit(b, i * LANES, block)

    for at in range(len(steps) + 2):
        if at < len(steps):
            score(at)
        if 0 <= at - 1 < len(steps):
            weigh(at - 1)
        if 0 <= at - 2:
            mix(at - 2)
    for b in range(branch):
        emit(b, width - LANES, carry[b])


def attend(xs, tables, early, places, frames, outs):
    _, branch, share, width = xs[0].shape
    tokens = frames * share
    return pl.pallas_call(
        functools.partial(attend_kernel, len(xs), outs, places, bool(early)),
        out_shape=[VMEM((frames // outs, branch, share, width), BF16)] * outs,
        in_specs=[pl.BlockSpec(memory_space=VMEM)] * (len(xs) + len(tables) + len(early)),
        out_specs=[pl.BlockSpec(memory_space=VMEM)] * outs,
        scratch_shapes=[
            *head_shapes(xs),
            VMEM((branch * HEADS // 2, tokens, 2 * tokens), F32),
            VMEM((branch * HEADS // 2, 2 * tokens, tokens), BF16),
        ],
        compiler_params=params(20),
        name="attend",
    )(*xs, *tables, *early)


def project_kernel(exchange, ins, *refs):
    x_refs, (w_ref, gate_ref, residual_ref, out_ref) = refs[:ins], refs[ins:]
    _, branch, share, _ = x_refs[0].shape
    output = jnp.dot(gather_rows(x_refs), w_ref[...], preferred_element_type=F32)
    gated = (gate_ref[...] * output).reshape(-1, branch, share, output.shape[-1])
    for b in range(branch):
        if not exchange:
            out_ref[b] = residual_ref[b] + gated[:, b].reshape(out_ref.shape[1:])
            continue
        for at in range(gated.shape[0]):
            start = pl.multiple_of(block_of(at // 2, at % 2, exchange) * share, share)
            block = pl.ds(start, share)
            out_ref[b, block] = residual_ref[b, block] + gated[at, b]


def project(xs, w_proj, gate_row, rows, exchange):
    branch, patches, width = rows.shape
    cols = 384
    return pl.pallas_call(
        functools.partial(project_kernel, exchange, len(xs)),
        out_shape=jax.ShapeDtypeStruct(rows.shape, F32),
        grid=(width // cols,),
        in_specs=[pl.BlockSpec(x.shape, lambda j: (0, 0, 0, 0)) for x in xs]
        + [
            pl.BlockSpec((width, cols), lambda j: (0, j)),
            pl.BlockSpec((1, cols), lambda j: (0, j)),
            pl.BlockSpec((branch, patches, cols), lambda j: (0, 0, j)),
        ],
        out_specs=pl.BlockSpec((branch, patches, cols), lambda j: (0, 0, j)),
        compiler_params=params(12),
        name="project",
    )(*xs, w_proj, gate_row, rows)


def body(n, exchange, residual, w_qkv, w_proj, q_gain, k_gain, step_mods, timestep):
    rows = residual[:, 0]
    if exchange:
        swap = functools.partial(swap_parts, n)
    else:

        def swap(parts):
            return [lax.all_to_all(parts, "seq", split_axis=0, concat_axis=0, tiled=True)]

    early, places = (), None
    *parts, gate_row = modulate(rows, step_mods, timestep, n, exchange)
    parts = swap(*parts)
    w_first = stage_first(w_qkv, gate_row)
    tables = w_first, *stage_rest(w_qkv, q_gain, k_gain, gate_row)
    if exchange:
        places = (0, *send_order(n))
        first = places[: n // 4]
        early = early_heads([parts[j] for j in first], tables)
        parts = [parts[j] for j in places[n // 4 :]]
    parts = swap(*attend(parts, tables, early, places, n, 2 if exchange else 1))
    return project(parts, w_proj, gate_row, rows, exchange)[:, None]


def solution(mesh):
    in_specs = (P("groups", "seq", None, None), P(), P(), P(), P(), P(), P("groups"))
    out_specs = P("groups", "seq", None, None)
    n = mesh.shape["seq"]

    def step(residual, *others):
        share = residual.shape[2] // n
        exchange = 4 <= n <= 32 and n & (n - 1) == 0 and share % 8 == 0
        run = jax.shard_map(
            functools.partial(body, n, exchange),
            mesh=mesh,
            in_specs=in_specs,
            out_specs=out_specs,
            check_vma=False,
        )
        return run(residual, *others)

    return step
```

profile of v0, /device:TPU:0, one launch (start us, length us, event | category | flops | bytes accessed | tf_op | source)
XLA Modules:
  0.0 54.8 jit_solution(17999938538897466337)
XLA Ops:
  0.7 1.8 %modulate.1 = (bf16[8,2,8,1152]{3,2,1,0:T(8,128)(2,1)S(1)}, bf16[8,2,8,1152]{3,2,1,0:T(8,128)(2,1)S(1)}, f32[1,1152]{1,0:T(1,128)S(1)}) custom-call(s32[1]{0:T(128)S(6)} %copy.9.step_ref, f32[2,128,1152]{2,1,0:T(8,128)} %bitcast.5, f32[3,30,1152]{2,1,0:T(8,128)} %bitcast.7), custom_call_target="tpu_custom_call" | custom-call | tf_op jit(solution)/shard_map/modulate/pallas_call | solution.py:71
  2.5 0.6 %collective-permute-start = (bf16[8,2,8,1152]{3,2,1,0:T(8,128)(2,1)S(1)}, bf16[8,2,8,1152]{3,2,1,0:T(8,128)(2,1)S(1)}, u32[]{:S(2)}, u32[]{:S(2)}) collective-permute-start(bf16[8,2,8,1152]{3,2,1,0:T(8,128)(2,1)S(1)} %get-tuple-element.36), channel_id=1, source_target_pairs={{0,1},{1,0},{2,3},{3,2},{4,5},{5,4},{6,7},{7,6},{8,9},{9,8},{10,11... | collective-permute-start | bytes 884744 | tf_op jit(solution)/shard_map/ppermute | solution.py:182
  3.0 1.2 %collective-permute-done.got_ref = bf16[8,2,8,1152]{3,2,1,0:T(8,128)(2,1)S(1)} collective-permute-done((bf16[8,2,8,1152]{3,2,1,0:T(8,128)(2,1)S(1)}, bf16[8,2,8,1152]{3,2,1,0:T(8,128)(2,1)S(1)}, u32[]{:S(2)}, u32[]{:S(2)}) %collective-permute-start) | collective-permute-done | bytes 294944 | tf_op jit(solution)/shard_map/ppermute | solution.py:182
  4.3 4.0 %collective-permute-start.5 = (bf16[2,2,8,1152]{3,2,1,0:T(8,128)(2,1)S(1)}, bf16[2,2,8,1152]{3,2,1,0:T(8,128)(2,1)S(1)}, u32[]{:S(2)}, u32[]{:S(2)}) collective-permute-start(bf16[2,2,8,1152]{3,2,1,0:T(8,128)(2,1)S(1)} %get-tuple-element.49), channel_id=1, source_target_pairs={{0,8},{1,9},{2,10},{3,11},{4,12},{5,13},{6,14},{7,15},{8,0},{9,1},... | collective-permute-start | bytes 221192 | tf_op jit(solution)/shard_map/ppermute | solution.py:185
  8.3 1.3 %collective-permute-start.6 = (bf16[2,2,8,1152]{3,2,1,0:T(8,128)(2,1)S(1)}, bf16[2,2,8,1152]{3,2,1,0:T(8,128)(2,1)S(1)}, u32[]{:S(2)}, u32[]{:S(2)}) collective-permute-start(bf16[2,2,8,1152]{3,2,1,0:T(8,128)(2,1)S(1)} %get-tuple-element.50), channel_id=1, source_target_pairs={{0,10},{1,11},{2,8},{3,9},{4,14},{5,15},{6,12},{7,13},{8,2},{9,3},... | collective-permute-start | bytes 221192 | tf_op jit(solution)/shard_map/ppermute | solution.py:185
  9.6 3.6 %collective-permute-start.7 = (bf16[2,2,8,1152]{3,2,1,0:T(8,128)(2,1)S(1)}, bf16[2,2,8,1152]{3,2,1,0:T(8,128)(2,1)S(1)}, u32[]{:S(2)}, u32[]{:S(2)}) collective-permute-start(bf16[2,2,8,1152]{3,2,1,0:T(8,128)(2,1)S(1)} %get-tuple-element.51), channel_id=1, source_target_pairs={{0,12},{1,13},{2,14},{3,15},{4,8},{5,9},{6,10},{7,11},{8,4},{9,5},... | collective-permute-start | bytes 221192 | tf_op jit(solution)/shard_map/ppermute | solution.py:185
  13.2 1.7 %collective-permute-start.2 = (bf16[2,2,8,1152]{3,2,1,0:T(8,128)(2,1)S(1)}, bf16[2,2,8,1152]{3,2,1,0:T(8,128)(2,1)S(1)}, u32[]{:S(2)}, u32[]{:S(2)}) collective-permute-start(bf16[2,2,8,1152]{3,2,1,0:T(8,128)(2,1)S(1)} %get-tuple-element.38), channel_id=1, source_target_pairs={{0,2},{1,3},{2,0},{3,1},{4,6},{5,7},{6,4},{7,5},{8,10},{9,11},{10,... | collective-permute-start | bytes 221192 | tf_op jit(solution)/shard_map/ppermute | solution.py:185
  14.9 1.9 %collective-permute-start.3 = (bf16[2,2,8,1152]{3,2,1,0:T(8,128)(2,1)S(1)}, bf16[2,2,8,1152]{3,2,1,0:T(8,128)(2,1)S(1)}, u32[]{:S(2)}, u32[]{:S(2)}) collective-permute-start(bf16[2,2,8,1152]{3,2,1,0:T(8,128)(2,1)S(1)} %get-tuple-element.39), channel_id=1, source_target_pairs={{0,4},{1,5},{2,6},{3,7},{4,0},{5,1},{6,2},{7,3},{8,12},{9,13},{10,... | collective-permute-start | bytes 221192 | tf_op jit(solution)/shard_map/ppermute | solution.py:185
  16.8 2.7 %collective-permute-done.6.refs_2_ = bf16[2,2,8,1152]{3,2,1,0:T(8,128)(2,1)S(1)} collective-permute-done((bf16[2,2,8,1152]{3,2,1,0:T(8,128)(2,1)S(1)}, bf16[2,2,8,1152]{3,2,1,0:T(8,128)(2,1)S(1)}, u32[]{:S(2)}, u32[]{:S(2)}) %collective-permute-start.6) | collective-permute-done | bytes 73760 | tf_op jit(solution)/shard_map/ppermute | solution.py:185
  19.5 1.0 %collective-permute-start.4 = (bf16[2,2,8,1152]{3,2,1,0:T(8,128)(2,1)S(1)}, bf16[2,2,8,1152]{3,2,1,0:T(8,128)(2,1)S(1)}, u32[]{:S(2)}, u32[]{:S(2)}) collective-permute-start(bf16[2,2,8,1152]{3,2,1,0:T(8,128)(2,1)S(1)} %get-tuple-element.40), channel_id=1, source_target_pairs={{0,6},{1,7},{2,4},{3,5},{4,2},{5,3},{6,0},{7,1},{8,14},{9,15},{10,... | collective-permute-start | bytes 221192 | tf_op jit(solution)/shard_map/ppermute | solution.py:185
  20.5 1.8 %stage_first.1.refs_4_ = bf16[1152,1152]{1,0:T(8,128)(2,1)S(1)} custom-call(f32[1,1152]{1,0:T(1,128)S(1)} %get-tuple-element.41.after_ref.refs_9_, bf16[1152,3456]{1,0:T(8,128)(2,1)} %w_hbm.3), custom_call_target="tpu_custom_call" | custom-call | tf_op jit(solution)/shard_map/stage_first/pallas_call | solution.py:105
  22.3 2.6 %stage_rest.1 = (bf16[1152,1152]{1,0:T(8,128)(2,1)S(1)}, bf16[1152,1152]{1,0:T(8,128)(2,1)S(1)}, bf16[1152,128]{1,0:T(8,128)(2,1)S(1)}, bf16[128,1152]{1,0:T(8,1...) custom-call(f32[1,1152]{1,0:T(1,128)S(1)} %get-tuple-element.41.after_ref.refs_9_, bf16[1152,3456]{1,0:T(8,128)(2,1)} %w_hbm.3, ...), custom_call_target="tpu_custom_call" | custom-call | tf_op jit(solution)/shard_map/stage_rest/pallas_call | solution.py:141
  24.9 2.5 %heads.1 = (bf16[2,8,2,64,256]{4,3,2,1,0:T(8,128)(2,1)S(1)}, bf16[2,64,1152]{2,1,0:T(8,128)(2,1)S(1)}, bf16[2,8,2,64,256]{4,3,2,1,0:T(8,128)(2,1)S(1)}) custom-call(bf16[2,2,8,1152]{3,2,1,0:T(8,128)(2,1)S(1)} %get-tuple-element.48.refs_0_, bf16[2,2,8,1152]{3,2,1,0:T(8,128)(2,1)S(1)} %collective-permute-done.5.refs_1_, ...), custom_call_target="tpu_custom_call" | custom-call | tf_op jit(solution)/shard_map/heads/pallas_call | solution.py:265
  27.5 4.5 %attend.1 = (bf16[8,2,8,1152]{3,2,1,0:T(8,128)(2,1)S(1)}, bf16[8,2,8,1152]{3,2,1,0:T(8,128)(2,1)S(1)}) custom-call(bf16[2,2,8,1152]{3,2,1,0:T(8,128)(2,1)S(1)} %collective-permute-done.1.refs_0_, bf16[2,2,8,1152]{3,2,1,0:T(8,128)(2,1)S(1)} %collective-permute-done.2.refs_1_, bf16[2,2,8,1152]{3,2,1,0:T(8,128)(2,1)S(1)} %collective-permute-done.3.refs_2_, ...), custom_call_target="tpu_custom_call" | custom-call | tf_op jit(solution)/shard_map/attend/pallas_call | solution.py:354
  32.0 1.6 %collective-permute-done.8.got_ref = bf16[8,2,8,1152]{3,2,1,0:T(8,128)(2,1)S(1)} collective-permute-done((bf16[8,2,8,1152]{3,2,1,0:T(8,128)(2,1)S(1)}, bf16[8,2,8,1152]{3,2,1,0:T(8,128)(2,1)S(1)}, u32[]{:S(2)}, u32[]{:S(2)}) %collective-permute-start.8) | collective-permute-done | bytes 294944 | tf_op jit(solution)/shard_map/ppermute | solution.py:182
  33.7 1.1 %collective-permute-start.9 = (bf16[2,2,8,1152]{3,2,1,0:T(8,128)(2,1)S(1)}, bf16[2,2,8,1152]{3,2,1,0:T(8,128)(2,1)S(1)}, u32[]{:S(2)}, u32[]{:S(2)}) collective-permute-start(bf16[2,2,8,1152]{3,2,1,0:T(8,128)(2,1)S(1)} %get-tuple-element.58), channel_id=1, source_target_pairs={{0,2},{1,3},{2,0},{3,1},{4,6},{5,7},{6,4},{7,5},{8,10},{9,11},{10,... | collective-permute-start | bytes 221192 | tf_op jit(solution)/shard_map/ppermute | solution.py:185
  34.7 1.5 %collective-permute-start.10 = (bf16[2,2,8,1152]{3,2,1,0:T(8,128)(2,1)S(1)}, bf16[2,2,8,1152]{3,2,1,0:T(8,128)(2,1)S(1)}, u32[]{:S(2)}, u32[]{:S(2)}) collective-permute-start(bf16[2,2,8,1152]{3,2,1,0:T(8,128)(2,1)S(1)} %get-tuple-element.59), channel_id=1, source_target_pairs={{0,4},{1,5},{2,6},{3,7},{4,0},{5,1},{6,2},{7,3},{8,12},{9,13},{10,... | collective-permute-start | bytes 221192 | tf_op jit(solution)/shard_map/ppermute | solution.py:185
  36.3 1.4 %collective-permute-start.11 = (bf16[2,2,8,1152]{3,2,1,0:T(8,128)(2,1)S(1)}, bf16[2,2,8,1152]{3,2,1,0:T(8,128)(2,1)S(1)}, u32[]{:S(2)}, u32[]{:S(2)}) collective-permute-start(bf16[2,2,8,1152]{3,2,1,0:T(8,128)(2,1)S(1)} %get-tuple-element.60), channel_id=1, source_target_pairs={{0,6},{1,7},{2,4},{3,5},{4,2},{5,3},{6,0},{7,1},{8,14},{9,15},{10,... | collective-permute-start | bytes 221192 | tf_op jit(solution)/shard_map/ppermute | solution.py:185
  37.6 2.9 %collective-permute-start.12 = (bf16[2,2,8,1152]{3,2,1,0:T(8,128)(2,1)S(1)}, bf16[2,2,8,1152]{3,2,1,0:T(8,128)(2,1)S(1)}, u32[]{:S(2)}, u32[]{:S(2)}) collective-permute-start(bf16[2,2,8,1152]{3,2,1,0:T(8,128)(2,1)S(1)} %get-tuple-element.61), channel_id=1, source_target_pairs={{0,8},{1,9},{2,10},{3,11},{4,12},{5,13},{6,14},{7,15},{8,0},{9,1},... | collective-permute-start | bytes 221192 | tf_op jit(solution)/shard_map/ppermute | solution.py:185
  40.6 0.9 %collective-permute-start.13 = (bf16[2,2,8,1152]{3,2,1,0:T(8,128)(2,1)S(1)}, bf16[2,2,8,1152]{3,2,1,0:T(8,128)(2,1)S(1)}, u32[]{:S(2)}, u32[]{:S(2)}) collective-permute-start(bf16[2,2,8,1152]{3,2,1,0:T(8,128)(2,1)S(1)} %get-tuple-element.62), channel_id=1, source_target_pairs={{0,10},{1,11},{2,8},{3,9},{4,14},{5,15},{6,12},{7,13},{8,2},{9,3},... | collective-permute-start | bytes 221192 | tf_op jit(solution)/shard_map/ppermute | solution.py:185
  41.5 2.4 %collective-permute-start.14 = (bf16[2,2,8,1152]{3,2,1,0:T(8,128)(2,1)S(1)}, bf16[2,2,8,1152]{3,2,1,0:T(8,128)(2,1)S(1)}, u32[]{:S(2)}, u32[]{:S(2)}) collective-permute-start(bf16[2,2,8,1152]{3,2,1,0:T(8,128)(2,1)S(1)} %get-tuple-element.63), channel_id=1, source_target_pairs={{0,12},{1,13},{2,14},{3,15},{4,8},{5,9},{6,10},{7,11},{8,4},{9,5},... | collective-permute-start | bytes 221192 | tf_op jit(solution)/shard_map/ppermute | solution.py:185
  43.9 1.5 %collective-permute-start.15 = (bf16[2,2,8,1152]{3,2,1,0:T(8,128)(2,1)S(1)}, bf16[2,2,8,1152]{3,2,1,0:T(8,128)(2,1)S(1)}, u32[]{:S(2)}, u32[]{:S(2)}) collective-permute-start(bf16[2,2,8,1152]{3,2,1,0:T(8,128)(2,1)S(1)} %get-tuple-element.64), channel_id=1, source_target_pairs={{0,14},{1,15},{2,12},{3,13},{4,10},{5,11},{6,8},{7,9},{8,6},{9,7},... | collective-permute-start | bytes 221192 | tf_op jit(solution)/shard_map/ppermute | solution.py:185
  45.4 6.6 %collective-permute-done.13.refs_5_ = bf16[2,2,8,1152]{3,2,1,0:T(8,128)(2,1)S(1)} collective-permute-done((bf16[2,2,8,1152]{3,2,1,0:T(8,128)(2,1)S(1)}, bf16[2,2,8,1152]{3,2,1,0:T(8,128)(2,1)S(1)}, u32[]{:S(2)}, u32[]{:S(2)}) %collective-permute-start.13) | collective-permute-done | bytes 73760 | tf_op jit(solution)/shard_map/ppermute | solution.py:185
  52.0 2.8 %project.1 = f32[2,128,1152]{2,1,0:T(8,128)} custom-call(bf16[2,2,8,1152]{3,2,1,0:T(8,128)(2,1)S(1)} %get-tuple-element.57.refs_0_, bf16[2,2,8,1152]{3,2,1,0:T(8,128)(2,1)S(1)} %collective-permute-done.9.refs_1_, bf16[2,2,8,1152]{3,2,1,0:T(8,128)(2,1)S(1)} %collective-permute-done.10.refs_2_, bf16[2,2,8,1152]{3,2,1,0:T(8,128)(2,1)S(1)} %collective-permute-done.11.refs_3_, ...), custom_call_target="tpu_custom_call" | custom-call | tf_op jit(solution)/shard_map/project/pallas_call | solution.py:387
  (20 shorter events, 0.2 us)
Async XLA Ops:
  2.5 1.8 %collective-permute-start = (bf16[8,2,8,1152]{3,2,1,0:T(8,128)(2,1)S(1)}, bf16[8,2,8,1152]{3,2,1,0:T(8,128)(2,1)S(1)}, u32[]{:S(2)}, u32[]{:S(2)}) collective-permute-start(bf16[8,2,8,1152]{3,2,1,0:T(8,128)(2,1)S(1)} %get-tuple-element.36), channel_id=1, source_target_pairs={{0,1},{1,0},{2,3},{3,2},{4,5},{5,4},{6,7},{7,6},{8,9},{9,8},{10,11... | collective-permute-start | bytes 884744 | tf_op jit(solution)/shard_map/ppermute | solution.py:182
  4.3 10.6 %collective-permute-start.5 = (bf16[2,2,8,1152]{3,2,1,0:T(8,128)(2,1)S(1)}, bf16[2,2,8,1152]{3,2,1,0:T(8,128)(2,1)S(1)}, u32[]{:S(2)}, u32[]{:S(2)}) collective-permute-start(bf16[2,2,8,1152]{3,2,1,0:T(8,128)(2,1)S(1)} %get-tuple-element.49), channel_id=1, source_target_pairs={{0,8},{1,9},{2,10},{3,11},{4,12},{5,13},{6,14},{7,15},{8,0},{9,1},... | collective-permute-start | bytes 221192 | tf_op jit(solution)/shard_map/ppermute | solution.py:185
  8.3 11.3 %collective-permute-start.6 = (bf16[2,2,8,1152]{3,2,1,0:T(8,128)(2,1)S(1)}, bf16[2,2,8,1152]{3,2,1,0:T(8,128)(2,1)S(1)}, u32[]{:S(2)}, u32[]{:S(2)}) collective-permute-start(bf16[2,2,8,1152]{3,2,1,0:T(8,128)(2,1)S(1)} %get-tuple-element.50), channel_id=1, source_target_pairs={{0,10},{1,11},{2,8},{3,9},{4,14},{5,15},{6,12},{7,13},{8,2},{9,3},... | collective-permute-start | bytes 221192 | tf_op jit(solution)/shard_map/ppermute | solution.py:185
  9.6 15.3 %collective-permute-start.7 = (bf16[2,2,8,1152]{3,2,1,0:T(8,128)(2,1)S(1)}, bf16[2,2,8,1152]{3,2,1,0:T(8,128)(2,1)S(1)}, u32[]{:S(2)}, u32[]{:S(2)}) collective-permute-start(bf16[2,2,8,1152]{3,2,1,0:T(8,128)(2,1)S(1)} %get-tuple-element.51), channel_id=1, source_target_pairs={{0,12},{1,13},{2,14},{3,15},{4,8},{5,9},{6,10},{7,11},{8,4},{9,5},... | collective-permute-start | bytes 221192 | tf_op jit(solution)/shard_map/ppermute | solution.py:185
  13.2 14.2 %collective-permute-start.1 = (bf16[2,2,8,1152]{3,2,1,0:T(8,128)(2,1)S(1)}, bf16[2,2,8,1152]{3,2,1,0:T(8,128)(2,1)S(1)}, u32[]{:S(2)}, u32[]{:S(2)}) collective-permute-start(bf16[2,2,8,1152]{3,2,1,0:T(8,128)(2,1)S(1)} %get-tuple-element.37), channel_id=1, source_target_pairs={{0,14},{1,15},{2,12},{3,13},{4,10},{5,11},{6,8},{7,9},{8,6},{9,7},... | collective-permute-start | bytes 221192 | tf_op jit(solution)/shard_map/ppermute | solution.py:185
  13.2 14.2 %collective-permute-start.2 = (bf16[2,2,8,1152]{3,2,1,0:T(8,128)(2,1)S(1)}, bf16[2,2,8,1152]{3,2,1,0:T(8,128)(2,1)S(1)}, u32[]{:S(2)}, u32[]{:S(2)}) collective-permute-start(bf16[2,2,8,1152]{3,2,1,0:T(8,128)(2,1)S(1)} %get-tuple-element.38), channel_id=1, source_target_pairs={{0,2},{1,3},{2,0},{3,1},{4,6},{5,7},{6,4},{7,5},{8,10},{9,11},{10,... | collective-permute-start | bytes 221192 | tf_op jit(solution)/shard_map/ppermute | solution.py:185
  14.9 12.6 %collective-permute-start.3 = (bf16[2,2,8,1152]{3,2,1,0:T(8,128)(2,1)S(1)}, bf16[2,2,8,1152]{3,2,1,0:T(8,128)(2,1)S(1)}, u32[]{:S(2)}, u32[]{:S(2)}) collective-permute-start(bf16[2,2,8,1152]{3,2,1,0:T(8,128)(2,1)S(1)} %get-tuple-element.39), channel_id=1, source_target_pairs={{0,4},{1,5},{2,6},{3,7},{4,0},{5,1},{6,2},{7,3},{8,12},{9,13},{10,... | collective-permute-start | bytes 221192 | tf_op jit(solution)/shard_map/ppermute | solution.py:185
  19.5 7.9 %collective-permute-start.4 = (bf16[2,2,8,1152]{3,2,1,0:T(8,128)(2,1)S(1)}, bf16[2,2,8,1152]{3,2,1,0:T(8,128)(2,1)S(1)}, u32[]{:S(2)}, u32[]{:S(2)}) collective-permute-start(bf16[2,2,8,1152]{3,2,1,0:T(8,128)(2,1)S(1)} %get-tuple-element.40), channel_id=1, source_target_pairs={{0,6},{1,7},{2,4},{3,5},{4,2},{5,3},{6,0},{7,1},{8,14},{9,15},{10,... | collective-permute-start | bytes 221192 | tf_op jit(solution)/shard_map/ppermute | solution.py:185
  27.4 24.5 %copy-start = (f32[2,1,128,1152]{3,2,1,0:T(8,128)S(1)}, f32[2,1,128,1152]{3,2,1,0:T(8,128)}, u32[]{:S(2)}) copy-start(f32[2,1,128,1152]{3,2,1,0:T(8,128)} %param.7) | copy-start | bytes 3538948
  27.4 24.5 %copy-start.1 = (bf16[1152,1152]{1,0:T(8,128)(2,1)S(1)}, bf16[1152,1152]{1,0:T(8,128)(2,1)}, u32[]{:S(2)}) copy-start(bf16[1152,1152]{1,0:T(8,128)(2,1)} %refs_8_.1) | copy-start | bytes 7962628
  32.0 1.6 %collective-permute-start.8 = (bf16[8,2,8,1152]{3,2,1,0:T(8,128)(2,1)S(1)}, bf16[8,2,8,1152]{3,2,1,0:T(8,128)(2,1)S(1)}, u32[]{:S(2)}, u32[]{:S(2)}) collective-permute-start(bf16[8,2,8,1152]{3,2,1,0:T(8,128)(2,1)S(1)} %get-tuple-element.56), channel_id=1, source_target_pairs={{0,1},{1,0},{2,3},{3,2},{4,5},{5,4},{6,7},{7,6},{8,9},{9,8},{10,11... | collective-permute-start | bytes 884744 | tf_op jit(solution)/shard_map/ppermute | solution.py:182
  33.7 7.9 %collective-permute-start.9 = (bf16[2,2,8,1152]{3,2,1,0:T(8,128)(2,1)S(1)}, bf16[2,2,8,1152]{3,2,1,0:T(8,128)(2,1)S(1)}, u32[]{:S(2)}, u32[]{:S(2)}) collective-permute-start(bf16[2,2,8,1152]{3,2,1,0:T(8,128)(2,1)S(1)} %get-tuple-element.58), channel_id=1, source_target_pairs={{0,2},{1,3},{2,0},{3,1},{4,6},{5,7},{6,4},{7,5},{8,10},{9,11},{10,... | collective-permute-start | bytes 221192 | tf_op jit(solution)/shard_map/ppermute | solution.py:185
  34.7 9.2 %collective-permute-start.10 = (bf16[2,2,8,1152]{3,2,1,0:T(8,128)(2,1)S(1)}, bf16[2,2,8,1152]{3,2,1,0:T(8,128)(2,1)S(1)}, u32[]{:S(2)}, u32[]{:S(2)}) collective-permute-start(bf16[2,2,8,1152]{3,2,1,0:T(8,128)(2,1)S(1)} %get-tuple-element.59), channel_id=1, source_target_pairs={{0,4},{1,5},{2,6},{3,7},{4,0},{5,1},{6,2},{7,3},{8,12},{9,13},{10,... | collective-permute-start | bytes 221192 | tf_op jit(solution)/shard_map/ppermute | solution.py:185
  36.3 9.1 %collective-permute-start.11 = (bf16[2,2,8,1152]{3,2,1,0:T(8,128)(2,1)S(1)}, bf16[2,2,8,1152]{3,2,1,0:T(8,128)(2,1)S(1)}, u32[]{:S(2)}, u32[]{:S(2)}) collective-permute-start(bf16[2,2,8,1152]{3,2,1,0:T(8,128)(2,1)S(1)} %get-tuple-element.60), channel_id=1, source_target_pairs={{0,6},{1,7},{2,4},{3,5},{4,2},{5,3},{6,0},{7,1},{8,14},{9,15},{10,... | collective-permute-start | bytes 221192 | tf_op jit(solution)/shard_map/ppermute | solution.py:185
  37.6 7.7 %collective-permute-start.12 = (bf16[2,2,8,1152]{3,2,1,0:T(8,128)(2,1)S(1)}, bf16[2,2,8,1152]{3,2,1,0:T(8,128)(2,1)S(1)}, u32[]{:S(2)}, u32[]{:S(2)}) collective-permute-start(bf16[2,2,8,1152]{3,2,1,0:T(8,128)(2,1)S(1)} %get-tuple-element.61), channel_id=1, source_target_pairs={{0,8},{1,9},{2,10},{3,11},{4,12},{5,13},{6,14},{7,15},{8,0},{9,1},... | collective-permute-start | bytes 221192 | tf_op jit(solution)/shard_map/ppermute | solution.py:185
  40.6 11.4 %collective-permute-start.13 = (bf16[2,2,8,1152]{3,2,1,0:T(8,128)(2,1)S(1)}, bf16[2,2,8,1152]{3,2,1,0:T(8,128)(2,1)S(1)}, u32[]{:S(2)}, u32[]{:S(2)}) collective-permute-start(bf16[2,2,8,1152]{3,2,1,0:T(8,128)(2,1)S(1)} %get-tuple-element.62), channel_id=1, source_target_pairs={{0,10},{1,11},{2,8},{3,9},{4,14},{5,15},{6,12},{7,13},{8,2},{9,3},... | collective-permute-start | bytes 221192 | tf_op jit(solution)/shard_map/ppermute | solution.py:185
  41.5 10.4 %collective-permute-start.14 = (bf16[2,2,8,1152]{3,2,1,0:T(8,128)(2,1)S(1)}, bf16[2,2,8,1152]{3,2,1,0:T(8,128)(2,1)S(1)}, u32[]{:S(2)}, u32[]{:S(2)}) collective-permute-start(bf16[2,2,8,1152]{3,2,1,0:T(8,128)(2,1)S(1)} %get-tuple-element.63), channel_id=1, source_target_pairs={{0,12},{1,13},{2,14},{3,15},{4,8},{5,9},{6,10},{7,11},{8,4},{9,5},... | collective-permute-start | bytes 221192 | tf_op jit(solution)/shard_map/ppermute | solution.py:185
  43.9 8.1 %collective-permute-start.15 = (bf16[2,2,8,1152]{3,2,1,0:T(8,128)(2,1)S(1)}, bf16[2,2,8,1152]{3,2,1,0:T(8,128)(2,1)S(1)}, u32[]{:S(2)}, u32[]{:S(2)}) collective-permute-start(bf16[2,2,8,1152]{3,2,1,0:T(8,128)(2,1)S(1)} %get-tuple-element.64), channel_id=1, source_target_pairs={{0,14},{1,15},{2,12},{3,13},{4,10},{5,11},{6,8},{7,9},{8,6},{9,7},... | collective-permute-start | bytes 221192 | tf_op jit(solution)/shard_map/ppermute | solution.py:185
where the time goes:
time: 55.2 us; the launch traced here: 54.8 us
  starting transfers between devices  25.8 us (47%)
  Pallas kernels  16 us (29%)
  waiting for transfers between devices  12.1 us (22%)
  between operations  0.79 us (1%)
    ppermute x14, starting transfers between devices, swap_parts(): parts[j] = lax.ppermute(parts[j], 'seq', [(s, s ^ 2 * j) for s in range(n)])  25.2 us
    ppermute x14, waiting for transfers between devices, swap_parts(): parts[j] = lax.ppermute(parts[j], 'seq', [(s, s ^ 2 * j) for s in range(n)])  9.34 us
    pallas_call x1, Pallas kernels, attend(): pl.pallas_call(functools.partial(attend_kernel, len(xs), outs, places, bo...  4.49 us
    pallas_call x1, Pallas kernels, project(): pl.pallas_call(functools.partial(project_kernel, exchange, len(xs)), out_...  2.8 us
    ppermute x2, waiting for transfers between devices, swap_parts(): got = lax.ppermute(give, 'seq', [(s, s ^ 1) for s in range(n)])  2.78 us
    pallas_call x1, Pallas kernels, stage_rest(): pl.pallas_call(stage_rest_kernel, out_shape=[VMEM((width, width), w.dtype...  2.63 us
    pallas_call x1, Pallas kernels, early_heads(): pl.pallas_call(functools.partial(heads_kernel, len(xs)), out_shape=head_s...  2.47 us
    pallas_call x1, Pallas kernels, modulate(): pl.pallas_call(functools.partial(modulate_kernel, exchange), out_shape=[p...  1.8 us
  transfers between devices with their start and end apart: 16, of which 4 were waited for; matrix products, arithmetic and copies ran while one was open for 0% of the time, Pallas kernels for 13%

commit v1 on v0

--- a/solution.py
+++ b/solution.py
@@ -71,11 +71,7 @@
     return pl.pallas_call(
         functools.partial(modulate_kernel, exchange),
         out_shape=[part] * outs + [VMEM((1, width), F32)],
-        in_specs=[
-            pl.BlockSpec(memory_space=pltpu.SMEM),
-            pl.BlockSpec(memory_space=pltpu.HBM),
-            pl.BlockSpec(memory_space=pltpu.HBM),
-        ],
+        in_specs=[pl.BlockSpec(memory_space=pltpu.SMEM)] + [pl.BlockSpec(memory_space=pltpu.HBM)] * 2,
         out_specs=[pl.BlockSpec(memory_space=VMEM)] * (outs + 1),
         scratch_shapes=[
             VMEM((branch, patches, width), F32),
@@ -175,7 +171,8 @@
 
 
 def send_order(n):
-    return [*range(n // 4, n // 2), *range(1, n // 4)]
+    far, near = [*range(n // 4, n // 2)], [*range(1, n // 4)]
+    return [*far[:2], *near[-1:], *far[:1:-1], *near[-2::-1]]
 
 
 def swap_parts(n, keep, give):
@@ -203,14 +200,13 @@
     return high, wide - high.astype(F32)
 
 
-def head_scale(vectors, gather, spread):
+def head_factor(vectors, gather):
     high, low = high_low(vectors * vectors)
     square = jnp.dot(high, gather, preferred_element_type=F32)
     square += jnp.dot(low.astype(BF16), gather, preferred_element_type=F32)
     high, low = high_low(lax.rsqrt(square * (1.0 / HEAD_DIM) + 1e-06))
     place = lax.broadcasted_iota(jnp.int32, low.shape, 1)
-    both = jnp.where(place < HEADS, high.astype(F32), low).astype(BF16)
-    return vectors * jnp.dot(both, spread, preferred_element_type=F32)
+    return jnp.where(place < HEADS, high.astype(F32), low).astype(BF16)
 
 
 def pair_masks():
@@ -224,7 +220,7 @@
 
 
 def heads(x_refs, *refs):
-    *w_refs, gather_ref, spread_ref, q_gain_ref, k_gain_ref, q_ref, k_ref, v_ref = refs
+    *w_refs, gather_ref, spread_ref, q_gain_ref, k_gain_ref, q_ref, k_ref, v_ref, wide_ref = refs
     _, branch, share, width = x_refs[0].shape
     x = gather_rows(x_refs)
     gather, spread = gather_ref[...], spread_ref[...]
@@ -244,10 +240,17 @@
                     part = own[:, i * LANES : (i + 2) * LANES]
                     ref[b, i, side] = (part * row).astype(BF16)
 
-    store_pairs(head_scale(product(0), gather, spread), q_gain_ref, q_ref)
-    for b, own in enumerate(per_branch(head_scale(product(1), gather, spread))):
+    def scaled(part, factor):
+        return wide_ref[part] * jnp.dot(factor, spread, preferred_element_type=F32)
+
+    wide_ref[0] = product(0)
+    wide_ref[1] = product(1)
+    q_factor = head_factor(wide_ref[0], gather)
+    store_pairs(product(2), None, v_ref)
+    k_factor = head_factor(wide_ref[1], gather)
+    store_pairs(scaled(0, q_factor), q_gain_ref, q_ref)
+    for b, own in enumerate(per_branch(scaled(1, k_factor))):
         k_ref[b] = (own * k_gain_ref[...]).astype(BF16)
-    store_pairs(product(2), None, v_ref)
 
 
 def head_shapes(xs):
@@ -257,6 +260,11 @@
     return [VMEM(shape, BF16) for shape in (pairs, (branch, tokens, width), pairs)]
 
 
+def wide_shape(xs):
+    _, branch, share, width = xs[0].shape
+    return VMEM((2, sum(x.shape[0] for x in xs) * branch * share, width), F32)
+
+
 def heads_kernel(ins, *refs):
     heads(refs[:ins], *refs[ins:])
 
@@ -267,6 +275,7 @@
         out_shape=head_shapes(xs),
         in_specs=[pl.BlockSpec(memory_space=VMEM)] * (len(xs) + len(tables)),
         out_specs=[pl.BlockSpec(memory_space=VMEM)] * 3,
+        scratch_shapes=[wide_shape(xs)],
         compiler_params=params(10),
         name="heads",
     )(*xs, *tables)
@@ -275,8 +284,8 @@
 def attend_kernel(ins, outs, places, has_early, *refs):
     x_refs, table_refs, refs = refs[:ins], refs[ins : ins + 7], refs[ins + 7 :]
     early, refs = (refs[:3], refs[3:]) if has_early else ((), refs)
-    out_refs, late, scores_ref, probs_ref = refs[:outs], refs[outs:-2], refs[-2], refs[-1]
-    heads(x_refs, *table_refs, *late)
+    out_refs, (*late, wide_ref, scores_ref, probs_ref) = refs[:outs], refs[outs:]
+    heads(x_refs, *table_refs, *late, wide_ref)
     _, branch, share, width = x_refs[0].shape
     halves = [early, late] if has_early else [late]
     tokens = sum(half[1].shape[1] for half in halves)
@@ -358,6 +367,7 @@
         out_specs=[pl.BlockSpec(memory_space=VMEM)] * outs,
         scratch_shapes=[
             *head_shapes(xs),
+            wide_shape(xs),
             VMEM((branch * HEADS // 2, tokens, 2 * tokens), F32),
             VMEM((branch * HEADS // 2, 2 * tokens, tokens), BF16),
         ],
@@ -366,26 +376,20 @@
     )(*xs, *tables, *early)
 
 
-def project_kernel(exchange, ins, *refs):
+def project_kernel(ins, *refs):
     x_refs, (w_ref, gate_ref, residual_ref, out_ref) = refs[:ins], refs[ins:]
     _, branch, share, _ = x_refs[0].shape
     output = jnp.dot(gather_rows(x_refs), w_ref[...], preferred_element_type=F32)
     gated = (gate_ref[...] * output).reshape(-1, branch, share, output.shape[-1])
     for b in range(branch):
-        if not exchange:
-            out_ref[b] = residual_ref[b] + gated[:, b].reshape(out_ref.shape[1:])
-            continue
-        for at in range(gated.shape[0]):
-            start = pl.multiple_of(block_of(at // 2, at % 2, exchange) * share, share)
-            block = pl.ds(start, share)
-            out_ref[b, block] = residual_ref[b, block] + gated[at, b]
-
-
-def project(xs, w_proj, gate_row, rows, exchange):
+        out_ref[b] = residual_ref[b] + gated[:, b].reshape(out_ref.shape[1:])
+
+
+def project(xs, w_proj, gate_row, rows):
     branch, patches, width = rows.shape
     cols = 384
     return pl.pallas_call(
-        functools.partial(project_kernel, exchange, len(xs)),
+        functools.partial(project_kernel, len(xs)),
         out_shape=jax.ShapeDtypeStruct(rows.shape, F32),
         grid=(width // cols,),
         in_specs=[pl.BlockSpec(x.shape, lambda j: (0, 0, 0, 0)) for x in xs]
@@ -400,6 +404,59 @@
     )(*xs, w_proj, gate_row, rows)
 
 
+def project_part_kernel(places, *refs):
+    ins = len(places)
+    x_refs, (w_ref, gate_ref, residual_ref) = refs[:ins], refs[ins : ins + 3]
+    out_hbm, buffer_ref, sems = refs[-3:]
+    _, branch, share, width = x_refs[0].shape
+    x = gather_rows(x_refs)
+    core = lax.rem(lax.axis_index("seq"), 2)
+    cols = width // 3
+    copies = []
+    for at in range(0, width, cols):
+        columns = pl.ds(at, cols)
+        output = jnp.dot(x, w_ref[:, columns], preferred_element_type=F32)
+        gated = (gate_ref[:, columns] * output).reshape(ins, 2, branch, share, cols)
+        for slot, j in enumerate(places):
+            start = pl.multiple_of((block_of(j, 0, True) - core) * share, 2 * share)
+            for b in range(branch):
+                for r in range(2):
+                    own = pl.multiple_of(jnp.bitwise_xor(core, r) * share, share)
+                    block = pl.ds(pl.multiple_of(start + own, share), share)
+                    buffer_ref[slot, b, pl.ds(own, share), columns] = (
+                        residual_ref[b, block, columns] + gated[slot, r, b]
+                    )
+                copies.append(
+                    pltpu.make_async_copy(
+                        buffer_ref.at[slot, b, :, columns],
+                        out_hbm.at[b, pl.ds(start, 2 * share), columns],
+                        sems.at[len(copies)],
+                    )
+                )
+                copies[-1].start()
+    for copy in copies:
+        copy.wait()
+
+
+def project_part(xs, places, w_proj, gate_row, rows, before):
+    branch, _, width = rows.shape
+    share = xs[0].shape[2]
+    hbm = pl.BlockSpec(memory_space=pltpu.HBM)
+    return pl.pallas_call(
+        functools.partial(project_part_kernel, places),
+        out_shape=pltpu.HBM(rows.shape, F32),
+        in_specs=[pl.BlockSpec(memory_space=VMEM)] * (len(xs) + 3) + [hbm] * len(before),
+        out_specs=hbm,
+        scratch_shapes=[
+            VMEM((len(xs), branch, 2 * share, width), F32),
+            pltpu.SemaphoreType.DMA((3 * branch * len(xs),)),
+        ],
+        input_output_aliases={len(xs) + 3: 0} if before else {},
+        compiler_params=params(6),
+        name="project",
+    )(*xs, w_proj, gate_row, rows, *before)
+
+
 def body(n, exchange, residual, w_qkv, w_proj, q_gain, k_gain, step_mods, timestep):
     rows = residual[:, 0]
     if exchange:
@@ -420,7 +477,13 @@
         early = early_heads([parts[j] for j in first], tables)
         parts = [parts[j] for j in places[n // 4 :]]
     parts = swap(*attend(parts, tables, early, places, n, 2 if exchange else 1))
-    return project(parts, w_proj, gate_row, rows, exchange)[:, None]
+    if not exchange:
+        return project(parts, w_proj, gate_row, rows)[:, None]
+    out = []
+    for part in (places[: n // 4], places[n // 4 :]):
+        own = [parts[j] for j in part]
+        out = [project_part(own, part, w_proj, gate_row, rows, out)]
+    return out[0][:, None]
 
 
 def solution(mesh):

time: 55.2 us -> 52.3 us (0.947)
  starting transfers between devices: 25.8 us -> 24.1 us
    ppermute x14, starting transfers between devices: 25.2 us -> 23.5 us  [swap_parts(): parts[j] = lax.ppermute(parts[j], 'seq', [(s, s ^ 2 * j) for s in range(n)])]
    pallas_call x1 -> x2, Pallas kernels: 2.8 us -> 3.08 us  [project_part(): pl.pallas_call(functools.partial(project_part_kernel, places), out_shape=...]
  transfers between devices with their start and end apart: 16 -> 16, of which waited for: 4 -> 6; matrix products, arithmetic and copies ran while one was open for 0% -> 0% of each run, Pallas kernels for 13% -> 15%
where the time goes in v1:
time: 52.3 us; the launch traced here: 52.1 us
  starting transfers between devices  24.1 us (46%)
  Pallas kernels  15.6 us (30%)
  waiting for transfers between devices  11.6 us (22%)
  between operations  0.81 us (2%)
    ppermute x14, starting transfers between devices, swap_parts(): parts[j] = lax.ppermute(parts[j], 'seq', [(s, s ^ 2 * j) for s in range(n)])  23.5 us
    ppermute x14, waiting for transfers between devices, swap_parts(): parts[j] = lax.ppermute(parts[j], 'seq', [(s, s ^ 2 * j) for s in range(n)])  8.84 us
    pallas_call x1, Pallas kernels, attend(): pl.pallas_call(functools.partial(attend_kernel, len(xs), outs, places, bo...  4.19 us
    pallas_call x2, Pallas kernels, project_part(): pl.pallas_call(functools.partial(project_part_kernel, places), out_shape=...  3.08 us
    ppermute x2, waiting for transfers between devices, swap_parts(): got = lax.ppermute(give, 'seq', [(s, s ^ 1) for s in range(n)])  2.78 us
    pallas_call x1, Pallas kernels, stage_rest(): pl.pallas_call(stage_rest_kernel, out_shape=[VMEM((width, width), w.dtype...  2.63 us
    pallas_call x1, Pallas kernels, early_heads(): pl.pallas_call(functools.partial(heads_kernel, len(xs)), out_shape=head_s...  2.07 us
    pallas_call x1, Pallas kernels, modulate(): pl.pallas_call(functools.partial(modulate_kernel, exchange), out_shape=[p...  1.8 us
  transfers between devices with their start and end apart: 16, of which 6 were waited for; matrix products, arithmetic and copies ran while one was open for 0% of the time, Pallas kernels for 15%

profile of v1, /device:TPU:0, one launch (start us, length us, event | category | flops | bytes accessed | tf_op | source)
XLA Modules:
  0.0 52.1 jit_solution(175243890380675409)
XLA Ops:
  0.7 1.8 %modulate.1 = (bf16[8,2,8,1152]{3,2,1,0:T(8,128)(2,1)S(1)}, bf16[8,2,8,1152]{3,2,1,0:T(8,128)(2,1)S(1)}, f32[1,1152]{1,0:T(1,128)S(1)}) custom-call(s32[1]{0:T(128)S(6)} %copy.11.step_ref, f32[2,128,1152]{2,1,0:T(8,128)} %bitcast.5, f32[3,30,1152]{2,1,0:T(8,128)} %bitcast.8), custom_call_target="tpu_custom_call" | custom-call | tf_op jit(solution)/shard_map/modulate/pallas_call | solution.py:71
  3.0 1.2 %collective-permute-done.got_ref = bf16[8,2,8,1152]{3,2,1,0:T(8,128)(2,1)S(1)} collective-permute-done((bf16[8,2,8,1152]{3,2,1,0:T(8,128)(2,1)S(1)}, bf16[8,2,8,1152]{3,2,1,0:T(8,128)(2,1)S(1)}, u32[]{:S(2)}, u32[]{:S(2)}) %collective-permute-start) | collective-permute-done | bytes 294944 | tf_op jit(solution)/shard_map/ppermute | solution.py:179
  4.3 4.0 %collective-permute-start.5 = (bf16[2,2,8,1152]{3,2,1,0:T(8,128)(2,1)S(1)}, bf16[2,2,8,1152]{3,2,1,0:T(8,128)(2,1)S(1)}, u32[]{:S(2)}, u32[]{:S(2)}) collective-permute-start(bf16[2,2,8,1152]{3,2,1,0:T(8,128)(2,1)S(1)} %get-tuple-element.49), channel_id=1, source_target_pairs={{0,8},{1,9},{2,10},{3,11},{4,12},{5,13},{6,14},{7,15},{8,0},{9,1},... | collective-permute-start | bytes 221192 | tf_op jit(solution)/shard_map/ppermute | solution.py:182
  8.3 1.3 %collective-permute-start.6 = (bf16[2,2,8,1152]{3,2,1,0:T(8,128)(2,1)S(1)}, bf16[2,2,8,1152]{3,2,1,0:T(8,128)(2,1)S(1)}, u32[]{:S(2)}, u32[]{:S(2)}) collective-permute-start(bf16[2,2,8,1152]{3,2,1,0:T(8,128)(2,1)S(1)} %get-tuple-element.50), channel_id=1, source_target_pairs={{0,10},{1,11},{2,8},{3,9},{4,14},{5,15},{6,12},{7,13},{8,2},{9,3},... | collective-permute-start | bytes 221192 | tf_op jit(solution)/shard_map/ppermute | solution.py:182
  9.6 1.5 %collective-permute-start.7 = (bf16[2,2,8,1152]{3,2,1,0:T(8,128)(2,1)S(1)}, bf16[2,2,8,1152]{3,2,1,0:T(8,128)(2,1)S(1)}, u32[]{:S(2)}, u32[]{:S(2)}) collective-permute-start(bf16[2,2,8,1152]{3,2,1,0:T(8,128)(2,1)S(1)} %get-tuple-element.51), channel_id=1, source_target_pairs={{0,6},{1,7},{2,4},{3,5},{4,2},{5,3},{6,0},{7,1},{8,14},{9,15},{10,... | collective-permute-start | bytes 221192 | tf_op jit(solution)/shard_map/ppermute | solution.py:182
  11.1 3.4 %collective-permute-start.1 = (bf16[2,2,8,1152]{3,2,1,0:T(8,128)(2,1)S(1)}, bf16[2,2,8,1152]{3,2,1,0:T(8,128)(2,1)S(1)}, u32[]{:S(2)}, u32[]{:S(2)}) collective-permute-start(bf16[2,2,8,1152]{3,2,1,0:T(8,128)(2,1)S(1)} %get-tuple-element.37), channel_id=1, source_target_pairs={{0,14},{1,15},{2,12},{3,13},{4,10},{5,11},{6,8},{7,9},{8,6},{9,7},... | collective-permute-start | bytes 221192 | tf_op jit(solution)/shard_map/ppermute | solution.py:182
  14.5 1.3 %collective-permute-start.2 = (bf16[2,2,8,1152]{3,2,1,0:T(8,128)(2,1)S(1)}, bf16[2,2,8,1152]{3,2,1,0:T(8,128)(2,1)S(1)}, u32[]{:S(2)}, u32[]{:S(2)}) collective-permute-start(bf16[2,2,8,1152]{3,2,1,0:T(8,128)(2,1)S(1)} %get-tuple-element.38), channel_id=1, source_target_pairs={{0,12},{1,13},{2,14},{3,15},{4,8},{5,9},{6,10},{7,11},{8,4},{9,5},... | collective-permute-start | bytes 221192 | tf_op jit(solution)/shard_map/ppermute | solution.py:182
  15.9 3.6 %collective-permute-done.6.refs_2_ = bf16[2,2,8,1152]{3,2,1,0:T(8,128)(2,1)S(1)} collective-permute-done((bf16[2,2,8,1152]{3,2,1,0:T(8,128)(2,1)S(1)}, bf16[2,2,8,1152]{3,2,1,0:T(8,128)(2,1)S(1)}, u32[]{:S(2)}, u32[]{:S(2)}) %collective-permute-start.6) | collective-permute-done | bytes 73760 | tf_op jit(solution)/shard_map/ppermute | solution.py:182
  19.5 1.3 %collective-permute-start.4 = (bf16[2,2,8,1152]{3,2,1,0:T(8,128)(2,1)S(1)}, bf16[2,2,8,1152]{3,2,1,0:T(8,128)(2,1)S(1)}, u32[]{:S(2)}, u32[]{:S(2)}) collective-permute-start(bf16[2,2,8,1152]{3,2,1,0:T(8,128)(2,1)S(1)} %get-tuple-element.40), channel_id=1, source_target_pairs={{0,2},{1,3},{2,0},{3,1},{4,6},{5,7},{6,4},{7,5},{8,10},{9,11},{10,... | collective-permute-start | bytes 221192 | tf_op jit(solution)/shard_map/ppermute | solution.py:182
  20.8 1.8 %stage_first.1.refs_4_ = bf16[1152,1152]{1,0:T(8,128)(2,1)S(1)} custom-call(f32[1,1152]{1,0:T(1,128)S(1)} %get-tuple-element.41.after_ref.refs_5_, bf16[1152,3456]{1,0:T(8,128)(2,1)} %w_hbm.3), custom_call_target="tpu_custom_call" | custom-call | tf_op jit(solution)/shard_map/stage_first/pallas_call | solution.py:101
  22.6 2.6 %stage_rest.1 = (bf16[1152,1152]{1,0:T(8,128)(2,1)S(1)}, bf16[1152,1152]{1,0:T(8,128)(2,1)S(1)}, bf16[1152,128]{1,0:T(8,128)(2,1)S(1)}, bf16[128,1152]{1,0:T(8,1...) custom-call(f32[1,1152]{1,0:T(1,128)S(1)} %get-tuple-element.41.after_ref.refs_5_, bf16[1152,3456]{1,0:T(8,128)(2,1)} %w_hbm.3, ...), custom_call_target="tpu_custom_call" | custom-call | tf_op jit(solution)/shard_map/stage_rest/pallas_call | solution.py:137
  25.2 2.1 %heads.1 = (bf16[2,8,2,64,256]{4,3,2,1,0:T(8,128)(2,1)S(1)}, bf16[2,64,1152]{2,1,0:T(8,128)(2,1)S(1)}, bf16[2,8,2,64,256]{4,3,2,1,0:T(8,128)(2,1)S(1)}) custom-call(bf16[2,2,8,1152]{3,2,1,0:T(8,128)(2,1)S(1)} %get-tuple-element.48.refs_0_, bf16[2,2,8,1152]{3,2,1,0:T(8,128)(2,1)S(1)} %collective-permute-done.5.refs_1_, ...), custom_call_target="tpu_custom_call" | custom-call | tf_op jit(solution)/shard_map/heads/pallas_call | solution.py:273
  27.4 4.2 %attend.1 = (bf16[8,2,8,1152]{3,2,1,0:T(8,128)(2,1)S(1)}, bf16[8,2,8,1152]{3,2,1,0:T(8,128)(2,1)S(1)}) custom-call(bf16[2,2,8,1152]{3,2,1,0:T(8,128)(2,1)S(1)} %collective-permute-done.1.refs_0_, bf16[2,2,8,1152]{3,2,1,0:T(8,128)(2,1)S(1)} %collective-permute-done.2.refs_1_, bf16[2,2,8,1152]{3,2,1,0:T(8,128)(2,1)S(1)} %collective-permute-done.3.refs_2_, ...), custom_call_target="tpu_custom_call" | custom-call | tf_op jit(solution)/shard_map/attend/pallas_call | solution.py:363
  31.6 1.6 %collective-permute-done.8.got_ref = bf16[8,2,8,1152]{3,2,1,0:T(8,128)(2,1)S(1)} collective-permute-done((bf16[8,2,8,1152]{3,2,1,0:T(8,128)(2,1)S(1)}, bf16[8,2,8,1152]{3,2,1,0:T(8,128)(2,1)S(1)}, u32[]{:S(2)}, u32[]{:S(2)}) %collective-permute-start.8) | collective-permute-done | bytes 294944 | tf_op jit(solution)/shard_map/ppermute | solution.py:179
  33.2 1.0 %collective-permute-start.13 = (bf16[2,2,8,1152]{3,2,1,0:T(8,128)(2,1)S(1)}, bf16[2,2,8,1152]{3,2,1,0:T(8,128)(2,1)S(1)}, u32[]{:S(2)}, u32[]{:S(2)}) collective-permute-start(bf16[2,2,8,1152]{3,2,1,0:T(8,128)(2,1)S(1)} %get-tuple-element.62), channel_id=1, source_target_pairs={{0,8},{1,9},{2,10},{3,11},{4,12},{5,13},{6,14},{7,15},{8,0},{9,1},... | collective-permute-start | bytes 221192 | tf_op jit(solution)/shard_map/ppermute | solution.py:182
  34.3 2.1 %collective-permute-start.14 = (bf16[2,2,8,1152]{3,2,1,0:T(8,128)(2,1)S(1)}, bf16[2,2,8,1152]{3,2,1,0:T(8,128)(2,1)S(1)}, u32[]{:S(2)}, u32[]{:S(2)}) collective-permute-start(bf16[2,2,8,1152]{3,2,1,0:T(8,128)(2,1)S(1)} %get-tuple-element.63), channel_id=1, source_target_pairs={{0,10},{1,11},{2,8},{3,9},{4,14},{5,15},{6,12},{7,13},{8,2},{9,3},... | collective-permute-start | bytes 221192 | tf_op jit(solution)/shard_map/ppermute | solution.py:182
  36.4 3.3 %collective-permute-start.9 = (bf16[2,2,8,1152]{3,2,1,0:T(8,128)(2,1)S(1)}, bf16[2,2,8,1152]{3,2,1,0:T(8,128)(2,1)S(1)}, u32[]{:S(2)}, u32[]{:S(2)}) collective-permute-start(bf16[2,2,8,1152]{3,2,1,0:T(8,128)(2,1)S(1)} %get-tuple-element.57), channel_id=1, source_target_pairs={{0,14},{1,15},{2,12},{3,13},{4,10},{5,11},{6,8},{7,9},{8,6},{9,7},... | collective-permute-start | bytes 221192 | tf_op jit(solution)/shard_map/ppermute | solution.py:182
  39.7 2.1 %collective-permute-start.10 = (bf16[2,2,8,1152]{3,2,1,0:T(8,128)(2,1)S(1)}, bf16[2,2,8,1152]{3,2,1,0:T(8,128)(2,1)S(1)}, u32[]{:S(2)}, u32[]{:S(2)}) collective-permute-start(bf16[2,2,8,1152]{3,2,1,0:T(8,128)(2,1)S(1)} %get-tuple-element.58), channel_id=1, source_target_pairs={{0,12},{1,13},{2,14},{3,15},{4,8},{5,9},{6,10},{7,11},{8,4},{9,5},... | collective-permute-start | bytes 221192 | tf_op jit(solution)/shard_map/ppermute | solution.py:182
  41.8 1.4 %collective-permute-start.11 = (bf16[2,2,8,1152]{3,2,1,0:T(8,128)(2,1)S(1)}, bf16[2,2,8,1152]{3,2,1,0:T(8,128)(2,1)S(1)}, u32[]{:S(2)}, u32[]{:S(2)}) collective-permute-start(bf16[2,2,8,1152]{3,2,1,0:T(8,128)(2,1)S(1)} %get-tuple-element.59), channel_id=1, source_target_pairs={{0,4},{1,5},{2,6},{3,7},{4,0},{5,1},{6,2},{7,3},{8,12},{9,13},{10,... | collective-permute-start | bytes 221192 | tf_op jit(solution)/shard_map/ppermute | solution.py:182
  43.2 3.0 %collective-permute-done.14.refs_2_ = bf16[2,2,8,1152]{3,2,1,0:T(8,128)(2,1)S(1)} collective-permute-done((bf16[2,2,8,1152]{3,2,1,0:T(8,128)(2,1)S(1)}, bf16[2,2,8,1152]{3,2,1,0:T(8,128)(2,1)S(1)}, u32[]{:S(2)}, u32[]{:S(2)}) %collective-permute-start.14) | collective-permute-done | bytes 73760 | tf_op jit(solution)/shard_map/ppermute | solution.py:182
  46.8 1.5 %collective-permute-done.15.refs_3_ = bf16[2,2,8,1152]{3,2,1,0:T(8,128)(2,1)S(1)} collective-permute-done((bf16[2,2,8,1152]{3,2,1,0:T(8,128)(2,1)S(1)}, bf16[2,2,8,1152]{3,2,1,0:T(8,128)(2,1)S(1)}, u32[]{:S(2)}, u32[]{:S(2)}) %collective-permute-start.15) | collective-permute-done | bytes 73760 | tf_op jit(solution)/shard_map/ppermute | solution.py:182
  48.3 1.5 %project.2.refs_7_ = f32[2,128,1152]{2,1,0:T(8,128)} custom-call(bf16[2,2,8,1152]{3,2,1,0:T(8,128)(2,1)S(1)} %get-tuple-element.61.refs_0_, bf16[2,2,8,1152]{3,2,1,0:T(8,128)(2,1)S(1)} %collective-permute-done.13.refs_1_, bf16[2,2,8,1152]{3,2,1,0:T(8,128)(2,1)S(1)} %collective-permute-done.14.refs_2_, ...), custom_call_target="tpu_custom_call" | custom-call | tf_op jit(solution)/shard_map/project/pallas_call | solution.py:445
  49.9 0.7 %collective-permute-done.12.refs_3_ = bf16[2,2,8,1152]{3,2,1,0:T(8,128)(2,1)S(1)} collective-permute-done((bf16[2,2,8,1152]{3,2,1,0:T(8,128)(2,1)S(1)}, bf16[2,2,8,1152]{3,2,1,0:T(8,128)(2,1)S(1)}, u32[]{:S(2)}, u32[]{:S(2)}) %collective-permute-start.12) | collective-permute-done | bytes 73760 | tf_op jit(solution)/shard_map/ppermute | solution.py:182
  50.6 1.5 %project.3 = f32[2,128,1152]{2,1,0:T(8,128)} custom-call(bf16[2,2,8,1152]{3,2,1,0:T(8,128)(2,1)S(1)} %collective-permute-done.9.refs_0_, bf16[2,2,8,1152]{3,2,1,0:T(8,128)(2,1)S(1)} %collective-permute-done.10.refs_1_, bf16[2,2,8,1152]{3,2,1,0:T(8,128)(2,1)S(1)} %collective-permute-done.11.refs_2_, ...), custom_call_target="tpu_custom_call", output_to_operand_aliasing={{}: (7, {})} | custom-call | tf_op jit(solution)/shard_map/project/pallas_call | solution.py:445
  (21 shorter events, 1.4 us)
Async XLA Ops:
  2.5 1.8 %collective-permute-start = (bf16[8,2,8,1152]{3,2,1,0:T(8,128)(2,1)S(1)}, bf16[8,2,8,1152]{3,2,1,0:T(8,128)(2,1)S(1)}, u32[]{:S(2)}, u32[]{:S(2)}) collective-permute-start(bf16[8,2,8,1152]{3,2,1,0:T(8,128)(2,1)S(1)} %get-tuple-element.36), channel_id=1, source_target_pairs={{0,1},{1,0},{2,3},{3,2},{4,5},{5,4},{6,7},{7,6},{8,9},{9,8},{10,11... | collective-permute-start | bytes 884744 | tf_op jit(solution)/shard_map/ppermute | solution.py:179
  4.3 11.6 %collective-permute-start.5 = (bf16[2,2,8,1152]{3,2,1,0:T(8,128)(2,1)S(1)}, bf16[2,2,8,1152]{3,2,1,0:T(8,128)(2,1)S(1)}, u32[]{:S(2)}, u32[]{:S(2)}) collective-permute-start(bf16[2,2,8,1152]{3,2,1,0:T(8,128)(2,1)S(1)} %get-tuple-element.49), channel_id=1, source_target_pairs={{0,8},{1,9},{2,10},{3,11},{4,12},{5,13},{6,14},{7,15},{8,0},{9,1},... | collective-permute-start | bytes 221192 | tf_op jit(solution)/shard_map/ppermute | solution.py:182
  8.3 11.2 %collective-permute-start.6 = (bf16[2,2,8,1152]{3,2,1,0:T(8,128)(2,1)S(1)}, bf16[2,2,8,1152]{3,2,1,0:T(8,128)(2,1)S(1)}, u32[]{:S(2)}, u32[]{:S(2)}) collective-permute-start(bf16[2,2,8,1152]{3,2,1,0:T(8,128)(2,1)S(1)} %get-tuple-element.50), channel_id=1, source_target_pairs={{0,10},{1,11},{2,8},{3,9},{4,14},{5,15},{6,12},{7,13},{8,2},{9,3},... | collective-permute-start | bytes 221192 | tf_op jit(solution)/shard_map/ppermute | solution.py:182
  9.6 15.6 %collective-permute-start.7 = (bf16[2,2,8,1152]{3,2,1,0:T(8,128)(2,1)S(1)}, bf16[2,2,8,1152]{3,2,1,0:T(8,128)(2,1)S(1)}, u32[]{:S(2)}, u32[]{:S(2)}) collective-permute-start(bf16[2,2,8,1152]{3,2,1,0:T(8,128)(2,1)S(1)} %get-tuple-element.51), channel_id=1, source_target_pairs={{0,6},{1,7},{2,4},{3,5},{4,2},{5,3},{6,0},{7,1},{8,14},{9,15},{10,... | collective-permute-start | bytes 221192 | tf_op jit(solution)/shard_map/ppermute | solution.py:182
  11.1 16.2 %collective-permute-start.1 = (bf16[2,2,8,1152]{3,2,1,0:T(8,128)(2,1)S(1)}, bf16[2,2,8,1152]{3,2,1,0:T(8,128)(2,1)S(1)}, u32[]{:S(2)}, u32[]{:S(2)}) collective-permute-start(bf16[2,2,8,1152]{3,2,1,0:T(8,128)(2,1)S(1)} %get-tuple-element.37), channel_id=1, source_target_pairs={{0,14},{1,15},{2,12},{3,13},{4,10},{5,11},{6,8},{7,9},{8,6},{9,7},... | collective-permute-start | bytes 221192 | tf_op jit(solution)/shard_map/ppermute | solution.py:182
  14.5 12.8 %collective-permute-start.2 = (bf16[2,2,8,1152]{3,2,1,0:T(8,128)(2,1)S(1)}, bf16[2,2,8,1152]{3,2,1,0:T(8,128)(2,1)S(1)}, u32[]{:S(2)}, u32[]{:S(2)}) collective-permute-start(bf16[2,2,8,1152]{3,2,1,0:T(8,128)(2,1)S(1)} %get-tuple-element.38), channel_id=1, source_target_pairs={{0,12},{1,13},{2,14},{3,15},{4,8},{5,9},{6,10},{7,11},{8,4},{9,5},... | collective-permute-start | bytes 221192 | tf_op jit(solution)/shard_map/ppermute | solution.py:182
  15.9 11.4 %collective-permute-start.3 = (bf16[2,2,8,1152]{3,2,1,0:T(8,128)(2,1)S(1)}, bf16[2,2,8,1152]{3,2,1,0:T(8,128)(2,1)S(1)}, u32[]{:S(2)}, u32[]{:S(2)}) collective-permute-start(bf16[2,2,8,1152]{3,2,1,0:T(8,128)(2,1)S(1)} %get-tuple-element.39), channel_id=1, source_target_pairs={{0,4},{1,5},{2,6},{3,7},{4,0},{5,1},{6,2},{7,3},{8,12},{9,13},{10,... | collective-permute-start | bytes 221192 | tf_op jit(solution)/shard_map/ppermute | solution.py:182
  19.5 7.8 %collective-permute-start.4 = (bf16[2,2,8,1152]{3,2,1,0:T(8,128)(2,1)S(1)}, bf16[2,2,8,1152]{3,2,1,0:T(8,128)(2,1)S(1)}, u32[]{:S(2)}, u32[]{:S(2)}) collective-permute-start(bf16[2,2,8,1152]{3,2,1,0:T(8,128)(2,1)S(1)} %get-tuple-element.40), channel_id=1, source_target_pairs={{0,2},{1,3},{2,0},{3,1},{4,6},{5,7},{6,4},{7,5},{8,10},{9,11},{10,... | collective-permute-start | bytes 221192 | tf_op jit(solution)/shard_map/ppermute | solution.py:182
  27.3 21.0 %copy-start = (bf16[1152,1152]{1,0:T(8,128)(2,1)S(1)}, bf16[1152,1152]{1,0:T(8,128)(2,1)}, u32[]{:S(2)}) copy-start(bf16[1152,1152]{1,0:T(8,128)(2,1)} %refs_4_.3) | copy-start | bytes 7962628
  27.3 21.0 %copy-start.1 = (f32[2,1,128,1152]{3,2,1,0:T(8,128)S(1)}, f32[2,1,128,1152]{3,2,1,0:T(8,128)}, u32[]{:S(2)}) copy-start(f32[2,1,128,1152]{3,2,1,0:T(8,128)} %param.7) | copy-start | bytes 3538948
  31.5 1.6 %collective-permute-start.8 = (bf16[8,2,8,1152]{3,2,1,0:T(8,128)(2,1)S(1)}, bf16[8,2,8,1152]{3,2,1,0:T(8,128)(2,1)S(1)}, u32[]{:S(2)}, u32[]{:S(2)}) collective-permute-start(bf16[8,2,8,1152]{3,2,1,0:T(8,128)(2,1)S(1)} %get-tuple-element.56), channel_id=1, source_target_pairs={{0,1},{1,0},{2,3},{3,2},{4,5},{5,4},{6,7},{7,6},{8,9},{9,8},{10,11... | collective-permute-start | bytes 884744 | tf_op jit(solution)/shard_map/ppermute | solution.py:179
  33.2 8.6 %collective-permute-start.13 = (bf16[2,2,8,1152]{3,2,1,0:T(8,128)(2,1)S(1)}, bf16[2,2,8,1152]{3,2,1,0:T(8,128)(2,1)S(1)}, u32[]{:S(2)}, u32[]{:S(2)}) collective-permute-start(bf16[2,2,8,1152]{3,2,1,0:T(8,128)(2,1)S(1)} %get-tuple-element.62), channel_id=1, source_target_pairs={{0,8},{1,9},{2,10},{3,11},{4,12},{5,13},{6,14},{7,15},{8,0},{9,1},... | collective-permute-start | bytes 221192 | tf_op jit(solution)/shard_map/ppermute | solution.py:182
  34.3 11.9 %collective-permute-start.14 = (bf16[2,2,8,1152]{3,2,1,0:T(8,128)(2,1)S(1)}, bf16[2,2,8,1152]{3,2,1,0:T(8,128)(2,1)S(1)}, u32[]{:S(2)}, u32[]{:S(2)}) collective-permute-start(bf16[2,2,8,1152]{3,2,1,0:T(8,128)(2,1)S(1)} %get-tuple-element.63), channel_id=1, source_target_pairs={{0,10},{1,11},{2,8},{3,9},{4,14},{5,15},{6,12},{7,13},{8,2},{9,3},... | collective-permute-start | bytes 221192 | tf_op jit(solution)/shard_map/ppermute | solution.py:182
  36.4 13.5 %collective-permute-start.9 = (bf16[2,2,8,1152]{3,2,1,0:T(8,128)(2,1)S(1)}, bf16[2,2,8,1152]{3,2,1,0:T(8,128)(2,1)S(1)}, u32[]{:S(2)}, u32[]{:S(2)}) collective-permute-start(bf16[2,2,8,1152]{3,2,1,0:T(8,128)(2,1)S(1)} %get-tuple-element.57), channel_id=1, source_target_pairs={{0,14},{1,15},{2,12},{3,13},{4,10},{5,11},{6,8},{7,9},{8,6},{9,7},... | collective-permute-start | bytes 221192 | tf_op jit(solution)/shard_map/ppermute | solution.py:182
  39.7 8.6 %collective-permute-start.15 = (bf16[2,2,8,1152]{3,2,1,0:T(8,128)(2,1)S(1)}, bf16[2,2,8,1152]{3,2,1,0:T(8,128)(2,1)S(1)}, u32[]{:S(2)}, u32[]{:S(2)}) collective-permute-start(bf16[2,2,8,1152]{3,2,1,0:T(8,128)(2,1)S(1)} %get-tuple-element.64), channel_id=1, source_target_pairs={{0,6},{1,7},{2,4},{3,5},{4,2},{5,3},{6,0},{7,1},{8,14},{9,15},{10,... | collective-permute-start | bytes 221192 | tf_op jit(solution)/shard_map/ppermute | solution.py:182
  39.7 10.2 %collective-permute-start.10 = (bf16[2,2,8,1152]{3,2,1,0:T(8,128)(2,1)S(1)}, bf16[2,2,8,1152]{3,2,1,0:T(8,128)(2,1)S(1)}, u32[]{:S(2)}, u32[]{:S(2)}) collective-permute-start(bf16[2,2,8,1152]{3,2,1,0:T(8,128)(2,1)S(1)} %get-tuple-element.58), channel_id=1, source_target_pairs={{0,12},{1,13},{2,14},{3,15},{4,8},{5,9},{6,10},{7,11},{8,4},{9,5},... | collective-permute-start | bytes 221192 | tf_op jit(solution)/shard_map/ppermute | solution.py:182
  41.8 8.1 %collective-permute-start.11 = (bf16[2,2,8,1152]{3,2,1,0:T(8,128)(2,1)S(1)}, bf16[2,2,8,1152]{3,2,1,0:T(8,128)(2,1)S(1)}, u32[]{:S(2)}, u32[]{:S(2)}) collective-permute-start(bf16[2,2,8,1152]{3,2,1,0:T(8,128)(2,1)S(1)} %get-tuple-element.59), channel_id=1, source_target_pairs={{0,4},{1,5},{2,6},{3,7},{4,0},{5,1},{6,2},{7,3},{8,12},{9,13},{10,... | collective-permute-start | bytes 221192 | tf_op jit(solution)/shard_map/ppermute | solution.py:182
  46.2 4.4 %collective-permute-start.12 = (bf16[2,2,8,1152]{3,2,1,0:T(8,128)(2,1)S(1)}, bf16[2,2,8,1152]{3,2,1,0:T(8,128)(2,1)S(1)}, u32[]{:S(2)}, u32[]{:S(2)}) collective-permute-start(bf16[2,2,8,1152]{3,2,1,0:T(8,128)(2,1)S(1)} %get-tuple-element.60), channel_id=1, source_target_pairs={{0,2},{1,3},{2,0},{3,1},{4,6},{5,7},{6,4},{7,5},{8,10},{9,11},{10,... | collective-permute-start | bytes 221192 | tf_op jit(solution)/shard_map/ppermute | solution.py:182

commit v2 on v1

v2 whole, which is shorter than its diff:
```python
import functools

import jax
import jax.numpy as jnp
from jax import lax
from jax.experimental import pallas as pl
from jax.experimental.pallas import tpu as pltpu
from jax.sharding import PartitionSpec as P

HEADS = 16
HEAD_DIM = 72
LANES = 128
LOG2_E = 1.4426950408889634
F32 = jnp.float32
BF16 = jnp.bfloat16
VMEM = pltpu.VMEM


def params(mebibytes):
    return pltpu.CompilerParams(vmem_limit_bytes=mebibytes << 20)


def in_hbm(array):
    return pltpu.with_memory_space_constraint(array, pltpu.HBM)


def block_of(j, r, exchange):
    if not exchange:
        return j
    me = lax.axis_index("seq")
    return jnp.bitwise_xor(me, 2 * j + r)


def modulate_rows(rows_ref, scale_row, shift_row, out_ref, r, exchange, branches):
    count, _, share, width = out_ref.shape
    group = 1 if exchange else max(1, 32 // share)
    for b in branches:
        for j in range(0, count, group):
            start = block_of(j, r, exchange) * share
            if exchange:
                start = pl.multiple_of(start, share)
            rows = rows_ref[b, pl.ds(start, group * share)]
            centre = jnp.mean(rows, axis=-1, keepdims=True)
            centred = rows - centre
            variance = jnp.mean(centred * centred, axis=-1, keepdims=True)
            normed = centred * lax.rsqrt(variance + 1e-06) * scale_row + shift_row
            out_ref[j : j + group, b] = normed.reshape(group, share, width).astype(BF16)


def modulate_kernel(exchange, step_ref, rows_hbm, mods_hbm, out_ref, *refs):
    scale_ref, shift_ref, gate_ref, rows_ref, mods_ref, sems = refs
    branch = rows_ref.shape[0]

    def fetch(b):
        return pltpu.make_async_copy(rows_hbm.at[b], rows_ref.at[b], sems.at[b])

    mods = pltpu.make_async_copy(mods_hbm, mods_ref, sems.at[branch])
    fetch(0).start()
    mods.start()
    for b in range(1, branch):
        fetch(b).start()
    mods.wait()
    step = pl.ds(step_ref[0], 1)
    shift_row, scale_row = mods_ref[0, step, :], 1.0 + mods_ref[1, step, :]
    shift_ref[...] = shift_row
    scale_ref[...] = scale_row
    gate_ref[...] = mods_ref[2, step, :]
    for b in range(branch):
        fetch(b).wait()
        modulate_rows(rows_ref, scale_row, shift_row, out_ref, 1, exchange, [b])


def modulate(rows, step_mods, timestep, n, exchange):
    branch, patches, width = rows.shape
    outs = 2 if exchange else 1
    row = VMEM((1, width), F32)
    return pl.pallas_call(
        functools.partial(modulate_kernel, exchange),
        out_shape=[
            VMEM((n // outs, branch, patches // n, width), BF16),
            row,
            row,
            row,
            VMEM((branch, patches, width), F32),
        ],
        in_specs=[pl.BlockSpec(memory_space=pltpu.SMEM)]
        + [pl.BlockSpec(memory_space=pltpu.HBM)] * 2,
        out_specs=[pl.BlockSpec(memory_space=VMEM)] * 5,
        scratch_shapes=[
            VMEM((3, step_mods.shape[0], width), F32),
            pltpu.SemaphoreType.DMA((branch + 1,)),
        ],
        compiler_params=params(8),
        name="modulate",
    )(timestep, in_hbm(rows), in_hbm(jnp.swapaxes(step_mods, 0, 1)))


def keep_kernel(rows_ref, scale_ref, shift_ref, out_ref):
    branches = range(rows_ref.shape[0])
    modulate_rows(rows_ref, scale_ref[...], shift_ref[...], out_ref, 0, True, branches)


def modulate_kept(rows, scale_row, shift_row, like):
    return pl.pallas_call(
        keep_kernel,
        out_shape=VMEM(like.shape, BF16),
        in_specs=[pl.BlockSpec(memory_space=VMEM)] * 3,
        out_specs=pl.BlockSpec(memory_space=VMEM),
        compiler_params=params(4),
        name="keep",
    )(rows, scale_row, shift_row)


def tables_kernel(after_ref, q_gain_hbm, k_gain_hbm, *refs):
    gather_ref, spread_ref, q_row_ref, k_row_ref, line_ref, sems = refs
    del after_ref
    gains = [
        pltpu.make_async_copy(gain, line_ref.at[at], sems.at[at])
        for at, gain in enumerate((q_gain_hbm, k_gain_hbm))
    ]
    for copy in gains:
        copy.start()
    gather_ref[...] = head_of(gather_ref.shape, 0)
    spread_ref[...] = head_of(spread_ref.shape, 1)
    for at, row_ref in enumerate((q_row_ref, k_row_ref)):
        gains[at].wait()
        row_ref[...] = line_ref[at].reshape(row_ref.shape)


def make_tables(q_gain, k_gain, after):
    width = q_gain.shape[0]
    hbm = pl.BlockSpec(memory_space=pltpu.HBM)
    return pl.pallas_call(
        tables_kernel,
        out_shape=[
            VMEM((width, LANES), BF16),
            VMEM((LANES, width), BF16),
            VMEM((1, width), F32),
            VMEM((1, width), F32),
        ],
        in_specs=[pl.BlockSpec(memory_space=VMEM), hbm, hbm],
        out_specs=[pl.BlockSpec(memory_space=VMEM)] * 4,
        scratch_shapes=[VMEM((2, width), F32), pltpu.SemaphoreType.DMA((2,))],
        compiler_params=params(2),
        name="tables",
    )(after, in_hbm(q_gain), in_hbm(k_gain))


def pack_kernel(keep_ref, got_ref, *out_refs):
    for j, out_ref in enumerate(out_refs):
        out_ref[0] = keep_ref[j]
        out_ref[1] = got_ref[j]


def pack(keep, got):
    count, *part = keep.shape
    return pl.pallas_call(
        pack_kernel,
        out_shape=[VMEM((2, *part), keep.dtype)] * count,
        in_specs=[pl.BlockSpec(memory_space=VMEM)] * 2,
        out_specs=[pl.BlockSpec(memory_space=VMEM)] * count,
        compiler_params=params(1),
        cost_estimate=pl.CostEstimate(flops=10**10, bytes_accessed=10**7, transcendentals=0),
        name="pack",
    )(keep, got)


def send_order(n):
    far, near = [*range(n // 4, n // 2)], [*range(1, n // 4)]
    return [*far[:2], *near[-1:], *far[:1:-1], *near[-2::-1]]


def swap_parts(n, give, make_keep):
    got = lax.ppermute(give, "seq", [(s, s ^ 1) for s in range(n)])
    keep = make_keep()
    parts = list(pack(keep, got))
    for j in send_order(n):
        parts[j] = lax.ppermute(parts[j], "seq", [(s, s ^ (2 * j)) for s in range(n)])
    return parts


def gather_rows(x_refs):
    return jnp.concatenate([ref[...].reshape(-1, ref.shape[-1]) for ref in x_refs], axis=0)


def head_of(shape, feature_dim):
    feature = lax.broadcasted_iota(jnp.int32, shape, feature_dim)
    place = lax.broadcasted_iota(jnp.int32, shape, 1 - feature_dim)
    first = lax.rem(place, HEADS) * HEAD_DIM
    inside = (feature >= first) & (feature < first + HEAD_DIM) & (place < 2 * HEADS)
    return jnp.where(inside, 1.0, 0.0).astype(BF16)


def high_low(wide):
    high = wide.astype(BF16)
    return high, wide - high.astype(F32)


def head_factors(vectors, gather):
    high, low = high_low(vectors * vectors)
    rows = vectors.shape[0]
    stacked = jnp.concatenate([high, low.astype(BF16)], axis=0)
    square = jnp.dot(stacked, gather, preferred_element_type=F32)
    square = square[:rows] + square[rows:]
    high, low = high_low(lax.rsqrt(square * (1.0 / HEAD_DIM) + 1e-06))
    place = lax.broadcasted_iota(jnp.int32, low.shape, 1)
    return jnp.where(place < HEADS, high.astype(F32), low).astype(BF16)


def pair_masks():
    lane = lax.broadcasted_iota(jnp.int32, (1, 2 * LANES), 1)
    for i in range(HEADS // 2):
        masks = []
        for h in (2 * i, 2 * i + 1):
            start = h * HEAD_DIM - i * LANES
            masks.append(jnp.where((lane >= start) & (lane < start + HEAD_DIM), 1.0, 0.0))
        yield i, pl.ds(i * LANES, 2 * LANES), masks


def heads(x_refs, outs, *refs):
    w_ref, gather_ref, spread_ref, q_gain_ref, k_gain_ref, q_ref, k_ref, v_ref, wide_ref = refs
    _, branch, share, width = x_refs[0].shape
    x = gather_rows(x_refs)
    rows = x.shape[0]

    def product(part):
        columns = w_ref[:, part * width : (part + 1) * width]
        return jnp.dot(x, columns, preferred_element_type=F32)

    def per_branch(values):
        values = values.reshape(-1, branch, share, width)
        return [values[:, b].reshape(-1, width) for b in range(branch)]

    wide_ref[:rows] = product(0)
    wide_ref[rows:] = product(1)
    factors = head_factors(wide_ref[...], gather_ref[...])
    for b, own in enumerate(per_branch(product(2))):
        v_ref[b] = own.astype(BF16)
    wide_ref[...] *= jnp.dot(factors, spread_ref[...], preferred_element_type=F32)
    for b, own in enumerate(per_branch(wide_ref[:rows])):
        own = own.reshape(-1, outs, share, width)
        for r in range(outs):
            mine = own[:, r].reshape(-1, width)
            for i, columns, masks in pair_masks():
                part = mine[:, i * LANES : (i + 2) * LANES]
                for side, mask in enumerate(masks):
                    gain = mask * q_gain_ref[:, columns]
                    q_ref[r, b, i, side] = (part * gain).astype(BF16)
    for b, own in enumerate(per_branch(wide_ref[rows:])):
        k_ref[b] = (own * k_gain_ref[...]).astype(BF16)


def head_shapes(xs, outs):
    _, branch, share, width = xs[0].shape
    tokens = sum(x.shape[0] for x in xs) * share
    queries = (outs, branch, HEADS // 2, 2, tokens // outs, 2 * LANES)
    return [VMEM(shape, BF16) for shape in (queries, *[(branch, tokens, width)] * 2)]


def wide_shape(xs):
    _, branch, share, width = xs[0].shape
    return VMEM((2 * sum(x.shape[0] for x in xs) * branch * share, width), F32)


def heads_kernel(ins, outs, *refs):
    heads(refs[:ins], outs, *refs[ins:])


def make_heads(xs, tables, outs):
    return pl.pallas_call(
        functools.partial(heads_kernel, len(xs), outs),
        out_shape=head_shapes(xs, outs),
        in_specs=[pl.BlockSpec(memory_space=VMEM)] * (len(xs) + len(tables)),
        out_specs=[pl.BlockSpec(memory_space=VMEM)] * 3,
        scratch_shapes=[wide_shape(xs)],
        compiler_params=params(10),
        name="heads",
    )(*xs, *tables)


def attend_kernel(r, places, share, *refs):
    *in_refs, out_ref, scores_ref, probs_ref = refs
    groups = [in_refs[at : at + 3] for at in range(0, len(in_refs), 3)]
    _, branch, tokens, queries = scores_ref.shape[0], *out_ref.shape[1:2], *scores_ref.shape[1:]
    frames = tokens // share
    width = out_ref.shape[-1]
    same = lax.broadcasted_iota(jnp.int32, (share, queries), 0) == lax.rem(
        lax.broadcasted_iota(jnp.int32, (share, queries), 1), share
    )

    def rows_of(which, b, columns):
        return jnp.concatenate([group[which][b, :, columns] for group in groups], axis=0)

    def queries_of(b, i):
        return jnp.concatenate(
            [group[0][r, b, i, side] for side in range(2) for group in groups], axis=0
        )

    def emit(b, at, block):
        block = block.astype(BF16).reshape(-1, share, LANES)
        if places is None:
            out_ref[:, b, :, pl.ds(at, LANES)] = block
            return
        for slot, place in enumerate(places):
            out_ref[place, b, :, pl.ds(at, LANES)] = block[slot]

    steps = [(i, columns, masks, b) for i, columns, masks in pair_masks() for b in range(branch)]
    carry = [None] * branch

    def score(at):
        i, columns, _, b = steps[at]
        scores_ref[at] = lax.dot_general(
            rows_of(1, b, columns),
            queries_of(b, i),
            (((1,), (1,)), ((), ())),
            preferred_element_type=F32,
        )

    def weigh(at):
        scores = scores_ref[at].reshape(frames, share, queries)
        top = jnp.max(scores, axis=0)
        weights = jnp.exp2((scores - top) * (HEAD_DIM ** (-0.5) * LOG2_E))
        total = jnp.sum(weights, axis=0)
        probs = weights * jnp.where(same, 1.0 / total, 0.0)
        probs_ref[at] = probs.reshape(tokens, queries).astype(BF16)

    def mix(at):
        i, columns, masks, b = steps[at]
        mixed = lax.dot_general(
            probs_ref[at],
            rows_of(2, b, columns),
            (((0,), (0,)), ((), ())),
            preferred_element_type=F32,
        )
        half = queries // 2
        mixed = jnp.where(
            masks[0] > 0.0, mixed[:half], jnp.where(masks[1] > 0.0, mixed[half:], 0.0)
        )
        block = mixed[:, :LANES]
        if carry[b] is not None:
            block = block + carry[b]
        carry[b] = mixed[:, LANES:]
        emit(b, i * LANES, block)

    for at in range(len(steps) + 2):
        if at < len(steps):
            score(at)
        if 0 <= at - 1 < len(steps):
            weigh(at - 1)
        if 0 <= at - 2:
            mix(at - 2)
    for b in range(branch):
        emit(b, width - LANES, carry[b])


def attend(r, groups, places, frames, share, outs):
    branch, _, width = groups[0][1].shape
    tokens = frames * share
    steps, queries = branch * HEADS // 2, 2 * tokens // outs
    flat = [array for group in groups for array in group]
    return pl.pallas_call(
        functools.partial(attend_kernel, r, places, share),
        out_shape=VMEM((frames // outs, branch, share, width), BF16),
        in_specs=[pl.BlockSpec(memory_space=VMEM)] * len(flat),
        out_specs=pl.BlockSpec(memory_space=VMEM),
        scratch_shapes=[
            VMEM((steps, tokens, queries), F32),
            VMEM((steps, tokens, queries), BF16),
        ],
        compiler_params=params(10),
        name="attend",
    )(*flat)


def project_kernel(ins, *refs):
    x_refs, (w_ref, gate_ref, residual_ref, out_ref) = refs[:ins], refs[ins:]
    _, branch, share, _ = x_refs[0].shape
    output = jnp.dot(gather_rows(x_refs), w_ref[...], preferred_element_type=F32)
    gated = (gate_ref[...] * output).reshape(-1, branch, share, output.shape[-1])
    for b in range(branch):
        out_ref[b] = residual_ref[b] + gated[:, b].reshape(out_ref.shape[1:])


def project(xs, w_proj, gate_row, rows):
    branch, patches, width = rows.shape
    cols = 384
    return pl.pallas_call(
        functools.partial(project_kernel, len(xs)),
        out_shape=jax.ShapeDtypeStruct(rows.shape, F32),
        grid=(width // cols,),
        in_specs=[pl.BlockSpec(x.shape, lambda j: (0, 0, 0, 0)) for x in xs]
        + [
            pl.BlockSpec((width, cols), lambda j: (0, j)),
            pl.BlockSpec((1, cols), lambda j: (0, j)),
            pl.BlockSpec((branch, patches, cols), lambda j: (0, 0, j)),
        ],
        out_specs=pl.BlockSpec((branch, patches, cols), lambda j: (0, 0, j)),
        compiler_params=params(12),
        name="project",
    )(*xs, w_proj, gate_row, rows)


def project_part_kernel(places, *refs):
    ins = len(places)
    x_refs, (w_ref, gate_ref, residual_ref) = refs[:ins], refs[ins : ins + 3]
    out_hbm, buffer_ref, sems = refs[-3:]
    _, branch, share, width = x_refs[0].shape
    x = gather_rows(x_refs)
    core = lax.rem(lax.axis_index("seq"), 2)
    cols = width // 3
    copies = []
    for at in range(0, width, cols):
        columns = pl.ds(at, cols)
        output = jnp.dot(x, w_ref[:, columns], preferred_element_type=F32)
        gated = (gate_ref[:, columns] * output).reshape(ins, 2, branch, share, cols)
        for slot, j in enumerate(places):
            start = pl.multiple_of((block_of(j, 0, True) - core) * share, 2 * share)
            for b in range(branch):
                for r in range(2):
                    own = pl.multiple_of(jnp.bitwise_xor(core, r) * share, share)
                    block = pl.ds(pl.multiple_of(start + own, share), share)
                    buffer_ref[slot, b, pl.ds(own, share), columns] = (
                        residual_ref[b, block, columns] + gated[slot, r, b]
                    )
                copies.append(
                    pltpu.make_async_copy(
                        buffer_ref.at[slot, b, :, columns],
                        out_hbm.at[b, pl.ds(start, 2 * share), columns],
                        sems.at[len(copies)],
                    )
                )
                copies[-1].start()
    for copy in copies:
        copy.wait()


def project_part(xs, places, w_proj, gate_row, rows, before):
    branch, _, width = rows.shape
    share = xs[0].shape[2]
    hbm = pl.BlockSpec(memory_space=pltpu.HBM)
    return pl.pallas_call(
        functools.partial(project_part_kernel, places),
        out_shape=pltpu.HBM(rows.shape, F32),
        in_specs=[pl.BlockSpec(memory_space=VMEM)] * (len(xs) + 3) + [hbm] * len(before),
        out_specs=hbm,
        scratch_shapes=[
            VMEM((len(xs), branch, 2 * share, width), F32),
            pltpu.SemaphoreType.DMA((3 * branch * len(xs),)),
        ],
        input_output_aliases={len(xs) + 3: 0} if before else {},
        compiler_params=params(6),
        name="project",
    )(*xs, w_proj, gate_row, rows, *before)


def body(n, exchange, residual, w_qkv, w_proj, q_gain, k_gain, step_mods, timestep):
    rows = residual[:, 0]
    share = rows.shape[1] // n
    if not exchange:
        swap = functools.partial(
            lax.all_to_all, axis_name="seq", split_axis=0, concat_axis=0, tiled=True
        )
        parts, *_, gate_row, _ = modulate(rows, step_mods, timestep, n, exchange)
        tables = w_qkv, *make_tables(q_gain, k_gain, gate_row)
        group = make_heads([swap(parts)], tables, 1)
        attended = swap(attend(0, [group], None, n, share, 1))
        return project([attended], w_proj, gate_row, rows)[:, None]

    places = (0, *send_order(n))
    first, last = places[: n // 4], places[n // 4 :]
    give, scale_row, shift_row, gate_row, held = modulate(rows, step_mods, timestep, n, exchange)
    parts = swap_parts(n, give, lambda: modulate_kept(held, scale_row, shift_row, give))
    tables = w_qkv, *make_tables(q_gain, k_gain, gate_row)
    early = make_heads([parts[j] for j in first], tables, 2)
    groups = early, make_heads([parts[j] for j in last], tables, 2)
    give = attend(1, groups, places, n, share, 2)
    parts = swap_parts(n, give, lambda: attend(0, groups, places, n, share, 2))
    out = []
    for part in (first, last):
        own = [parts[j] for j in part]
        out = [project_part(own, part, w_proj, gate_row, rows, out)]
    return out[0][:, None]


def solution(mesh):
    in_specs = (P("groups", "seq", None, None), P(), P(), P(), P(), P(), P("groups"))
    out_specs = P("groups", "seq", None, None)
    n = mesh.shape["seq"]

    def step(residual, *others):
        share = residual.shape[2] // n
        exchange = 4 <= n <= 32 and n & (n - 1) == 0 and share % 8 == 0
        run = jax.shard_map(
            functools.partial(body, n, exchange),
            mesh=mesh,
            in_specs=in_specs,
            out_specs=out_specs,
            check_vma=False,
        )
        return run(residual, *others)

    return step
```

time: 52.3 us -> 47.7 us (0.912)
  Pallas kernels: 15.6 us -> 11.9 us
  waiting for transfers between devices: 11.6 us -> 10.2 us
  starting transfers between devices: 24.1 us -> 24.7 us
    pallas_call x5 -> x7, Pallas kernels: 12.4 us -> 8.69 us  [the longest x2 4.05 us: make_heads(): pl.pallas_call(functools.partial(heads_kernel, len(xs), outs), out_shape=...]
    ppermute x2, waiting for transfers between devices: 2.78 us -> 1.48 us  [swap_parts(): got = lax.ppermute(give, 'seq', [(s, s ^ 1) for s in range(n)])]
    ppermute x14, starting transfers between devices: 23.5 us -> 24 us  [swap_parts(): parts[j] = lax.ppermute(parts[j], 'seq', [(s, s ^ 2 * j) for s in range(n)])]
  transfers between devices with their start and end apart: 16 -> 16, of which waited for: 6 -> 9; matrix products, arithmetic and copies ran while one was open for 0% -> 0% of each run, Pallas kernels for 15% -> 12%
where the time goes in v2:
time: 47.7 us; the launch traced here: 47.6 us
  starting transfers between devices  24.7 us (52%)
  Pallas kernels  11.9 us (25%)
  waiting for transfers between devices  10.2 us (21%)
  between operations  0.82 us (2%)
    ppermute x14, starting transfers between devices, swap_parts(): parts[j] = lax.ppermute(parts[j], 'seq', [(s, s ^ 2 * j) for s in range(n)])  24 us
    ppermute x14, waiting for transfers between devices, swap_parts(): parts[j] = lax.ppermute(parts[j], 'seq', [(s, s ^ 2 * j) for s in range(n)])  8.72 us
    pallas_call x2, Pallas kernels, make_heads(): pl.pallas_call(functools.partial(heads_kernel, len(xs), outs), out_shape=...  4.05 us
    pallas_call x2, Pallas kernels, project_part(): pl.pallas_call(functools.partial(project_part_kernel, places), out_shape=...  3.08 us
    pallas_call x2, Pallas kernels, attend(): pl.pallas_call(functools.partial(attend_kernel, r, places, share), out_sh...  1.95 us
    pallas_call x1, Pallas kernels, modulate(): pl.pallas_call(functools.partial(modulate_kernel, exchange), out_shape=[V...  1.69 us
    ppermute x2, waiting for transfers between devices, swap_parts(): got = lax.ppermute(give, 'seq', [(s, s ^ 1) for s in range(n)])  1.48 us
  transfers between devices with their start and end apart: 16, of which 9 were waited for; matrix products, arithmetic and copies ran while one was open for 0% of the time, Pallas kernels for 12%

profile of v2, /device:TPU:0, one launch (start us, length us, event | category | flops | bytes accessed | tf_op | source)
XLA Modules:
  0.0 47.6 jit_solution(18205819921761489697)
XLA Ops:
  0.7 1.7 %modulate.1 = (bf16[8,2,8,1152]{3,2,1,0:T(8,128)(2,1)S(1)}, f32[1,1152]{1,0:T(1,128)S(1)}, f32[1,1152]{1,0:T(1,128)S(1)}, f32[1,1152]{1,0:T(1,128)S(1)}, f32[2,128,1152]{2,1,0:T(8,128)S(1)}) custom-call(s32[1]{0:T(128)S(6)} %copy.11.step_ref, f32[2,128,1152]{2,1,0:T(8,128)} %bitcast.7, f32[3,30,1152]{2,1,0:T(8,128)} %bitcast.10), custom_call_target="tpu_custom_call" | custom-call | tf_op jit(solution)/shard_map/modulate/pallas_call | solution.py:77
  3.2 0.9 %collective-permute-done.got_ref = bf16[8,2,8,1152]{3,2,1,0:T(8,128)(2,1)S(1)} collective-permute-done((bf16[8,2,8,1152]{3,2,1,0:T(8,128)(2,1)S(1)}, bf16[8,2,8,1152]{3,2,1,0:T(8,128)(2,1)S(1)}, u32[]{:S(2)}, u32[]{:S(2)}) %collective-permute-start) | collective-permute-done | bytes 294944 | tf_op jit(solution)/shard_map/ppermute | solution.py:174
  4.2 6.0 %collective-permute-start.4 = (bf16[2,2,8,1152]{3,2,1,0:T(8,128)(2,1)S(1)}, bf16[2,2,8,1152]{3,2,1,0:T(8,128)(2,1)S(1)}, u32[]{:S(2)}, u32[]{:S(2)}) collective-permute-start(bf16[2,2,8,1152]{3,2,1,0:T(8,128)(2,1)S(1)} %get-tuple-element.52), channel_id=1, source_target_pairs={{0,14},{1,15},{2,12},{3,13},{4,10},{5,11},{6,8},{7,9},{8,6},{9,7},... | collective-permute-start | bytes 221192 | tf_op jit(solution)/shard_map/ppermute | solution.py:178
  10.8 4.2 %collective-permute-start.1 = (bf16[2,2,8,1152]{3,2,1,0:T(8,128)(2,1)S(1)}, bf16[2,2,8,1152]{3,2,1,0:T(8,128)(2,1)S(1)}, u32[]{:S(2)}, u32[]{:S(2)}) collective-permute-start(bf16[2,2,8,1152]{3,2,1,0:T(8,128)(2,1)S(1)} %get-tuple-element.41), channel_id=1, source_target_pairs={{0,8},{1,9},{2,10},{3,11},{4,12},{5,13},{6,14},{7,15},{8,0},{9,1},... | collective-permute-start | bytes 221192 | tf_op jit(solution)/shard_map/ppermute | solution.py:178
  15.0 2.9 %collective-permute-start.2 = (bf16[2,2,8,1152]{3,2,1,0:T(8,128)(2,1)S(1)}, bf16[2,2,8,1152]{3,2,1,0:T(8,128)(2,1)S(1)}, u32[]{:S(2)}, u32[]{:S(2)}) collective-permute-start(bf16[2,2,8,1152]{3,2,1,0:T(8,128)(2,1)S(1)} %get-tuple-element.42), channel_id=1, source_target_pairs={{0,10},{1,11},{2,8},{3,9},{4,14},{5,15},{6,12},{7,13},{8,2},{9,3},... | collective-permute-start | bytes 221192 | tf_op jit(solution)/shard_map/ppermute | solution.py:178
  17.9 0.8 %collective-permute-start.3 = (bf16[2,2,8,1152]{3,2,1,0:T(8,128)(2,1)S(1)}, bf16[2,2,8,1152]{3,2,1,0:T(8,128)(2,1)S(1)}, u32[]{:S(2)}, u32[]{:S(2)}) collective-permute-start(bf16[2,2,8,1152]{3,2,1,0:T(8,128)(2,1)S(1)} %get-tuple-element.43), channel_id=1, source_target_pairs={{0,6},{1,7},{2,4},{3,5},{4,2},{5,3},{6,0},{7,1},{8,14},{9,15},{10,... | collective-permute-start | bytes 221192 | tf_op jit(solution)/shard_map/ppermute | solution.py:178
  18.8 0.7 %tables.1 = (bf16[1152,128]{1,0:T(8,128)(2,1)S(1)}, bf16[128,1152]{1,0:T(8,128)(2,1)S(1)}, f32[1,1152]{1,0:T(1,128)S(1)}, f32[1,1152]{1,0:T(1,128)S(1)}) custom-call(f32[1,1152]{1,0:T(1,128)S(1)} %get-tuple-element.44.after_ref.refs_5_, f32[1152]{0:T(1024)} %q_gain_hbm.1, f32[1152]{0:T(1024)} %k_gain_hbm.1), custom_call_target="tpu_custom_call" | custom-call | tf_op jit(solution)/shard_map/tables/pallas_call | solution.py:133
  19.5 2.0 %heads.3 = (bf16[2,2,8,2,32,256]{5,4,3,2,1,0:T(8,128)(2,1)S(1)}, bf16[2,64,1152]{2,1,0:T(8,128)(2,1)S(1)}, bf16[2,64,1152]{2,1,0:T(8,128)(2,1)S(1)}) custom-call(bf16[2,2,8,1152]{3,2,1,0:T(8,128)(2,1)S(1)} %collective-permute-done.4.refs_0_, bf16[2,2,8,1152]{3,2,1,0:T(8,128)(2,1)S(1)} %collective-permute-done.5.refs_1_, ...), custom_call_target="tpu_custom_call" | custom-call | tf_op jit(solution)/shard_map/heads/pallas_call | solution.py:270
  22.0 1.0 %collective-permute-done.2.refs_2_ = bf16[2,2,8,1152]{3,2,1,0:T(8,128)(2,1)S(1)} collective-permute-done((bf16[2,2,8,1152]{3,2,1,0:T(8,128)(2,1)S(1)}, bf16[2,2,8,1152]{3,2,1,0:T(8,128)(2,1)S(1)}, u32[]{:S(2)}, u32[]{:S(2)}) %collective-permute-start.2) | collective-permute-done | bytes 73760 | tf_op jit(solution)/shard_map/ppermute | solution.py:178
  23.0 0.7 %collective-permute-done.3.refs_3_ = bf16[2,2,8,1152]{3,2,1,0:T(8,128)(2,1)S(1)} collective-permute-done((bf16[2,2,8,1152]{3,2,1,0:T(8,128)(2,1)S(1)}, bf16[2,2,8,1152]{3,2,1,0:T(8,128)(2,1)S(1)}, u32[]{:S(2)}, u32[]{:S(2)}) %collective-permute-start.3) | collective-permute-done | bytes 73760 | tf_op jit(solution)/shard_map/ppermute | solution.py:178
  23.7 2.0 %heads.2 = (bf16[2,2,8,2,32,256]{5,4,3,2,1,0:T(8,128)(2,1)S(1)}, bf16[2,64,1152]{2,1,0:T(8,128)(2,1)S(1)}, bf16[2,64,1152]{2,1,0:T(8,128)(2,1)S(1)}) custom-call(bf16[2,2,8,1152]{3,2,1,0:T(8,128)(2,1)S(1)} %get-tuple-element.40.refs_0_, bf16[2,2,8,1152]{3,2,1,0:T(8,128)(2,1)S(1)} %collective-permute-done.1.refs_1_, ...), custom_call_target="tpu_custom_call" | custom-call | tf_op jit(solution)/shard_map/heads/pallas_call | solution.py:270
  25.7 1.0 %attend.3 = bf16[8,2,8,1152]{3,2,1,0:T(8,128)(2,1)S(1)} custom-call(bf16[2,2,8,2,32,256]{5,4,3,2,1,0:T(8,128)(2,1)S(1)} %get-tuple-element.49.refs_0_, bf16[2,64,1152]{2,1,0:T(8,128)(2,1)S(1)} %get-tuple-element.50.refs_1_, bf16[2,64,1152]{2,1,0:T(8,128)(2,1)S(1)} %get-tuple-element.51.refs_2_, ...), custom_call_target="tpu_custom_call" | custom-call | tf_op jit(solution)/shard_map/attend/pallas_call | solution.py:361
  26.8 1.0 %attend.2.keep_ref = bf16[8,2,8,1152]{3,2,1,0:T(8,128)(2,1)S(1)} custom-call(bf16[2,2,8,2,32,256]{5,4,3,2,1,0:T(8,128)(2,1)S(1)} %get-tuple-element.49.refs_0_, bf16[2,64,1152]{2,1,0:T(8,128)(2,1)S(1)} %get-tuple-element.50.refs_1_, bf16[2,64,1152]{2,1,0:T(8,128)(2,1)S(1)} %get-tuple-element.51.refs_2_, ...), custom_call_target="tpu_custom_call" | custom-call | tf_op jit(solution)/shard_map/attend/pallas_call | solution.py:361
  28.4 3.0 %collective-permute-start.13 = (bf16[2,2,8,1152]{3,2,1,0:T(8,128)(2,1)S(1)}, bf16[2,2,8,1152]{3,2,1,0:T(8,128)(2,1)S(1)}, u32[]{:S(2)}, u32[]{:S(2)}) collective-permute-start(bf16[2,2,8,1152]{3,2,1,0:T(8,128)(2,1)S(1)} %get-tuple-element.64), channel_id=1, source_target_pairs={{0,8},{1,9},{2,10},{3,11},{4,12},{5,13},{6,14},{7,15},{8,0},{9,1},... | collective-permute-start | bytes 221192 | tf_op jit(solution)/shard_map/ppermute | solution.py:178
  31.4 0.8 %collective-permute-start.14 = (bf16[2,2,8,1152]{3,2,1,0:T(8,128)(2,1)S(1)}, bf16[2,2,8,1152]{3,2,1,0:T(8,128)(2,1)S(1)}, u32[]{:S(2)}, u32[]{:S(2)}) collective-permute-start(bf16[2,2,8,1152]{3,2,1,0:T(8,128)(2,1)S(1)} %get-tuple-element.65), channel_id=1, source_target_pairs={{0,10},{1,11},{2,8},{3,9},{4,14},{5,15},{6,12},{7,13},{8,2},{9,3},... | collective-permute-start | bytes 221192 | tf_op jit(solution)/shard_map/ppermute | solution.py:178
  32.2 1.8 %collective-permute-start.9 = (bf16[2,2,8,1152]{3,2,1,0:T(8,128)(2,1)S(1)}, bf16[2,2,8,1152]{3,2,1,0:T(8,128)(2,1)S(1)}, u32[]{:S(2)}, u32[]{:S(2)}) collective-permute-start(bf16[2,2,8,1152]{3,2,1,0:T(8,128)(2,1)S(1)} %get-tuple-element.59), channel_id=1, source_target_pairs={{0,14},{1,15},{2,12},{3,13},{4,10},{5,11},{6,8},{7,9},{8,6},{9,7},... | collective-permute-start | bytes 221192 | tf_op jit(solution)/shard_map/ppermute | solution.py:178
  34.0 0.7 %collective-permute-start.15 = (bf16[2,2,8,1152]{3,2,1,0:T(8,128)(2,1)S(1)}, bf16[2,2,8,1152]{3,2,1,0:T(8,128)(2,1)S(1)}, u32[]{:S(2)}, u32[]{:S(2)}) collective-permute-start(bf16[2,2,8,1152]{3,2,1,0:T(8,128)(2,1)S(1)} %get-tuple-element.66), channel_id=1, source_target_pairs={{0,6},{1,7},{2,4},{3,5},{4,2},{5,3},{6,0},{7,1},{8,14},{9,15},{10,... | collective-permute-start | bytes 221192 | tf_op jit(solution)/shard_map/ppermute | solution.py:178
  34.7 2.0 %collective-permute-start.10 = (bf16[2,2,8,1152]{3,2,1,0:T(8,128)(2,1)S(1)}, bf16[2,2,8,1152]{3,2,1,0:T(8,128)(2,1)S(1)}, u32[]{:S(2)}, u32[]{:S(2)}) collective-permute-start(bf16[2,2,8,1152]{3,2,1,0:T(8,128)(2,1)S(1)} %get-tuple-element.60), channel_id=1, source_target_pairs={{0,12},{1,13},{2,14},{3,15},{4,8},{5,9},{6,10},{7,11},{8,4},{9,5},... | collective-permute-start | bytes 221192 | tf_op jit(solution)/shard_map/ppermute | solution.py:178
  36.7 1.5 %collective-permute-done.13.refs_1_ = bf16[2,2,8,1152]{3,2,1,0:T(8,128)(2,1)S(1)} collective-permute-done((bf16[2,2,8,1152]{3,2,1,0:T(8,128)(2,1)S(1)}, bf16[2,2,8,1152]{3,2,1,0:T(8,128)(2,1)S(1)}, u32[]{:S(2)}, u32[]{:S(2)}) %collective-permute-start.13) | collective-permute-done | bytes 73760 | tf_op jit(solution)/shard_map/ppermute | solution.py:178
  38.2 3.5 %collective-permute-done.14.refs_2_ = bf16[2,2,8,1152]{3,2,1,0:T(8,128)(2,1)S(1)} collective-permute-done((bf16[2,2,8,1152]{3,2,1,0:T(8,128)(2,1)S(1)}, bf16[2,2,8,1152]{3,2,1,0:T(8,128)(2,1)S(1)}, u32[]{:S(2)}, u32[]{:S(2)}) %collective-permute-start.14) | collective-permute-done | bytes 73760 | tf_op jit(solution)/shard_map/ppermute | solution.py:178
  41.7 1.2 %collective-permute-start.12 = (bf16[2,2,8,1152]{3,2,1,0:T(8,128)(2,1)S(1)}, bf16[2,2,8,1152]{3,2,1,0:T(8,128)(2,1)S(1)}, u32[]{:S(2)}, u32[]{:S(2)}) collective-permute-start(bf16[2,2,8,1152]{3,2,1,0:T(8,128)(2,1)S(1)} %get-tuple-element.62), channel_id=1, source_target_pairs={{0,2},{1,3},{2,0},{3,1},{4,6},{5,7},{6,4},{7,5},{8,10},{9,11},{10,... | collective-permute-start | bytes 221192 | tf_op jit(solution)/shard_map/ppermute | solution.py:178
  42.8 1.2 %collective-permute-done.15.refs_3_ = bf16[2,2,8,1152]{3,2,1,0:T(8,128)(2,1)S(1)} collective-permute-done((bf16[2,2,8,1152]{3,2,1,0:T(8,128)(2,1)S(1)}, bf16[2,2,8,1152]{3,2,1,0:T(8,128)(2,1)S(1)}, u32[]{:S(2)}, u32[]{:S(2)}) %collective-permute-start.15) | collective-permute-done | bytes 73760 | tf_op jit(solution)/shard_map/ppermute | solution.py:178
  44.0 1.5 %project.2.refs_7_ = f32[2,128,1152]{2,1,0:T(8,128)} custom-call(bf16[2,2,8,1152]{3,2,1,0:T(8,128)(2,1)S(1)} %get-tuple-element.63.refs_0_, bf16[2,2,8,1152]{3,2,1,0:T(8,128)(2,1)S(1)} %collective-permute-done.13.refs_1_, bf16[2,2,8,1152]{3,2,1,0:T(8,128)(2,1)S(1)} %collective-permute-done.14.refs_2_, ...), custom_call_target="tpu_custom_call" | custom-call | tf_op jit(solution)/shard_map/project/pallas_call | solution.py:441
  46.0 1.5 %project.3 = f32[2,128,1152]{2,1,0:T(8,128)} custom-call(bf16[2,2,8,1152]{3,2,1,0:T(8,128)(2,1)S(1)} %collective-permute-done.9.refs_0_, bf16[2,2,8,1152]{3,2,1,0:T(8,128)(2,1)S(1)} %collective-permute-done.10.refs_1_, bf16[2,2,8,1152]{3,2,1,0:T(8,128)(2,1)S(1)} %collective-permute-done.11.refs_2_, ...), custom_call_target="tpu_custom_call", output_to_operand_aliasing={{}: (7, {})} | custom-call | tf_op jit(solution)/shard_map/project/pallas_call | solution.py:441
  (28 shorter events, 3.1 us)
Async XLA Ops:
  2.3 1.8 %collective-permute-start = (bf16[8,2,8,1152]{3,2,1,0:T(8,128)(2,1)S(1)}, bf16[8,2,8,1152]{3,2,1,0:T(8,128)(2,1)S(1)}, u32[]{:S(2)}, u32[]{:S(2)}) collective-permute-start(bf16[8,2,8,1152]{3,2,1,0:T(8,128)(2,1)S(1)} %get-tuple-element.39), channel_id=1, source_target_pairs={{0,1},{1,0},{2,3},{3,2},{4,5},{5,4},{6,7},{7,6},{8,9},{9,8},{10,11... | collective-permute-start | bytes 884744 | tf_op jit(solution)/shard_map/ppermute | solution.py:174
  2.9 16.6 %slice-start = ((s8[7962624]{0:T(1024)(128)(4,1)}), s8[4194304]{0:T(1024)(128)(4,1)S(1)}, s32[]{:S(2)}) async-start(s8[7962624]{0:T(1024)(128)(4,1)} %bitcast.5), calls=%async_computation | async-start | bytes 8388608
  3.2 16.3 %slice-start.1 = ((s8[7962624]{0:T(1024)(128)(4,1)}), s8[3768320]{0:T(1024)(128)(4,1)S(1)}, s32[]{:S(2)}) async-start(s8[7962624]{0:T(1024)(128)(4,1)} %bitcast.5), calls=%async_computation.1 | async-start | bytes 7536640
  4.2 10.9 %collective-permute-start.4 = (bf16[2,2,8,1152]{3,2,1,0:T(8,128)(2,1)S(1)}, bf16[2,2,8,1152]{3,2,1,0:T(8,128)(2,1)S(1)}, u32[]{:S(2)}, u32[]{:S(2)}) collective-permute-start(bf16[2,2,8,1152]{3,2,1,0:T(8,128)(2,1)S(1)} %get-tuple-element.52), channel_id=1, source_target_pairs={{0,14},{1,15},{2,12},{3,13},{4,10},{5,11},{6,8},{7,9},{8,6},{9,7},... | collective-permute-start | bytes 221192 | tf_op jit(solution)/shard_map/ppermute | solution.py:178
  10.1 7.8 %collective-permute-start.5 = (bf16[2,2,8,1152]{3,2,1,0:T(8,128)(2,1)S(1)}, bf16[2,2,8,1152]{3,2,1,0:T(8,128)(2,1)S(1)}, u32[]{:S(2)}, u32[]{:S(2)}) collective-permute-start(bf16[2,2,8,1152]{3,2,1,0:T(8,128)(2,1)S(1)} %get-tuple-element.53), channel_id=1, source_target_pairs={{0,12},{1,13},{2,14},{3,15},{4,8},{5,9},{6,10},{7,11},{8,4},{9,5},... | collective-permute-start | bytes 221192 | tf_op jit(solution)/shard_map/ppermute | solution.py:178
  10.4 9.1 %collective-permute-start.6 = (bf16[2,2,8,1152]{3,2,1,0:T(8,128)(2,1)S(1)}, bf16[2,2,8,1152]{3,2,1,0:T(8,128)(2,1)S(1)}, u32[]{:S(2)}, u32[]{:S(2)}) collective-permute-start(bf16[2,2,8,1152]{3,2,1,0:T(8,128)(2,1)S(1)} %get-tuple-element.54), channel_id=1, source_target_pairs={{0,4},{1,5},{2,6},{3,7},{4,0},{5,1},{6,2},{7,3},{8,12},{9,13},{10,... | collective-permute-start | bytes 221192 | tf_op jit(solution)/shard_map/ppermute | solution.py:178
  10.4 9.1 %collective-permute-start.7 = (bf16[2,2,8,1152]{3,2,1,0:T(8,128)(2,1)S(1)}, bf16[2,2,8,1152]{3,2,1,0:T(8,128)(2,1)S(1)}, u32[]{:S(2)}, u32[]{:S(2)}) collective-permute-start(bf16[2,2,8,1152]{3,2,1,0:T(8,128)(2,1)S(1)} %get-tuple-element.55), channel_id=1, source_target_pairs={{0,2},{1,3},{2,0},{3,1},{4,6},{5,7},{6,4},{7,5},{8,10},{9,11},{10,... | collective-permute-start | bytes 221192 | tf_op jit(solution)/shard_map/ppermute | solution.py:178
  10.8 11.2 %collective-permute-start.1 = (bf16[2,2,8,1152]{3,2,1,0:T(8,128)(2,1)S(1)}, bf16[2,2,8,1152]{3,2,1,0:T(8,128)(2,1)S(1)}, u32[]{:S(2)}, u32[]{:S(2)}) collective-permute-start(bf16[2,2,8,1152]{3,2,1,0:T(8,128)(2,1)S(1)} %get-tuple-element.41), channel_id=1, source_target_pairs={{0,8},{1,9},{2,10},{3,11},{4,12},{5,13},{6,14},{7,15},{8,0},{9,1},... | collective-permute-start | bytes 221192 | tf_op jit(solution)/shard_map/ppermute | solution.py:178
  15.0 7.9 %collective-permute-start.2 = (bf16[2,2,8,1152]{3,2,1,0:T(8,128)(2,1)S(1)}, bf16[2,2,8,1152]{3,2,1,0:T(8,128)(2,1)S(1)}, u32[]{:S(2)}, u32[]{:S(2)}) collective-permute-start(bf16[2,2,8,1152]{3,2,1,0:T(8,128)(2,1)S(1)} %get-tuple-element.42), channel_id=1, source_target_pairs={{0,10},{1,11},{2,8},{3,9},{4,14},{5,15},{6,12},{7,13},{8,2},{9,3},... | collective-permute-start | bytes 221192 | tf_op jit(solution)/shard_map/ppermute | solution.py:178
  17.9 5.8 %collective-permute-start.3 = (bf16[2,2,8,1152]{3,2,1,0:T(8,128)(2,1)S(1)}, bf16[2,2,8,1152]{3,2,1,0:T(8,128)(2,1)S(1)}, u32[]{:S(2)}, u32[]{:S(2)}) collective-permute-start(bf16[2,2,8,1152]{3,2,1,0:T(8,128)(2,1)S(1)} %get-tuple-element.43), channel_id=1, source_target_pairs={{0,6},{1,7},{2,4},{3,5},{4,2},{5,3},{6,0},{7,1},{8,14},{9,15},{10,... | collective-permute-start | bytes 221192 | tf_op jit(solution)/shard_map/ppermute | solution.py:178
  26.7 1.6 %collective-permute-start.8 = (bf16[8,2,8,1152]{3,2,1,0:T(8,128)(2,1)S(1)}, bf16[8,2,8,1152]{3,2,1,0:T(8,128)(2,1)S(1)}, u32[]{:S(2)}, u32[]{:S(2)}) collective-permute-start(bf16[8,2,8,1152]{3,2,1,0:T(8,128)(2,1)S(1)} %attend.3), channel_id=1, source_target_pairs={{0,1},{1,0},{2,3},{3,2},{4,5},{5,4},{6,7},{7,6},{8,9},{9,8},{10,11... | collective-permute-start | bytes 884744 | tf_op jit(solution)/shard_map/ppermute | solution.py:174
  27.8 16.2 %copy-start.1 = (f32[2,1,128,1152]{3,2,1,0:T(8,128)S(1)}, f32[2,1,128,1152]{3,2,1,0:T(8,128)}, u32[]{:S(2)}) copy-start(f32[2,1,128,1152]{3,2,1,0:T(8,128)} %param.7) | copy-start | bytes 3538948
  28.4 15.7 %copy-start = (bf16[1152,1152]{1,0:T(8,128)(2,1)S(1)}, bf16[1152,1152]{1,0:T(8,128)(2,1)}, u32[]{:S(2)}) copy-start(bf16[1152,1152]{1,0:T(8,128)(2,1)} %refs_4_.7) | copy-start | bytes 7962628
  28.4 9.8 %collective-permute-start.13 = (bf16[2,2,8,1152]{3,2,1,0:T(8,128)(2,1)S(1)}, bf16[2,2,8,1152]{3,2,1,0:T(8,128)(2,1)S(1)}, u32[]{:S(2)}, u32[]{:S(2)}) collective-permute-start(bf16[2,2,8,1152]{3,2,1,0:T(8,128)(2,1)S(1)} %get-tuple-element.64), channel_id=1, source_target_pairs={{0,8},{1,9},{2,10},{3,11},{4,12},{5,13},{6,14},{7,15},{8,0},{9,1},... | collective-permute-start | bytes 221192 | tf_op jit(solution)/shard_map/ppermute | solution.py:178
  31.4 10.3 %collective-permute-start.14 = (bf16[2,2,8,1152]{3,2,1,0:T(8,128)(2,1)S(1)}, bf16[2,2,8,1152]{3,2,1,0:T(8,128)(2,1)S(1)}, u32[]{:S(2)}, u32[]{:S(2)}) collective-permute-start(bf16[2,2,8,1152]{3,2,1,0:T(8,128)(2,1)S(1)} %get-tuple-element.65), channel_id=1, source_target_pairs={{0,10},{1,11},{2,8},{3,9},{4,14},{5,15},{6,12},{7,13},{8,2},{9,3},... | collective-permute-start | bytes 221192 | tf_op jit(solution)/shard_map/ppermute | solution.py:178
  32.2 13.4 %collective-permute-start.9 = (bf16[2,2,8,1152]{3,2,1,0:T(8,128)(2,1)S(1)}, bf16[2,2,8,1152]{3,2,1,0:T(8,128)(2,1)S(1)}, u32[]{:S(2)}, u32[]{:S(2)}) collective-permute-start(bf16[2,2,8,1152]{3,2,1,0:T(8,128)(2,1)S(1)} %get-tuple-element.59), channel_id=1, source_target_pairs={{0,14},{1,15},{2,12},{3,13},{4,10},{5,11},{6,8},{7,9},{8,6},{9,7},... | collective-permute-start | bytes 221192 | tf_op jit(solution)/shard_map/ppermute | solution.py:178
  34.0 10.0 %collective-permute-start.15 = (bf16[2,2,8,1152]{3,2,1,0:T(8,128)(2,1)S(1)}, bf16[2,2,8,1152]{3,2,1,0:T(8,128)(2,1)S(1)}, u32[]{:S(2)}, u32[]{:S(2)}) collective-permute-start(bf16[2,2,8,1152]{3,2,1,0:T(8,128)(2,1)S(1)} %get-tuple-element.66), channel_id=1, source_target_pairs={{0,6},{1,7},{2,4},{3,5},{4,2},{5,3},{6,0},{7,1},{8,14},{9,15},{10,... | collective-permute-start | bytes 221192 | tf_op jit(solution)/shard_map/ppermute | solution.py:178
  34.7 10.9 %collective-permute-start.10 = (bf16[2,2,8,1152]{3,2,1,0:T(8,128)(2,1)S(1)}, bf16[2,2,8,1152]{3,2,1,0:T(8,128)(2,1)S(1)}, u32[]{:S(2)}, u32[]{:S(2)}) collective-permute-start(bf16[2,2,8,1152]{3,2,1,0:T(8,128)(2,1)S(1)} %get-tuple-element.60), channel_id=1, source_target_pairs={{0,12},{1,13},{2,14},{3,15},{4,8},{5,9},{6,10},{7,11},{8,4},{9,5},... | collective-permute-start | bytes 221192 | tf_op jit(solution)/shard_map/ppermute | solution.py:178
  38.2 7.4 %collective-permute-start.11 = (bf16[2,2,8,1152]{3,2,1,0:T(8,128)(2,1)S(1)}, bf16[2,2,8,1152]{3,2,1,0:T(8,128)(2,1)S(1)}, u32[]{:S(2)}, u32[]{:S(2)}) collective-permute-start(bf16[2,2,8,1152]{3,2,1,0:T(8,128)(2,1)S(1)} %get-tuple-element.61), channel_id=1, source_target_pairs={{0,4},{1,5},{2,6},{3,7},{4,0},{5,1},{6,2},{7,3},{8,12},{9,13},{10,... | collective-permute-start | bytes 221192 | tf_op jit(solution)/shard_map/ppermute | solution.py:178
  41.7 4.4 %collective-permute-start.12 = (bf16[2,2,8,1152]{3,2,1,0:T(8,128)(2,1)S(1)}, bf16[2,2,8,1152]{3,2,1,0:T(8,128)(2,1)S(1)}, u32[]{:S(2)}, u32[]{:S(2)}) collective-permute-start(bf16[2,2,8,1152]{3,2,1,0:T(8,128)(2,1)S(1)} %get-tuple-element.62), channel_id=1, source_target_pairs={{0,2},{1,3},{2,0},{3,1},{4,6},{5,7},{6,4},{7,5},{8,10},{9,11},{10,... | collective-permute-start | bytes 221192 | tf_op jit(solution)/shard_map/ppermute | solution.py:178

commit v3 on v2

--- a/solution.py
+++ b/solution.py
@@ -95,17 +95,18 @@
     )(timestep, in_hbm(rows), in_hbm(jnp.swapaxes(step_mods, 0, 1)))
 
 
-def keep_kernel(rows_ref, scale_ref, shift_ref, out_ref):
+def keep_kernel(lead, rows_ref, scale_ref, shift_ref, out_ref, lead_ref):
     branches = range(rows_ref.shape[0])
     modulate_rows(rows_ref, scale_ref[...], shift_ref[...], out_ref, 0, True, branches)
-
-
-def modulate_kept(rows, scale_row, shift_row, like):
-    return pl.pallas_call(
-        keep_kernel,
-        out_shape=VMEM(like.shape, BF16),
+    lead_ref[0] = out_ref[lead]
+
+
+def modulate_kept(rows, scale_row, shift_row, like, lead):
+    return pl.pallas_call(
+        functools.partial(keep_kernel, lead),
+        out_shape=[VMEM(like.shape, BF16), VMEM((1, *like.shape[1:]), BF16)],
         in_specs=[pl.BlockSpec(memory_space=VMEM)] * 3,
-        out_specs=pl.BlockSpec(memory_space=VMEM),
+        out_specs=[pl.BlockSpec(memory_space=VMEM)] * 2,
         compiler_params=params(4),
         name="keep",
     )(rows, scale_row, shift_row)
@@ -146,17 +147,20 @@
     )(after, in_hbm(q_gain), in_hbm(k_gain))
 
 
-def pack_kernel(keep_ref, got_ref, *out_refs):
+def pack_kernel(lead, keep_ref, got_ref, *out_refs):
     for j, out_ref in enumerate(out_refs):
-        out_ref[0] = keep_ref[j]
-        out_ref[1] = got_ref[j]
-
-
-def pack(keep, got):
+        if j == lead:
+            out_ref[0] = got_ref[j]
+        else:
+            out_ref[0] = keep_ref[j]
+            out_ref[1] = got_ref[j]
+
+
+def pack(keep, got, lead):
     count, *part = keep.shape
     return pl.pallas_call(
-        pack_kernel,
-        out_shape=[VMEM((2, *part), keep.dtype)] * count,
+        functools.partial(pack_kernel, lead),
+        out_shape=[VMEM((1 if j == lead else 2, *part), keep.dtype) for j in range(count)],
         in_specs=[pl.BlockSpec(memory_space=VMEM)] * 2,
         out_specs=[pl.BlockSpec(memory_space=VMEM)] * count,
         compiler_params=params(1),
@@ -171,11 +175,17 @@
 
 
 def swap_parts(n, give, make_keep):
+    def send(j, part):
+        return lax.ppermute(part, "seq", [(s, s ^ (2 * j)) for s in range(n)])
+
+    order = send_order(n)
     got = lax.ppermute(give, "seq", [(s, s ^ 1) for s in range(n)])
-    keep = make_keep()
-    parts = list(pack(keep, got))
-    for j in send_order(n):
-        parts[j] = lax.ppermute(parts[j], "seq", [(s, s ^ (2 * j)) for s in range(n)])
+    keep, first = make_keep()
+    first = send(order[0], first)
+    parts = [[part] for part in pack(keep, got, order[0])]
+    for j in order:
+        parts[j] = [send(j, parts[j][0])]
+    parts[order[0]].insert(0, first)
     return parts
 
 
@@ -278,8 +288,10 @@
     )(*xs, *tables)
 
 
-def attend_kernel(r, places, share, *refs):
-    *in_refs, out_ref, scores_ref, probs_ref = refs
+def attend_kernel(r, places, share, lead, *refs):
+    *in_refs, scores_ref, probs_ref = refs
+    lead_ref = None if lead is None else in_refs.pop()
+    out_ref = in_refs.pop()
     groups = [in_refs[at : at + 3] for at in range(0, len(in_refs), 3)]
     _, branch, tokens, queries = scores_ref.shape[0], *out_ref.shape[1:2], *scores_ref.shape[1:]
     frames = tokens // share
@@ -303,6 +315,8 @@
             return
         for slot, place in enumerate(places):
             out_ref[place, b, :, pl.ds(at, LANES)] = block[slot]
+            if place == lead:
+                lead_ref[0, b, :, pl.ds(at, LANES)] = block[slot]
 
     steps = [(i, columns, masks, b) for i, columns, masks in pair_masks() for b in range(branch)]
     carry = [None] * branch
@@ -353,16 +367,19 @@
         emit(b, width - LANES, carry[b])
 
 
-def attend(r, groups, places, frames, share, outs):
+def attend(r, groups, places, frames, share, outs, lead=None):
     branch, _, width = groups[0][1].shape
     tokens = frames * share
     steps, queries = branch * HEADS // 2, 2 * tokens // outs
     flat = [array for group in groups for array in group]
-    return pl.pallas_call(
-        functools.partial(attend_kernel, r, places, share),
-        out_shape=VMEM((frames // outs, branch, share, width), BF16),
+    shapes = [VMEM((frames // outs, branch, share, width), BF16)]
+    if lead is not None:
+        shapes.append(VMEM((1, branch, share, width), BF16))
+    return pl.pallas_call(
+        functools.partial(attend_kernel, r, places, share, lead),
+        out_shape=shapes,
         in_specs=[pl.BlockSpec(memory_space=VMEM)] * len(flat),
-        out_specs=pl.BlockSpec(memory_space=VMEM),
+        out_specs=[pl.BlockSpec(memory_space=VMEM)] * len(shapes),
         scratch_shapes=[
             VMEM((steps, tokens, queries), F32),
             VMEM((steps, tokens, queries), BF16),
@@ -400,8 +417,7 @@
     )(*xs, w_proj, gate_row, rows)
 
 
-def project_part_kernel(places, *refs):
-    ins = len(places)
+def project_part_kernel(places, ins, *refs):
     x_refs, (w_ref, gate_ref, residual_ref) = refs[:ins], refs[ins : ins + 3]
     out_hbm, buffer_ref, sems = refs[-3:]
     _, branch, share, width = x_refs[0].shape
@@ -412,7 +428,7 @@
     for at in range(0, width, cols):
         columns = pl.ds(at, cols)
         output = jnp.dot(x, w_ref[:, columns], preferred_element_type=F32)
-        gated = (gate_ref[:, columns] * output).reshape(ins, 2, branch, share, cols)
+        gated = (gate_ref[:, columns] * output).reshape(-1, 2, branch, share, cols)
         for slot, j in enumerate(places):
             start = pl.multiple_of((block_of(j, 0, True) - core) * share, 2 * share)
             for b in range(branch):
@@ -439,13 +455,13 @@
     share = xs[0].shape[2]
     hbm = pl.BlockSpec(memory_space=pltpu.HBM)
     return pl.pallas_call(
-        functools.partial(project_part_kernel, places),
+        functools.partial(project_part_kernel, places, len(xs)),
         out_shape=pltpu.HBM(rows.shape, F32),
         in_specs=[pl.BlockSpec(memory_space=VMEM)] * (len(xs) + 3) + [hbm] * len(before),
         out_specs=hbm,
         scratch_shapes=[
-            VMEM((len(xs), branch, 2 * share, width), F32),
-            pltpu.SemaphoreType.DMA((3 * branch * len(xs),)),
+            VMEM((len(places), branch, 2 * share, width), F32),
+            pltpu.SemaphoreType.DMA((3 * branch * len(places),)),
         ],
         input_output_aliases={len(xs) + 3: 0} if before else {},
         compiler_params=params(6),
@@ -463,22 +479,25 @@
         parts, *_, gate_row, _ = modulate(rows, step_mods, timestep, n, exchange)
         tables = w_qkv, *make_tables(q_gain, k_gain, gate_row)
         group = make_heads([swap(parts)], tables, 1)
-        attended = swap(attend(0, [group], None, n, share, 1))
+        attended = swap(attend(0, [group], None, n, share, 1)[0])
         return project([attended], w_proj, gate_row, rows)[:, None]
 
     places = (0, *send_order(n))
     first, last = places[: n // 4], places[n // 4 :]
+    lead = places[1]
     give, scale_row, shift_row, gate_row, held = modulate(rows, step_mods, timestep, n, exchange)
-    parts = swap_parts(n, give, lambda: modulate_kept(held, scale_row, shift_row, give))
+    parts = swap_parts(
+        n, give, lambda: modulate_kept(held, scale_row, shift_row, give, lead)
+    )
     tables = w_qkv, *make_tables(q_gain, k_gain, gate_row)
-    early = make_heads([parts[j] for j in first], tables, 2)
-    groups = early, make_heads([parts[j] for j in last], tables, 2)
-    give = attend(1, groups, places, n, share, 2)
-    parts = swap_parts(n, give, lambda: attend(0, groups, places, n, share, 2))
+    early = make_heads([part for j in first for part in parts[j]], tables, 2)
+    groups = early, make_heads([part for j in last for part in parts[j]], tables, 2)
+    (give,) = attend(1, groups, places, n, share, 2)
+    parts = swap_parts(n, give, lambda: attend(0, groups, places, n, share, 2, lead))
     out = []
-    for part in (first, last):
-        own = [parts[j] for j in part]
-        out = [project_part(own, part, w_proj, gate_row, rows, out)]
+    for chips in (first, last):
+        own = [part for j in chips for part in parts[j]]
+        out = [project_part(own, chips, w_proj, gate_row, rows, out)]
     return out[0][:, None]
 
 
@@ -489,7 +508,7 @@
 
     def step(residual, *others):
         share = residual.shape[2] // n
-        exchange = 4 <= n <= 32 and n & (n - 1) == 0 and share % 8 == 0
+        exchange = 8 <= n <= 32 and n & (n - 1) == 0 and share % 8 == 0
         run = jax.shard_map(
             functools.partial(body, n, exchange),
             mesh=mesh,

time: 47.7 us -> 48.1 us (level)
  starting transfers between devices: 24.7 us -> 27.2 us
  waiting for transfers between devices: 10.2 us -> 8.04 us
    ppermute x14 -> x16, starting transfers between devices: 24 us -> 26.5 us  [send(): return lax.ppermute(part, 'seq', [(s, s ^ 2 * j) for s in range(n)])]
    ppermute x14 -> x16, waiting for transfers between devices: 8.72 us -> 6.53 us  [send(): return lax.ppermute(part, 'seq', [(s, s ^ 2 * j) for s in range(n)])]
  transfers between devices with their start and end apart: 16 -> 18, of which waited for: 9 -> 7; matrix products, arithmetic and copies ran while one was open for 0% -> 0% of each run, Pallas kernels for 12% -> 12%
where the time goes in v3:
time: 48.1 us; the launch traced here: 47.9 us
  starting transfers between devices  27.2 us (57%)
  Pallas kernels  11.9 us (25%)
  waiting for transfers between devices  8.04 us (17%)
  between operations  0.79 us (2%)
    ppermute x16, starting transfers between devices, send(): return lax.ppermute(part, 'seq', [(s, s ^ 2 * j) for s in range(n)])  26.5 us
    ppermute x16, waiting for transfers between devices, send(): return lax.ppermute(part, 'seq', [(s, s ^ 2 * j) for s in range(n)])  6.53 us
    pallas_call x2, Pallas kernels, make_heads(): pl.pallas_call(functools.partial(heads_kernel, len(xs), outs), out_shape=...  4.05 us
    pallas_call x2, Pallas kernels, project_part(): pl.pallas_call(functools.partial(project_part_kernel, places, len(xs)), o...  3.08 us
    pallas_call x2, Pallas kernels, attend(): pl.pallas_call(functools.partial(attend_kernel, r, places, share, lead),...  1.97 us
    pallas_call x1, Pallas kernels, modulate(): pl.pallas_call(functools.partial(modulate_kernel, exchange), out_shape=[V...  1.69 us
    ppermute x2, waiting for transfers between devices, swap_parts(): got = lax.ppermute(give, 'seq', [(s, s ^ 1) for s in range(n)])  1.5 us
  transfers between devices with their start and end apart: 18, of which 7 were waited for; matrix products, arithmetic and copies ran while one was open for 0% of the time, Pallas kernels for 12%

profile of v3, /device:TPU:0, one launch (start us, length us, event | category | flops | bytes accessed | tf_op | source)
XLA Modules:
  0.0 47.9 jit_solution(4341377731728017170)
XLA Ops:
  0.7 1.7 %modulate.1 = (bf16[8,2,8,1152]{3,2,1,0:T(8,128)(2,1)S(1)}, f32[1,1152]{1,0:T(1,128)S(1)}, f32[1,1152]{1,0:T(1,128)S(1)}, f32[1,1152]{1,0:T(1,128)S(1)}, f32[2,128,1152]{2,1,0:T(8,128)S(1)}) custom-call(s32[1]{0:T(128)S(6)} %copy.11.step_ref, f32[2,128,1152]{2,1,0:T(8,128)} %bitcast.7, f32[3,30,1152]{2,1,0:T(8,128)} %bitcast.10), custom_call_target="tpu_custom_call" | custom-call | tf_op jit(solution)/shard_map/modulate/pallas_call | solution.py:77
  3.2 0.9 %collective-permute-done.got_ref = bf16[8,2,8,1152]{3,2,1,0:T(8,128)(2,1)S(1)} collective-permute-done((bf16[8,2,8,1152]{3,2,1,0:T(8,128)(2,1)S(1)}, bf16[8,2,8,1152]{3,2,1,0:T(8,128)(2,1)S(1)}, u32[]{:S(2)}, u32[]{:S(2)}) %collective-permute-start) | collective-permute-done | bytes 294944 | tf_op jit(solution)/shard_map/ppermute | solution.py:182
  4.2 6.0 %collective-permute-start.5 = (bf16[2,2,8,1152]{3,2,1,0:T(8,128)(2,1)S(1)}, bf16[2,2,8,1152]{3,2,1,0:T(8,128)(2,1)S(1)}, u32[]{:S(2)}, u32[]{:S(2)}) collective-permute-start(bf16[2,2,8,1152]{3,2,1,0:T(8,128)(2,1)S(1)} %get-tuple-element.58), channel_id=1, source_target_pairs={{0,14},{1,15},{2,12},{3,13},{4,10},{5,11},{6,8},{7,9},{8,6},{9,7},... | collective-permute-start | bytes 221192 | tf_op jit(solution)/shard_map/ppermute | solution.py:179
  10.8 5.2 %collective-permute-start.3 = (bf16[2,2,8,1152]{3,2,1,0:T(8,128)(2,1)S(1)}, bf16[2,2,8,1152]{3,2,1,0:T(8,128)(2,1)S(1)}, u32[]{:S(2)}, u32[]{:S(2)}) collective-permute-start(bf16[2,2,8,1152]{3,2,1,0:T(8,128)(2,1)S(1)} %get-tuple-element.48), channel_id=1, source_target_pairs={{0,10},{1,11},{2,8},{3,9},{4,14},{5,15},{6,12},{7,13},{8,2},{9,3},... | collective-permute-start | bytes 221192 | tf_op jit(solution)/shard_map/ppermute | solution.py:179
  16.0 1.1 %collective-permute-done.6.refs_1_ = bf16[2,2,8,1152]{3,2,1,0:T(8,128)(2,1)S(1)} collective-permute-done((bf16[2,2,8,1152]{3,2,1,0:T(8,128)(2,1)S(1)}, bf16[2,2,8,1152]{3,2,1,0:T(8,128)(2,1)S(1)}, u32[]{:S(2)}, u32[]{:S(2)}) %collective-permute-start.6) | collective-permute-done | bytes 73760 | tf_op jit(solution)/shard_map/ppermute | solution.py:179
  17.1 2.5 %collective-permute-start.1 = (bf16[1,2,8,1152]{3,2,1,0:T(8,128)(2,1)S(1)}, bf16[1,2,8,1152]{3,2,1,0:T(8,128)(2,1)S(1)}, u32[]{:S(2)}, u32[]{:S(2)}) collective-permute-start(bf16[1,2,8,1152]{3,2,1,0:T(8,128)(2,1)S(1)} %get-tuple-element.46), channel_id=1, source_target_pairs={{0,8},{1,9},{2,10},{3,11},{4,12},{5,13},{6,14},{7,15},{8,0},{9,1},... | collective-permute-start | bytes 110600 | tf_op jit(solution)/shard_map/ppermute | solution.py:179
  20.0 0.7 %tables.1 = (bf16[1152,128]{1,0:T(8,128)(2,1)S(1)}, bf16[128,1152]{1,0:T(8,128)(2,1)S(1)}, f32[1,1152]{1,0:T(1,128)S(1)}, f32[1,1152]{1,0:T(1,128)S(1)}) custom-call(f32[1,1152]{1,0:T(1,128)S(1)} %get-tuple-element.50.after_ref.refs_6_.refs_5_, f32[1152]{0:T(1024)} %q_gain_hbm.1, f32[1152]{0:T(1024)} %k_gain_hbm.1), custom_call_target="tpu_custom_call" | custom-call | tf_op jit(solution)/shard_map/tables/pallas_call | solution.py:134
  20.8 2.0 %heads.3 = (bf16[2,2,8,2,32,256]{5,4,3,2,1,0:T(8,128)(2,1)S(1)}, bf16[2,64,1152]{2,1,0:T(8,128)(2,1)S(1)}, bf16[2,64,1152]{2,1,0:T(8,128)(2,1)S(1)}) custom-call(bf16[2,2,8,1152]{3,2,1,0:T(8,128)(2,1)S(1)} %collective-permute-done.5.refs_0_, bf16[2,2,8,1152]{3,2,1,0:T(8,128)(2,1)S(1)} %collective-permute-done.6.refs_1_, ...), custom_call_target="tpu_custom_call" | custom-call | tf_op jit(solution)/shard_map/heads/pallas_call | solution.py:280
  22.8 1.8 %collective-permute-done.2.refs_2_ = bf16[1,2,8,1152]{3,2,1,0:T(8,128)(2,1)S(1)} collective-permute-done((bf16[1,2,8,1152]{3,2,1,0:T(8,128)(2,1)S(1)}, bf16[1,2,8,1152]{3,2,1,0:T(8,128)(2,1)S(1)}, u32[]{:S(2)}, u32[]{:S(2)}) %collective-permute-start.2) | collective-permute-done | bytes 36896 | tf_op jit(solution)/shard_map/ppermute | solution.py:179
  24.6 2.0 %heads.2 = (bf16[2,2,8,2,32,256]{5,4,3,2,1,0:T(8,128)(2,1)S(1)}, bf16[2,64,1152]{2,1,0:T(8,128)(2,1)S(1)}, bf16[2,64,1152]{2,1,0:T(8,128)(2,1)S(1)}) custom-call(bf16[2,2,8,1152]{3,2,1,0:T(8,128)(2,1)S(1)} %get-tuple-element.45.refs_0_, bf16[1,2,8,1152]{3,2,1,0:T(8,128)(2,1)S(1)} %collective-permute-done.1.refs_1_, ...), custom_call_target="tpu_custom_call" | custom-call | tf_op jit(solution)/shard_map/heads/pallas_call | solution.py:280
  26.6 1.0 %attend.3 = bf16[8,2,8,1152]{3,2,1,0:T(8,128)(2,1)S(1)} custom-call(bf16[2,2,8,2,32,256]{5,4,3,2,1,0:T(8,128)(2,1)S(1)} %get-tuple-element.55.refs_0_, bf16[2,64,1152]{2,1,0:T(8,128)(2,1)S(1)} %get-tuple-element.56.refs_1_, bf16[2,64,1152]{2,1,0:T(8,128)(2,1)S(1)} %get-tuple-element.57.refs_2_, ...), custom_call_target="tpu_custom_call" | custom-call | tf_op jit(solution)/shard_map/attend/pallas_call | solution.py:378
  27.7 1.0 %attend.2 = (bf16[8,2,8,1152]{3,2,1,0:T(8,128)(2,1)S(1)}, bf16[1,2,8,1152]{3,2,1,0:T(8,128)(2,1)S(1)}) custom-call(bf16[2,2,8,2,32,256]{5,4,3,2,1,0:T(8,128)(2,1)S(1)} %get-tuple-element.55.refs_0_, bf16[2,64,1152]{2,1,0:T(8,128)(2,1)S(1)} %get-tuple-element.56.refs_1_, bf16[2,64,1152]{2,1,0:T(8,128)(2,1)S(1)} %get-tuple-element.57.refs_2_, ...), custom_call_target="tpu_custom_call" | custom-call | tf_op jit(solution)/shard_map/attend/pallas_call | solution.py:378
  29.3 0.8 %collective-permute-start.16 = (bf16[2,2,8,1152]{3,2,1,0:T(8,128)(2,1)S(1)}, bf16[2,2,8,1152]{3,2,1,0:T(8,128)(2,1)S(1)}, u32[]{:S(2)}, u32[]{:S(2)}) collective-permute-start(bf16[2,2,8,1152]{3,2,1,0:T(8,128)(2,1)S(1)} %get-tuple-element.73), channel_id=1, source_target_pairs={{0,10},{1,11},{2,8},{3,9},{4,14},{5,15},{6,12},{7,13},{8,2},{9,3},... | collective-permute-start | bytes 221192 | tf_op jit(solution)/shard_map/ppermute | solution.py:179
  30.1 2.2 %collective-permute-start.14 = (bf16[1,2,8,1152]{3,2,1,0:T(8,128)(2,1)S(1)}, bf16[1,2,8,1152]{3,2,1,0:T(8,128)(2,1)S(1)}, u32[]{:S(2)}, u32[]{:S(2)}) collective-permute-start(bf16[1,2,8,1152]{3,2,1,0:T(8,128)(2,1)S(1)} %get-tuple-element.71), channel_id=1, source_target_pairs={{0,8},{1,9},{2,10},{3,11},{4,12},{5,13},{6,14},{7,15},{8,0},{9,1},... | collective-permute-start | bytes 110600 | tf_op jit(solution)/shard_map/ppermute | solution.py:179
  32.2 0.8 %collective-permute-start.15 = (bf16[1,2,8,1152]{3,2,1,0:T(8,128)(2,1)S(1)}, bf16[1,2,8,1152]{3,2,1,0:T(8,128)(2,1)S(1)}, u32[]{:S(2)}, u32[]{:S(2)}) collective-permute-start(bf16[1,2,8,1152]{3,2,1,0:T(8,128)(2,1)S(1)} %get-tuple-element.72), channel_id=1, source_target_pairs={{0,8},{1,9},{2,10},{3,11},{4,12},{5,13},{6,14},{7,15},{8,0},{9,1},... | collective-permute-start | bytes 110600 | tf_op jit(solution)/shard_map/ppermute | solution.py:179
  33.0 2.7 %collective-permute-start.10 = (bf16[2,2,8,1152]{3,2,1,0:T(8,128)(2,1)S(1)}, bf16[2,2,8,1152]{3,2,1,0:T(8,128)(2,1)S(1)}, u32[]{:S(2)}, u32[]{:S(2)}) collective-permute-start(bf16[2,2,8,1152]{3,2,1,0:T(8,128)(2,1)S(1)} %get-tuple-element.66), channel_id=1, source_target_pairs={{0,14},{1,15},{2,12},{3,13},{4,10},{5,11},{6,8},{7,9},{8,6},{9,7},... | collective-permute-start | bytes 221192 | tf_op jit(solution)/shard_map/ppermute | solution.py:179
  35.7 0.9 %collective-permute-start.17 = (bf16[2,2,8,1152]{3,2,1,0:T(8,128)(2,1)S(1)}, bf16[2,2,8,1152]{3,2,1,0:T(8,128)(2,1)S(1)}, u32[]{:S(2)}, u32[]{:S(2)}) collective-permute-start(bf16[2,2,8,1152]{3,2,1,0:T(8,128)(2,1)S(1)} %get-tuple-element.74), channel_id=1, source_target_pairs={{0,6},{1,7},{2,4},{3,5},{4,2},{5,3},{6,0},{7,1},{8,14},{9,15},{10,... | collective-permute-start | bytes 221192 | tf_op jit(solution)/shard_map/ppermute | solution.py:179
  36.6 2.4 %collective-permute-done.14.refs_1_ = bf16[1,2,8,1152]{3,2,1,0:T(8,128)(2,1)S(1)} collective-permute-done((bf16[1,2,8,1152]{3,2,1,0:T(8,128)(2,1)S(1)}, bf16[1,2,8,1152]{3,2,1,0:T(8,128)(2,1)S(1)}, u32[]{:S(2)}, u32[]{:S(2)}) %collective-permute-start.14) | collective-permute-done | bytes 36896 | tf_op jit(solution)/shard_map/ppermute | solution.py:179
  39.1 2.1 %collective-permute-start.11 = (bf16[2,2,8,1152]{3,2,1,0:T(8,128)(2,1)S(1)}, bf16[2,2,8,1152]{3,2,1,0:T(8,128)(2,1)S(1)}, u32[]{:S(2)}, u32[]{:S(2)}) collective-permute-start(bf16[2,2,8,1152]{3,2,1,0:T(8,128)(2,1)S(1)} %get-tuple-element.67), channel_id=1, source_target_pairs={{0,12},{1,13},{2,14},{3,15},{4,8},{5,9},{6,10},{7,11},{8,4},{9,5},... | collective-permute-start | bytes 221192 | tf_op jit(solution)/shard_map/ppermute | solution.py:179
  41.1 2.4 %collective-permute-start.13 = (bf16[2,2,8,1152]{3,2,1,0:T(8,128)(2,1)S(1)}, bf16[2,2,8,1152]{3,2,1,0:T(8,128)(2,1)S(1)}, u32[]{:S(2)}, u32[]{:S(2)}) collective-permute-start(bf16[2,2,8,1152]{3,2,1,0:T(8,128)(2,1)S(1)} %get-tuple-element.69), channel_id=1, source_target_pairs={{0,2},{1,3},{2,0},{3,1},{4,6},{5,7},{6,4},{7,5},{8,10},{9,11},{10,... | collective-permute-start | bytes 221192 | tf_op jit(solution)/shard_map/ppermute | solution.py:179
  43.5 1.5 %project.2.refs_7_ = f32[2,128,1152]{2,1,0:T(8,128)} custom-call(bf16[2,2,8,1152]{3,2,1,0:T(8,128)(2,1)S(1)} %get-tuple-element.70.refs_0_, bf16[1,2,8,1152]{3,2,1,0:T(8,128)(2,1)S(1)} %collective-permute-done.14.refs_1_, bf16[1,2,8,1152]{3,2,1,0:T(8,128)(2,1)S(1)} %collective-permute-done.15.refs_2_, ...), custom_call_target="tpu_custom_call" | custom-call | tf_op jit(solution)/shard_map/project/pallas_call | solution.py:457
  45.1 0.6 %collective-permute-done.11.refs_1_ = bf16[2,2,8,1152]{3,2,1,0:T(8,128)(2,1)S(1)} collective-permute-done((bf16[2,2,8,1152]{3,2,1,0:T(8,128)(2,1)S(1)}, bf16[2,2,8,1152]{3,2,1,0:T(8,128)(2,1)S(1)}, u32[]{:S(2)}, u32[]{:S(2)}) %collective-permute-start.11) | collective-permute-done | bytes 73760 | tf_op jit(solution)/shard_map/ppermute | solution.py:179
  45.7 0.6 %collective-permute-done.12.refs_2_ = bf16[2,2,8,1152]{3,2,1,0:T(8,128)(2,1)S(1)} collective-permute-done((bf16[2,2,8,1152]{3,2,1,0:T(8,128)(2,1)S(1)}, bf16[2,2,8,1152]{3,2,1,0:T(8,128)(2,1)S(1)}, u32[]{:S(2)}, u32[]{:S(2)}) %collective-permute-start.12) | collective-permute-done | bytes 73760 | tf_op jit(solution)/shard_map/ppermute | solution.py:179
  46.3 1.5 %project.3 = f32[2,128,1152]{2,1,0:T(8,128)} custom-call(bf16[2,2,8,1152]{3,2,1,0:T(8,128)(2,1)S(1)} %collective-permute-done.10.refs_0_, bf16[2,2,8,1152]{3,2,1,0:T(8,128)(2,1)S(1)} %collective-permute-done.11.refs_1_, bf16[2,2,8,1152]{3,2,1,0:T(8,128)(2,1)S(1)} %collective-permute-done.12.refs_2_, ...), custom_call_target="tpu_custom_call", output_to_operand_aliasing={{}: (7, {})} | custom-call | tf_op jit(solution)/shard_map/project/pallas_call | solution.py:457
  (32 shorter events, 2.7 us)
Async XLA Ops:
  2.3 1.8 %collective-permute-start = (bf16[8,2,8,1152]{3,2,1,0:T(8,128)(2,1)S(1)}, bf16[8,2,8,1152]{3,2,1,0:T(8,128)(2,1)S(1)}, u32[]{:S(2)}, u32[]{:S(2)}) collective-permute-start(bf16[8,2,8,1152]{3,2,1,0:T(8,128)(2,1)S(1)} %get-tuple-element.44), channel_id=1, source_target_pairs={{0,1},{1,0},{2,3},{3,2},{4,5},{5,4},{6,7},{7,6},{8,9},{9,8},{10,11... | collective-permute-start | bytes 884744 | tf_op jit(solution)/shard_map/ppermute | solution.py:182
  4.1 16.6 %slice-start = ((s8[7962624]{0:T(1024)(128)(4,1)}), s8[4194304]{0:T(1024)(128)(4,1)S(1)}, s32[]{:S(2)}) async-start(s8[7962624]{0:T(1024)(128)(4,1)} %bitcast.5), calls=%async_computation | async-start | bytes 8388608
  4.1 16.7 %slice-start.1 = ((s8[7962624]{0:T(1024)(128)(4,1)}), s8[3768320]{0:T(1024)(128)(4,1)S(1)}, s32[]{:S(2)}) async-start(s8[7962624]{0:T(1024)(128)(4,1)} %bitcast.5), calls=%async_computation.1 | async-start | bytes 7536640
  4.2 11.8 %collective-permute-start.5 = (bf16[2,2,8,1152]{3,2,1,0:T(8,128)(2,1)S(1)}, bf16[2,2,8,1152]{3,2,1,0:T(8,128)(2,1)S(1)}, u32[]{:S(2)}, u32[]{:S(2)}) collective-permute-start(bf16[2,2,8,1152]{3,2,1,0:T(8,128)(2,1)S(1)} %get-tuple-element.58), channel_id=1, source_target_pairs={{0,14},{1,15},{2,12},{3,13},{4,10},{5,11},{6,8},{7,9},{8,6},{9,7},... | collective-permute-start | bytes 221192 | tf_op jit(solution)/shard_map/ppermute | solution.py:179
  10.1 6.9 %collective-permute-start.6 = (bf16[2,2,8,1152]{3,2,1,0:T(8,128)(2,1)S(1)}, bf16[2,2,8,1152]{3,2,1,0:T(8,128)(2,1)S(1)}, u32[]{:S(2)}, u32[]{:S(2)}) collective-permute-start(bf16[2,2,8,1152]{3,2,1,0:T(8,128)(2,1)S(1)} %get-tuple-element.59), channel_id=1, source_target_pairs={{0,12},{1,13},{2,14},{3,15},{4,8},{5,9},{6,10},{7,11},{8,4},{9,5},... | collective-permute-start | bytes 221192 | tf_op jit(solution)/shard_map/ppermute | solution.py:179
  10.4 9.2 %collective-permute-start.7 = (bf16[2,2,8,1152]{3,2,1,0:T(8,128)(2,1)S(1)}, bf16[2,2,8,1152]{3,2,1,0:T(8,128)(2,1)S(1)}, u32[]{:S(2)}, u32[]{:S(2)}) collective-permute-start(bf16[2,2,8,1152]{3,2,1,0:T(8,128)(2,1)S(1)} %get-tuple-element.60), channel_id=1, source_target_pairs={{0,4},{1,5},{2,6},{3,7},{4,0},{5,1},{6,2},{7,3},{8,12},{9,13},{10,... | collective-permute-start | bytes 221192 | tf_op jit(solution)/shard_map/ppermute | solution.py:179
  10.4 10.4 %collective-permute-start.8 = (bf16[2,2,8,1152]{3,2,1,0:T(8,128)(2,1)S(1)}, bf16[2,2,8,1152]{3,2,1,0:T(8,128)(2,1)S(1)}, u32[]{:S(2)}, u32[]{:S(2)}) collective-permute-start(bf16[2,2,8,1152]{3,2,1,0:T(8,128)(2,1)S(1)} %get-tuple-element.61), channel_id=1, source_target_pairs={{0,2},{1,3},{2,0},{3,1},{4,6},{5,7},{6,4},{7,5},{8,10},{9,11},{10,... | collective-permute-start | bytes 221192 | tf_op jit(solution)/shard_map/ppermute | solution.py:179
  10.8 13.8 %collective-permute-start.3 = (bf16[2,2,8,1152]{3,2,1,0:T(8,128)(2,1)S(1)}, bf16[2,2,8,1152]{3,2,1,0:T(8,128)(2,1)S(1)}, u32[]{:S(2)}, u32[]{:S(2)}) collective-permute-start(bf16[2,2,8,1152]{3,2,1,0:T(8,128)(2,1)S(1)} %get-tuple-element.48), channel_id=1, source_target_pairs={{0,10},{1,11},{2,8},{3,9},{4,14},{5,15},{6,12},{7,13},{8,2},{9,3},... | collective-permute-start | bytes 221192 | tf_op jit(solution)/shard_map/ppermute | solution.py:179
  16.0 8.6 %collective-permute-start.4 = (bf16[2,2,8,1152]{3,2,1,0:T(8,128)(2,1)S(1)}, bf16[2,2,8,1152]{3,2,1,0:T(8,128)(2,1)S(1)}, u32[]{:S(2)}, u32[]{:S(2)}) collective-permute-start(bf16[2,2,8,1152]{3,2,1,0:T(8,128)(2,1)S(1)} %get-tuple-element.49), channel_id=1, source_target_pairs={{0,6},{1,7},{2,4},{3,5},{4,2},{5,3},{6,0},{7,1},{8,14},{9,15},{10,... | collective-permute-start | bytes 221192 | tf_op jit(solution)/shard_map/ppermute | solution.py:179
  17.1 5.7 %collective-permute-start.1 = (bf16[1,2,8,1152]{3,2,1,0:T(8,128)(2,1)S(1)}, bf16[1,2,8,1152]{3,2,1,0:T(8,128)(2,1)S(1)}, u32[]{:S(2)}, u32[]{:S(2)}) collective-permute-start(bf16[1,2,8,1152]{3,2,1,0:T(8,128)(2,1)S(1)} %get-tuple-element.46), channel_id=1, source_target_pairs={{0,8},{1,9},{2,10},{3,11},{4,12},{5,13},{6,14},{7,15},{8,0},{9,1},... | collective-permute-start | bytes 110600 | tf_op jit(solution)/shard_map/ppermute | solution.py:179
  19.6 5.0 %collective-permute-start.2 = (bf16[1,2,8,1152]{3,2,1,0:T(8,128)(2,1)S(1)}, bf16[1,2,8,1152]{3,2,1,0:T(8,128)(2,1)S(1)}, u32[]{:S(2)}, u32[]{:S(2)}) collective-permute-start(bf16[1,2,8,1152]{3,2,1,0:T(8,128)(2,1)S(1)} %get-tuple-element.47), channel_id=1, source_target_pairs={{0,8},{1,9},{2,10},{3,11},{4,12},{5,13},{6,14},{7,15},{8,0},{9,1},... | collective-permute-start | bytes 110600 | tf_op jit(solution)/shard_map/ppermute | solution.py:179
  27.6 1.6 %collective-permute-start.9 = (bf16[8,2,8,1152]{3,2,1,0:T(8,128)(2,1)S(1)}, bf16[8,2,8,1152]{3,2,1,0:T(8,128)(2,1)S(1)}, u32[]{:S(2)}, u32[]{:S(2)}) collective-permute-start(bf16[8,2,8,1152]{3,2,1,0:T(8,128)(2,1)S(1)} %attend.3), channel_id=1, source_target_pairs={{0,1},{1,0},{2,3},{3,2},{4,5},{5,4},{6,7},{7,6},{8,9},{9,8},{10,11... | collective-permute-start | bytes 884744 | tf_op jit(solution)/shard_map/ppermute | solution.py:182
  29.3 14.3 %copy-start = (bf16[1152,1152]{1,0:T(8,128)(2,1)S(1)}, bf16[1152,1152]{1,0:T(8,128)(2,1)}, u32[]{:S(2)}) copy-start(bf16[1152,1152]{1,0:T(8,128)(2,1)} %refs_4_.3) | copy-start | bytes 7962628
  29.3 14.3 %copy-start.1 = (f32[2,1,128,1152]{3,2,1,0:T(8,128)S(1)}, f32[2,1,128,1152]{3,2,1,0:T(8,128)}, u32[]{:S(2)}) copy-start(f32[2,1,128,1152]{3,2,1,0:T(8,128)} %param.7) | copy-start | bytes 3538948
  29.3 11.8 %collective-permute-start.16 = (bf16[2,2,8,1152]{3,2,1,0:T(8,128)(2,1)S(1)}, bf16[2,2,8,1152]{3,2,1,0:T(8,128)(2,1)S(1)}, u32[]{:S(2)}, u32[]{:S(2)}) collective-permute-start(bf16[2,2,8,1152]{3,2,1,0:T(8,128)(2,1)S(1)} %get-tuple-element.73), channel_id=1, source_target_pairs={{0,10},{1,11},{2,8},{3,9},{4,14},{5,15},{6,12},{7,13},{8,2},{9,3},... | collective-permute-start | bytes 221192 | tf_op jit(solution)/shard_map/ppermute | solution.py:179
  30.1 9.0 %collective-permute-start.14 = (bf16[1,2,8,1152]{3,2,1,0:T(8,128)(2,1)S(1)}, bf16[1,2,8,1152]{3,2,1,0:T(8,128)(2,1)S(1)}, u32[]{:S(2)}, u32[]{:S(2)}) collective-permute-start(bf16[1,2,8,1152]{3,2,1,0:T(8,128)(2,1)S(1)} %get-tuple-element.71), channel_id=1, source_target_pairs={{0,8},{1,9},{2,10},{3,11},{4,12},{5,13},{6,14},{7,15},{8,0},{9,1},... | collective-permute-start | bytes 110600 | tf_op jit(solution)/shard_map/ppermute | solution.py:179
  32.2 8.9 %collective-permute-start.15 = (bf16[1,2,8,1152]{3,2,1,0:T(8,128)(2,1)S(1)}, bf16[1,2,8,1152]{3,2,1,0:T(8,128)(2,1)S(1)}, u32[]{:S(2)}, u32[]{:S(2)}) collective-permute-start(bf16[1,2,8,1152]{3,2,1,0:T(8,128)(2,1)S(1)} %get-tuple-element.72), channel_id=1, source_target_pairs={{0,8},{1,9},{2,10},{3,11},{4,12},{5,13},{6,14},{7,15},{8,0},{9,1},... | collective-permute-start | bytes 110600 | tf_op jit(solution)/shard_map/ppermute | solution.py:179
  33.0 12.1 %collective-permute-start.10 = (bf16[2,2,8,1152]{3,2,1,0:T(8,128)(2,1)S(1)}, bf16[2,2,8,1152]{3,2,1,0:T(8,128)(2,1)S(1)}, u32[]{:S(2)}, u32[]{:S(2)}) collective-permute-start(bf16[2,2,8,1152]{3,2,1,0:T(8,128)(2,1)S(1)} %get-tuple-element.66), channel_id=1, source_target_pairs={{0,14},{1,15},{2,12},{3,13},{4,10},{5,11},{6,8},{7,9},{8,6},{9,7},... | collective-permute-start | bytes 221192 | tf_op jit(solution)/shard_map/ppermute | solution.py:179
  35.7 7.8 %collective-permute-start.17 = (bf16[2,2,8,1152]{3,2,1,0:T(8,128)(2,1)S(1)}, bf16[2,2,8,1152]{3,2,1,0:T(8,128)(2,1)S(1)}, u32[]{:S(2)}, u32[]{:S(2)}) collective-permute-start(bf16[2,2,8,1152]{3,2,1,0:T(8,128)(2,1)S(1)} %get-tuple-element.74), channel_id=1, source_target_pairs={{0,6},{1,7},{2,4},{3,5},{4,2},{5,3},{6,0},{7,1},{8,14},{9,15},{10,... | collective-permute-start | bytes 221192 | tf_op jit(solution)/shard_map/ppermute | solution.py:179
  39.1 6.6 %collective-permute-start.11 = (bf16[2,2,8,1152]{3,2,1,0:T(8,128)(2,1)S(1)}, bf16[2,2,8,1152]{3,2,1,0:T(8,128)(2,1)S(1)}, u32[]{:S(2)}, u32[]{:S(2)}) collective-permute-start(bf16[2,2,8,1152]{3,2,1,0:T(8,128)(2,1)S(1)} %get-tuple-element.67), channel_id=1, source_target_pairs={{0,12},{1,13},{2,14},{3,15},{4,8},{5,9},{6,10},{7,11},{8,4},{9,5},... | collective-permute-start | bytes 221192 | tf_op jit(solution)/shard_map/ppermute | solution.py:179
  41.1 5.2 %collective-permute-start.12 = (bf16[2,2,8,1152]{3,2,1,0:T(8,128)(2,1)S(1)}, bf16[2,2,8,1152]{3,2,1,0:T(8,128)(2,1)S(1)}, u32[]{:S(2)}, u32[]{:S(2)}) collective-permute-start(bf16[2,2,8,1152]{3,2,1,0:T(8,128)(2,1)S(1)} %get-tuple-element.68), channel_id=1, source_target_pairs={{0,4},{1,5},{2,6},{3,7},{4,0},{5,1},{6,2},{7,3},{8,12},{9,13},{10,... | collective-permute-start | bytes 221192 | tf_op jit(solution)/shard_map/ppermute | solution.py:179
  41.1 5.2 %collective-permute-start.13 = (bf16[2,2,8,1152]{3,2,1,0:T(8,128)(2,1)S(1)}, bf16[2,2,8,1152]{3,2,1,0:T(8,128)(2,1)S(1)}, u32[]{:S(2)}, u32[]{:S(2)}) collective-permute-start(bf16[2,2,8,1152]{3,2,1,0:T(8,128)(2,1)S(1)} %get-tuple-element.69), channel_id=1, source_target_pairs={{0,2},{1,3},{2,0},{3,1},{4,6},{5,7},{6,4},{7,5},{8,10},{9,11},{10,... | collective-permute-start | bytes 221192 | tf_op jit(solution)/shard_map/ppermute | solution.py:179

commit v4 on v3

--- a/solution.py
+++ b/solution.py
@@ -54,13 +54,30 @@
     def fetch(b):
         return pltpu.make_async_copy(rows_hbm.at[b], rows_ref.at[b], sems.at[b])
 
-    mods = pltpu.make_async_copy(mods_hbm, mods_ref, sems.at[branch])
+    steps, tile = mods_hbm.shape[1], mods_ref.shape[1]
+    whole = steps // tile * tile
+    step = step_ref[0]
+
+    def fetch_mods(act):
+        def full():
+            block = pl.ds(pl.multiple_of(step // tile * tile, tile), tile)
+            act(pltpu.make_async_copy(mods_hbm.at[:, block], mods_ref, sems.at[branch]))
+
+        def short():
+            block = pl.ds(whole, steps - whole)
+            part = mods_ref.at[:, pl.ds(0, steps - whole)]
+            act(pltpu.make_async_copy(mods_hbm.at[:, block], part, sems.at[branch]))
+
+        pl.when(step < whole)(full)
+        if whole < steps:
+            pl.when(step >= whole)(short)
+
+    fetch_mods(lambda copy: copy.start())
     fetch(0).start()
-    mods.start()
     for b in range(1, branch):
         fetch(b).start()
-    mods.wait()
-    step = pl.ds(step_ref[0], 1)
+    fetch_mods(lambda copy: copy.wait())
+    step = pl.ds(lax.rem(step, tile), 1)
     shift_row, scale_row = mods_ref[0, step, :], 1.0 + mods_ref[1, step, :]
     shift_ref[...] = shift_row
     scale_ref[...] = scale_row
@@ -87,7 +104,7 @@
         + [pl.BlockSpec(memory_space=pltpu.HBM)] * 2,
         out_specs=[pl.BlockSpec(memory_space=VMEM)] * 5,
         scratch_shapes=[
-            VMEM((3, step_mods.shape[0], width), F32),
+            VMEM((3, 8, width), F32),
             pltpu.SemaphoreType.DMA((branch + 1,)),
         ],
         compiler_params=params(8),

time: 48.1 us -> 48 us (level)
  no operation moved by 1% of the time
where the time goes in v4:
time: 48 us; the launch traced here: 47.8 us
  starting transfers between devices  27.2 us (57%)
  Pallas kernels  11.8 us (25%)
  waiting for transfers between devices  8.02 us (17%)
  between operations  0.79 us (2%)
    ppermute x16, starting transfers between devices, send(): return lax.ppermute(part, 'seq', [(s, s ^ 2 * j) for s in range(n)])  26.5 us
    ppermute x16, waiting for transfers between devices, send(): return lax.ppermute(part, 'seq', [(s, s ^ 2 * j) for s in range(n)])  6.52 us
    pallas_call x2, Pallas kernels, make_heads(): pl.pallas_call(functools.partial(heads_kernel, len(xs), outs), out_shape=...  4.06 us
    pallas_call x2, Pallas kernels, project_part(): pl.pallas_call(functools.partial(project_part_kernel, places, len(xs)), o...  3.08 us
    pallas_call x2, Pallas kernels, attend(): pl.pallas_call(functools.partial(attend_kernel, r, places, share, lead),...  1.97 us
    pallas_call x1, Pallas kernels, modulate(): pl.pallas_call(functools.partial(modulate_kernel, exchange), out_shape=[V...  1.62 us
    ppermute x2, waiting for transfers between devices, swap_parts(): got = lax.ppermute(give, 'seq', [(s, s ^ 1) for s in range(n)])  1.5 us
  transfers between devices with their start and end apart: 18, of which 7 were waited for; matrix products, arithmetic and copies ran while one was open for 0% of the time, Pallas kernels for 12%

profile of v4, /device:TPU:0, one launch (start us, length us, event | category | flops | bytes accessed | tf_op | source)
XLA Modules:
  0.0 47.8 jit_solution(4584657044249301148)
XLA Ops:
  0.7 1.6 %modulate.1 = (bf16[8,2,8,1152]{3,2,1,0:T(8,128)(2,1)S(1)}, f32[1,1152]{1,0:T(1,128)S(1)}, f32[1,1152]{1,0:T(1,128)S(1)}, f32[1,1152]{1,0:T(1,128)S(1)}, f32[2,128,1152]{2,1,0:T(8,128)S(1)}) custom-call(s32[1]{0:T(128)S(6)} %copy.11.step_ref, f32[2,128,1152]{2,1,0:T(8,128)} %bitcast.7, f32[3,30,1152]{2,1,0:T(8,128)} %bitcast.10), custom_call_target="tpu_custom_call" | custom-call | tf_op jit(solution)/shard_map/modulate/pallas_call | solution.py:94
  3.1 0.9 %collective-permute-done.got_ref = bf16[8,2,8,1152]{3,2,1,0:T(8,128)(2,1)S(1)} collective-permute-done((bf16[8,2,8,1152]{3,2,1,0:T(8,128)(2,1)S(1)}, bf16[8,2,8,1152]{3,2,1,0:T(8,128)(2,1)S(1)}, u32[]{:S(2)}, u32[]{:S(2)}) %collective-permute-start) | collective-permute-done | bytes 294944 | tf_op jit(solution)/shard_map/ppermute | solution.py:199
  4.1 6.0 %collective-permute-start.5 = (bf16[2,2,8,1152]{3,2,1,0:T(8,128)(2,1)S(1)}, bf16[2,2,8,1152]{3,2,1,0:T(8,128)(2,1)S(1)}, u32[]{:S(2)}, u32[]{:S(2)}) collective-permute-start(bf16[2,2,8,1152]{3,2,1,0:T(8,128)(2,1)S(1)} %get-tuple-element.58), channel_id=1, source_target_pairs={{0,14},{1,15},{2,12},{3,13},{4,10},{5,11},{6,8},{7,9},{8,6},{9,7},... | collective-permute-start | bytes 221192 | tf_op jit(solution)/shard_map/ppermute | solution.py:196
  10.7 5.2 %collective-permute-start.3 = (bf16[2,2,8,1152]{3,2,1,0:T(8,128)(2,1)S(1)}, bf16[2,2,8,1152]{3,2,1,0:T(8,128)(2,1)S(1)}, u32[]{:S(2)}, u32[]{:S(2)}) collective-permute-start(bf16[2,2,8,1152]{3,2,1,0:T(8,128)(2,1)S(1)} %get-tuple-element.48), channel_id=1, source_target_pairs={{0,10},{1,11},{2,8},{3,9},{4,14},{5,15},{6,12},{7,13},{8,2},{9,3},... | collective-permute-start | bytes 221192 | tf_op jit(solution)/shard_map/ppermute | solution.py:196
  15.9 1.1 %collective-permute-done.6.refs_1_ = bf16[2,2,8,1152]{3,2,1,0:T(8,128)(2,1)S(1)} collective-permute-done((bf16[2,2,8,1152]{3,2,1,0:T(8,128)(2,1)S(1)}, bf16[2,2,8,1152]{3,2,1,0:T(8,128)(2,1)S(1)}, u32[]{:S(2)}, u32[]{:S(2)}) %collective-permute-start.6) | collective-permute-done | bytes 73760 | tf_op jit(solution)/shard_map/ppermute | solution.py:196
  17.0 2.5 %collective-permute-start.1 = (bf16[1,2,8,1152]{3,2,1,0:T(8,128)(2,1)S(1)}, bf16[1,2,8,1152]{3,2,1,0:T(8,128)(2,1)S(1)}, u32[]{:S(2)}, u32[]{:S(2)}) collective-permute-start(bf16[1,2,8,1152]{3,2,1,0:T(8,128)(2,1)S(1)} %get-tuple-element.46), channel_id=1, source_target_pairs={{0,8},{1,9},{2,10},{3,11},{4,12},{5,13},{6,14},{7,15},{8,0},{9,1},... | collective-permute-start | bytes 110600 | tf_op jit(solution)/shard_map/ppermute | solution.py:196
  20.0 0.7 %tables.1 = (bf16[1152,128]{1,0:T(8,128)(2,1)S(1)}, bf16[128,1152]{1,0:T(8,128)(2,1)S(1)}, f32[1,1152]{1,0:T(1,128)S(1)}, f32[1,1152]{1,0:T(1,128)S(1)}) custom-call(f32[1,1152]{1,0:T(1,128)S(1)} %get-tuple-element.50.after_ref.refs_6_.refs_5_, f32[1152]{0:T(1024)} %q_gain_hbm.1, f32[1152]{0:T(1024)} %k_gain_hbm.1), custom_call_target="tpu_custom_call" | custom-call | tf_op jit(solution)/shard_map/tables/pallas_call | solution.py:151
  20.7 2.0 %heads.3 = (bf16[2,2,8,2,32,256]{5,4,3,2,1,0:T(8,128)(2,1)S(1)}, bf16[2,64,1152]{2,1,0:T(8,128)(2,1)S(1)}, bf16[2,64,1152]{2,1,0:T(8,128)(2,1)S(1)}) custom-call(bf16[2,2,8,1152]{3,2,1,0:T(8,128)(2,1)S(1)} %collective-permute-done.5.refs_0_, bf16[2,2,8,1152]{3,2,1,0:T(8,128)(2,1)S(1)} %collective-permute-done.6.refs_1_, ...), custom_call_target="tpu_custom_call" | custom-call | tf_op jit(solution)/shard_map/heads/pallas_call | solution.py:297
  22.8 1.7 %collective-permute-done.2.refs_2_ = bf16[1,2,8,1152]{3,2,1,0:T(8,128)(2,1)S(1)} collective-permute-done((bf16[1,2,8,1152]{3,2,1,0:T(8,128)(2,1)S(1)}, bf16[1,2,8,1152]{3,2,1,0:T(8,128)(2,1)S(1)}, u32[]{:S(2)}, u32[]{:S(2)}) %collective-permute-start.2) | collective-permute-done | bytes 36896 | tf_op jit(solution)/shard_map/ppermute | solution.py:196
  24.5 2.0 %heads.2 = (bf16[2,2,8,2,32,256]{5,4,3,2,1,0:T(8,128)(2,1)S(1)}, bf16[2,64,1152]{2,1,0:T(8,128)(2,1)S(1)}, bf16[2,64,1152]{2,1,0:T(8,128)(2,1)S(1)}) custom-call(bf16[2,2,8,1152]{3,2,1,0:T(8,128)(2,1)S(1)} %get-tuple-element.45.refs_0_, bf16[1,2,8,1152]{3,2,1,0:T(8,128)(2,1)S(1)} %collective-permute-done.1.refs_1_, ...), custom_call_target="tpu_custom_call" | custom-call | tf_op jit(solution)/shard_map/heads/pallas_call | solution.py:297
  26.6 1.0 %attend.3 = bf16[8,2,8,1152]{3,2,1,0:T(8,128)(2,1)S(1)} custom-call(bf16[2,2,8,2,32,256]{5,4,3,2,1,0:T(8,128)(2,1)S(1)} %get-tuple-element.55.refs_0_, bf16[2,64,1152]{2,1,0:T(8,128)(2,1)S(1)} %get-tuple-element.56.refs_1_, bf16[2,64,1152]{2,1,0:T(8,128)(2,1)S(1)} %get-tuple-element.57.refs_2_, ...), custom_call_target="tpu_custom_call" | custom-call | tf_op jit(solution)/shard_map/attend/pallas_call | solution.py:395
  27.6 1.0 %attend.2 = (bf16[8,2,8,1152]{3,2,1,0:T(8,128)(2,1)S(1)}, bf16[1,2,8,1152]{3,2,1,0:T(8,128)(2,1)S(1)}) custom-call(bf16[2,2,8,2,32,256]{5,4,3,2,1,0:T(8,128)(2,1)S(1)} %get-tuple-element.55.refs_0_, bf16[2,64,1152]{2,1,0:T(8,128)(2,1)S(1)} %get-tuple-element.56.refs_1_, bf16[2,64,1152]{2,1,0:T(8,128)(2,1)S(1)} %get-tuple-element.57.refs_2_, ...), custom_call_target="tpu_custom_call" | custom-call | tf_op jit(solution)/shard_map/attend/pallas_call | solution.py:395
  29.2 0.8 %collective-permute-start.16 = (bf16[2,2,8,1152]{3,2,1,0:T(8,128)(2,1)S(1)}, bf16[2,2,8,1152]{3,2,1,0:T(8,128)(2,1)S(1)}, u32[]{:S(2)}, u32[]{:S(2)}) collective-permute-start(bf16[2,2,8,1152]{3,2,1,0:T(8,128)(2,1)S(1)} %get-tuple-element.73), channel_id=1, source_target_pairs={{0,10},{1,11},{2,8},{3,9},{4,14},{5,15},{6,12},{7,13},{8,2},{9,3},... | collective-permute-start | bytes 221192 | tf_op jit(solution)/shard_map/ppermute | solution.py:196
  30.0 2.2 %collective-permute-start.14 = (bf16[1,2,8,1152]{3,2,1,0:T(8,128)(2,1)S(1)}, bf16[1,2,8,1152]{3,2,1,0:T(8,128)(2,1)S(1)}, u32[]{:S(2)}, u32[]{:S(2)}) collective-permute-start(bf16[1,2,8,1152]{3,2,1,0:T(8,128)(2,1)S(1)} %get-tuple-element.71), channel_id=1, source_target_pairs={{0,8},{1,9},{2,10},{3,11},{4,12},{5,13},{6,14},{7,15},{8,0},{9,1},... | collective-permute-start | bytes 110600 | tf_op jit(solution)/shard_map/ppermute | solution.py:196
  32.2 0.8 %collective-permute-start.15 = (bf16[1,2,8,1152]{3,2,1,0:T(8,128)(2,1)S(1)}, bf16[1,2,8,1152]{3,2,1,0:T(8,128)(2,1)S(1)}, u32[]{:S(2)}, u32[]{:S(2)}) collective-permute-start(bf16[1,2,8,1152]{3,2,1,0:T(8,128)(2,1)S(1)} %get-tuple-element.72), channel_id=1, source_target_pairs={{0,8},{1,9},{2,10},{3,11},{4,12},{5,13},{6,14},{7,15},{8,0},{9,1},... | collective-permute-start | bytes 110600 | tf_op jit(solution)/shard_map/ppermute | solution.py:196
  33.0 2.7 %collective-permute-start.10 = (bf16[2,2,8,1152]{3,2,1,0:T(8,128)(2,1)S(1)}, bf16[2,2,8,1152]{3,2,1,0:T(8,128)(2,1)S(1)}, u32[]{:S(2)}, u32[]{:S(2)}) collective-permute-start(bf16[2,2,8,1152]{3,2,1,0:T(8,128)(2,1)S(1)} %get-tuple-element.66), channel_id=1, source_target_pairs={{0,14},{1,15},{2,12},{3,13},{4,10},{5,11},{6,8},{7,9},{8,6},{9,7},... | collective-permute-start | bytes 221192 | tf_op jit(solution)/shard_map/ppermute | solution.py:196
  35.7 0.9 %collective-permute-start.17 = (bf16[2,2,8,1152]{3,2,1,0:T(8,128)(2,1)S(1)}, bf16[2,2,8,1152]{3,2,1,0:T(8,128)(2,1)S(1)}, u32[]{:S(2)}, u32[]{:S(2)}) collective-permute-start(bf16[2,2,8,1152]{3,2,1,0:T(8,128)(2,1)S(1)} %get-tuple-element.74), channel_id=1, source_target_pairs={{0,6},{1,7},{2,4},{3,5},{4,2},{5,3},{6,0},{7,1},{8,14},{9,15},{10,... | collective-permute-start | bytes 221192 | tf_op jit(solution)/shard_map/ppermute | solution.py:196
  36.6 2.4 %collective-permute-done.14.refs_1_ = bf16[1,2,8,1152]{3,2,1,0:T(8,128)(2,1)S(1)} collective-permute-done((bf16[1,2,8,1152]{3,2,1,0:T(8,128)(2,1)S(1)}, bf16[1,2,8,1152]{3,2,1,0:T(8,128)(2,1)S(1)}, u32[]{:S(2)}, u32[]{:S(2)}) %collective-permute-start.14) | collective-permute-done | bytes 36896 | tf_op jit(solution)/shard_map/ppermute | solution.py:196
  39.0 2.1 %collective-permute-start.11 = (bf16[2,2,8,1152]{3,2,1,0:T(8,128)(2,1)S(1)}, bf16[2,2,8,1152]{3,2,1,0:T(8,128)(2,1)S(1)}, u32[]{:S(2)}, u32[]{:S(2)}) collective-permute-start(bf16[2,2,8,1152]{3,2,1,0:T(8,128)(2,1)S(1)} %get-tuple-element.67), channel_id=1, source_target_pairs={{0,12},{1,13},{2,14},{3,15},{4,8},{5,9},{6,10},{7,11},{8,4},{9,5},... | collective-permute-start | bytes 221192 | tf_op jit(solution)/shard_map/ppermute | solution.py:196
  41.1 2.4 %collective-permute-start.13 = (bf16[2,2,8,1152]{3,2,1,0:T(8,128)(2,1)S(1)}, bf16[2,2,8,1152]{3,2,1,0:T(8,128)(2,1)S(1)}, u32[]{:S(2)}, u32[]{:S(2)}) collective-permute-start(bf16[2,2,8,1152]{3,2,1,0:T(8,128)(2,1)S(1)} %get-tuple-element.69), channel_id=1, source_target_pairs={{0,2},{1,3},{2,0},{3,1},{4,6},{5,7},{6,4},{7,5},{8,10},{9,11},{10,... | collective-permute-start | bytes 221192 | tf_op jit(solution)/shard_map/ppermute | solution.py:196
  43.5 1.5 %project.2.refs_7_ = f32[2,128,1152]{2,1,0:T(8,128)} custom-call(bf16[2,2,8,1152]{3,2,1,0:T(8,128)(2,1)S(1)} %get-tuple-element.70.refs_0_, bf16[1,2,8,1152]{3,2,1,0:T(8,128)(2,1)S(1)} %collective-permute-done.14.refs_1_, bf16[1,2,8,1152]{3,2,1,0:T(8,128)(2,1)S(1)} %collective-permute-done.15.refs_2_, ...), custom_call_target="tpu_custom_call" | custom-call | tf_op jit(solution)/shard_map/project/pallas_call | solution.py:474
  45.0 0.6 %collective-permute-done.11.refs_1_ = bf16[2,2,8,1152]{3,2,1,0:T(8,128)(2,1)S(1)} collective-permute-done((bf16[2,2,8,1152]{3,2,1,0:T(8,128)(2,1)S(1)}, bf16[2,2,8,1152]{3,2,1,0:T(8,128)(2,1)S(1)}, u32[]{:S(2)}, u32[]{:S(2)}) %collective-permute-start.11) | collective-permute-done | bytes 73760 | tf_op jit(solution)/shard_map/ppermute | solution.py:196
  45.6 0.6 %collective-permute-done.12.refs_2_ = bf16[2,2,8,1152]{3,2,1,0:T(8,128)(2,1)S(1)} collective-permute-done((bf16[2,2,8,1152]{3,2,1,0:T(8,128)(2,1)S(1)}, bf16[2,2,8,1152]{3,2,1,0:T(8,128)(2,1)S(1)}, u32[]{:S(2)}, u32[]{:S(2)}) %collective-permute-start.12) | collective-permute-done | bytes 73760 | tf_op jit(solution)/shard_map/ppermute | solution.py:196
  46.3 1.5 %project.3 = f32[2,128,1152]{2,1,0:T(8,128)} custom-call(bf16[2,2,8,1152]{3,2,1,0:T(8,128)(2,1)S(1)} %collective-permute-done.10.refs_0_, bf16[2,2,8,1152]{3,2,1,0:T(8,128)(2,1)S(1)} %collective-permute-done.11.refs_1_, bf16[2,2,8,1152]{3,2,1,0:T(8,128)(2,1)S(1)} %collective-permute-done.12.refs_2_, ...), custom_call_target="tpu_custom_call", output_to_operand_aliasing={{}: (7, {})} | custom-call | tf_op jit(solution)/shard_map/project/pallas_call | solution.py:474
  (32 shorter events, 2.7 us)
Async XLA Ops:
  2.3 1.8 %collective-permute-start = (bf16[8,2,8,1152]{3,2,1,0:T(8,128)(2,1)S(1)}, bf16[8,2,8,1152]{3,2,1,0:T(8,128)(2,1)S(1)}, u32[]{:S(2)}, u32[]{:S(2)}) collective-permute-start(bf16[8,2,8,1152]{3,2,1,0:T(8,128)(2,1)S(1)} %get-tuple-element.44), channel_id=1, source_target_pairs={{0,1},{1,0},{2,3},{3,2},{4,5},{5,4},{6,7},{7,6},{8,9},{9,8},{10,11... | collective-permute-start | bytes 884744 | tf_op jit(solution)/shard_map/ppermute | solution.py:199
  4.1 16.6 %slice-start = ((s8[7962624]{0:T(1024)(128)(4,1)}), s8[4194304]{0:T(1024)(128)(4,1)S(1)}, s32[]{:S(2)}) async-start(s8[7962624]{0:T(1024)(128)(4,1)} %bitcast.5), calls=%async_computation | async-start | bytes 8388608
  4.1 16.7 %slice-start.1 = ((s8[7962624]{0:T(1024)(128)(4,1)}), s8[3768320]{0:T(1024)(128)(4,1)S(1)}, s32[]{:S(2)}) async-start(s8[7962624]{0:T(1024)(128)(4,1)} %bitcast.5), calls=%async_computation.1 | async-start | bytes 7536640
  4.1 11.8 %collective-permute-start.5 = (bf16[2,2,8,1152]{3,2,1,0:T(8,128)(2,1)S(1)}, bf16[2,2,8,1152]{3,2,1,0:T(8,128)(2,1)S(1)}, u32[]{:S(2)}, u32[]{:S(2)}) collective-permute-start(bf16[2,2,8,1152]{3,2,1,0:T(8,128)(2,1)S(1)} %get-tuple-element.58), channel_id=1, source_target_pairs={{0,14},{1,15},{2,12},{3,13},{4,10},{5,11},{6,8},{7,9},{8,6},{9,7},... | collective-permute-start | bytes 221192 | tf_op jit(solution)/shard_map/ppermute | solution.py:196
  10.1 6.9 %collective-permute-start.6 = (bf16[2,2,8,1152]{3,2,1,0:T(8,128)(2,1)S(1)}, bf16[2,2,8,1152]{3,2,1,0:T(8,128)(2,1)S(1)}, u32[]{:S(2)}, u32[]{:S(2)}) collective-permute-start(bf16[2,2,8,1152]{3,2,1,0:T(8,128)(2,1)S(1)} %get-tuple-element.59), channel_id=1, source_target_pairs={{0,12},{1,13},{2,14},{3,15},{4,8},{5,9},{6,10},{7,11},{8,4},{9,5},... | collective-permute-start | bytes 221192 | tf_op jit(solution)/shard_map/ppermute | solution.py:196
  10.3 9.2 %collective-permute-start.7 = (bf16[2,2,8,1152]{3,2,1,0:T(8,128)(2,1)S(1)}, bf16[2,2,8,1152]{3,2,1,0:T(8,128)(2,1)S(1)}, u32[]{:S(2)}, u32[]{:S(2)}) collective-permute-start(bf16[2,2,8,1152]{3,2,1,0:T(8,128)(2,1)S(1)} %get-tuple-element.60), channel_id=1, source_target_pairs={{0,4},{1,5},{2,6},{3,7},{4,0},{5,1},{6,2},{7,3},{8,12},{9,13},{10,... | collective-permute-start | bytes 221192 | tf_op jit(solution)/shard_map/ppermute | solution.py:196
  10.3 10.4 %collective-permute-start.8 = (bf16[2,2,8,1152]{3,2,1,0:T(8,128)(2,1)S(1)}, bf16[2,2,8,1152]{3,2,1,0:T(8,128)(2,1)S(1)}, u32[]{:S(2)}, u32[]{:S(2)}) collective-permute-start(bf16[2,2,8,1152]{3,2,1,0:T(8,128)(2,1)S(1)} %get-tuple-element.61), channel_id=1, source_target_pairs={{0,2},{1,3},{2,0},{3,1},{4,6},{5,7},{6,4},{7,5},{8,10},{9,11},{10,... | collective-permute-start | bytes 221192 | tf_op jit(solution)/shard_map/ppermute | solution.py:196
  10.7 13.8 %collective-permute-start.3 = (bf16[2,2,8,1152]{3,2,1,0:T(8,128)(2,1)S(1)}, bf16[2,2,8,1152]{3,2,1,0:T(8,128)(2,1)S(1)}, u32[]{:S(2)}, u32[]{:S(2)}) collective-permute-start(bf16[2,2,8,1152]{3,2,1,0:T(8,128)(2,1)S(1)} %get-tuple-element.48), channel_id=1, source_target_pairs={{0,10},{1,11},{2,8},{3,9},{4,14},{5,15},{6,12},{7,13},{8,2},{9,3},... | collective-permute-start | bytes 221192 | tf_op jit(solution)/shard_map/ppermute | solution.py:196
  15.9 8.6 %collective-permute-start.4 = (bf16[2,2,8,1152]{3,2,1,0:T(8,128)(2,1)S(1)}, bf16[2,2,8,1152]{3,2,1,0:T(8,128)(2,1)S(1)}, u32[]{:S(2)}, u32[]{:S(2)}) collective-permute-start(bf16[2,2,8,1152]{3,2,1,0:T(8,128)(2,1)S(1)} %get-tuple-element.49), channel_id=1, source_target_pairs={{0,6},{1,7},{2,4},{3,5},{4,2},{5,3},{6,0},{7,1},{8,14},{9,15},{10,... | collective-permute-start | bytes 221192 | tf_op jit(solution)/shard_map/ppermute | solution.py:196
  17.0 5.7 %collective-permute-start.1 = (bf16[1,2,8,1152]{3,2,1,0:T(8,128)(2,1)S(1)}, bf16[1,2,8,1152]{3,2,1,0:T(8,128)(2,1)S(1)}, u32[]{:S(2)}, u32[]{:S(2)}) collective-permute-start(bf16[1,2,8,1152]{3,2,1,0:T(8,128)(2,1)S(1)} %get-tuple-element.46), channel_id=1, source_target_pairs={{0,8},{1,9},{2,10},{3,11},{4,12},{5,13},{6,14},{7,15},{8,0},{9,1},... | collective-permute-start | bytes 110600 | tf_op jit(solution)/shard_map/ppermute | solution.py:196
  19.5 5.0 %collective-permute-start.2 = (bf16[1,2,8,1152]{3,2,1,0:T(8,128)(2,1)S(1)}, bf16[1,2,8,1152]{3,2,1,0:T(8,128)(2,1)S(1)}, u32[]{:S(2)}, u32[]{:S(2)}) collective-permute-start(bf16[1,2,8,1152]{3,2,1,0:T(8,128)(2,1)S(1)} %get-tuple-element.47), channel_id=1, source_target_pairs={{0,8},{1,9},{2,10},{3,11},{4,12},{5,13},{6,14},{7,15},{8,0},{9,1},... | collective-permute-start | bytes 110600 | tf_op jit(solution)/shard_map/ppermute | solution.py:196
  27.5 1.6 %collective-permute-start.9 = (bf16[8,2,8,1152]{3,2,1,0:T(8,128)(2,1)S(1)}, bf16[8,2,8,1152]{3,2,1,0:T(8,128)(2,1)S(1)}, u32[]{:S(2)}, u32[]{:S(2)}) collective-permute-start(bf16[8,2,8,1152]{3,2,1,0:T(8,128)(2,1)S(1)} %attend.3), channel_id=1, source_target_pairs={{0,1},{1,0},{2,3},{3,2},{4,5},{5,4},{6,7},{7,6},{8,9},{9,8},{10,11... | collective-permute-start | bytes 884744 | tf_op jit(solution)/shard_map/ppermute | solution.py:199
  29.2 14.3 %copy-start = (bf16[1152,1152]{1,0:T(8,128)(2,1)S(1)}, bf16[1152,1152]{1,0:T(8,128)(2,1)}, u32[]{:S(2)}) copy-start(bf16[1152,1152]{1,0:T(8,128)(2,1)} %refs_4_.3) | copy-start | bytes 7962628
  29.2 14.3 %copy-start.1 = (f32[2,1,128,1152]{3,2,1,0:T(8,128)S(1)}, f32[2,1,128,1152]{3,2,1,0:T(8,128)}, u32[]{:S(2)}) copy-start(f32[2,1,128,1152]{3,2,1,0:T(8,128)} %param.7) | copy-start | bytes 3538948
  29.2 11.8 %collective-permute-start.16 = (bf16[2,2,8,1152]{3,2,1,0:T(8,128)(2,1)S(1)}, bf16[2,2,8,1152]{3,2,1,0:T(8,128)(2,1)S(1)}, u32[]{:S(2)}, u32[]{:S(2)}) collective-permute-start(bf16[2,2,8,1152]{3,2,1,0:T(8,128)(2,1)S(1)} %get-tuple-element.73), channel_id=1, source_target_pairs={{0,10},{1,11},{2,8},{3,9},{4,14},{5,15},{6,12},{7,13},{8,2},{9,3},... | collective-permute-start | bytes 221192 | tf_op jit(solution)/shard_map/ppermute | solution.py:196
  30.0 9.0 %collective-permute-start.14 = (bf16[1,2,8,1152]{3,2,1,0:T(8,128)(2,1)S(1)}, bf16[1,2,8,1152]{3,2,1,0:T(8,128)(2,1)S(1)}, u32[]{:S(2)}, u32[]{:S(2)}) collective-permute-start(bf16[1,2,8,1152]{3,2,1,0:T(8,128)(2,1)S(1)} %get-tuple-element.71), channel_id=1, source_target_pairs={{0,8},{1,9},{2,10},{3,11},{4,12},{5,13},{6,14},{7,15},{8,0},{9,1},... | collective-permute-start | bytes 110600 | tf_op jit(solution)/shard_map/ppermute | solution.py:196
  32.2 8.9 %collective-permute-start.15 = (bf16[1,2,8,1152]{3,2,1,0:T(8,128)(2,1)S(1)}, bf16[1,2,8,1152]{3,2,1,0:T(8,128)(2,1)S(1)}, u32[]{:S(2)}, u32[]{:S(2)}) collective-permute-start(bf16[1,2,8,1152]{3,2,1,0:T(8,128)(2,1)S(1)} %get-tuple-element.72), channel_id=1, source_target_pairs={{0,8},{1,9},{2,10},{3,11},{4,12},{5,13},{6,14},{7,15},{8,0},{9,1},... | collective-permute-start | bytes 110600 | tf_op jit(solution)/shard_map/ppermute | solution.py:196
  33.0 12.1 %collective-permute-start.10 = (bf16[2,2,8,1152]{3,2,1,0:T(8,128)(2,1)S(1)}, bf16[2,2,8,1152]{3,2,1,0:T(8,128)(2,1)S(1)}, u32[]{:S(2)}, u32[]{:S(2)}) collective-permute-start(bf16[2,2,8,1152]{3,2,1,0:T(8,128)(2,1)S(1)} %get-tuple-element.66), channel_id=1, source_target_pairs={{0,14},{1,15},{2,12},{3,13},{4,10},{5,11},{6,8},{7,9},{8,6},{9,7},... | collective-permute-start | bytes 221192 | tf_op jit(solution)/shard_map/ppermute | solution.py:196
  35.7 7.8 %collective-permute-start.17 = (bf16[2,2,8,1152]{3,2,1,0:T(8,128)(2,1)S(1)}, bf16[2,2,8,1152]{3,2,1,0:T(8,128)(2,1)S(1)}, u32[]{:S(2)}, u32[]{:S(2)}) collective-permute-start(bf16[2,2,8,1152]{3,2,1,0:T(8,128)(2,1)S(1)} %get-tuple-element.74), channel_id=1, source_target_pairs={{0,6},{1,7},{2,4},{3,5},{4,2},{5,3},{6,0},{7,1},{8,14},{9,15},{10,... | collective-permute-start | bytes 221192 | tf_op jit(solution)/shard_map/ppermute | solution.py:196
  39.0 6.6 %collective-permute-start.11 = (bf16[2,2,8,1152]{3,2,1,0:T(8,128)(2,1)S(1)}, bf16[2,2,8,1152]{3,2,1,0:T(8,128)(2,1)S(1)}, u32[]{:S(2)}, u32[]{:S(2)}) collective-permute-start(bf16[2,2,8,1152]{3,2,1,0:T(8,128)(2,1)S(1)} %get-tuple-element.67), channel_id=1, source_target_pairs={{0,12},{1,13},{2,14},{3,15},{4,8},{5,9},{6,10},{7,11},{8,4},{9,5},... | collective-permute-start | bytes 221192 | tf_op jit(solution)/shard_map/ppermute | solution.py:196
  41.1 5.2 %collective-permute-start.12 = (bf16[2,2,8,1152]{3,2,1,0:T(8,128)(2,1)S(1)}, bf16[2,2,8,1152]{3,2,1,0:T(8,128)(2,1)S(1)}, u32[]{:S(2)}, u32[]{:S(2)}) collective-permute-start(bf16[2,2,8,1152]{3,2,1,0:T(8,128)(2,1)S(1)} %get-tuple-element.68), channel_id=1, source_target_pairs={{0,4},{1,5},{2,6},{3,7},{4,0},{5,1},{6,2},{7,3},{8,12},{9,13},{10,... | collective-permute-start | bytes 221192 | tf_op jit(solution)/shard_map/ppermute | solution.py:196
  41.1 5.2 %collective-permute-start.13 = (bf16[2,2,8,1152]{3,2,1,0:T(8,128)(2,1)S(1)}, bf16[2,2,8,1152]{3,2,1,0:T(8,128)(2,1)S(1)}, u32[]{:S(2)}, u32[]{:S(2)}) collective-permute-start(bf16[2,2,8,1152]{3,2,1,0:T(8,128)(2,1)S(1)} %get-tuple-element.69), channel_id=1, source_target_pairs={{0,2},{1,3},{2,0},{3,1},{4,6},{5,7},{6,4},{7,5},{8,10},{9,11},{10,... | collective-permute-start | bytes 221192 | tf_op jit(solution)/shard_map/ppermute | solution.py:196
